TPU v7x, 32 devices: a whole 2x2x4 slice. The times are simulated.
32 devices in a mesh: groups: 2 (over x), blk: 16 (over z, y, core).
Axes of the slice: x: 2, y: 2, z: 4, core: 2. Of those that a mesh axis runs over, the one named last changes fastest.
Arguments:
- queries: float32 [64, 8192], P(('groups', 'blk')), parts along dimension 0, may hold values from -50 to 50
- prefix_keys: float32 [4096, 512], P(('groups', 'blk')), parts along dimension 0, may hold values from -40 to 40
- prefix_values: float32 [4096, 512], P(('groups', 'blk')), parts along dimension 0, may hold values from -8 to 8
- out_weight: float32 [8192, 4096], P('blk'), may hold values from -0.0625 to 0.0625
- lengths: int32 [4], P('groups'), parts along dimension 0, may hold values from 512 to 2048, as said below
Outputs:
- mixed: float32 [64, 4096], P(('groups', 'blk')), parts along dimension 0
There are 2 independent parts, one for each index of `groups`. A program takes and returns all parts, laid end to end along the dimension named above; an argument that names none is the same for every part. Nothing has to cross between parts.
Inputs may be any that keep to these rules, and one draw needn't show every extreme that they name: `lengths`: each request sees at least the first 512 prefix tokens, and some request sees all 2048 of them.
All inputs are finite; a program needn't handle non-finite values.
Results may differ from a plain program's by a relative error of at most 0.0003.
Values sent between devices are 32-bit elements; how exact they have to be, the bound alone decides.
No kernel may reach another device: no remote copies, remote signals or barrier semaphores. Data moves between devices by JAX's collectives and lax.ppermute only.
A program may use at most 128 MiB of HBM per device.

v0:
```python
import functools
import math

import jax
import jax.numpy as jnp
from jax import lax
from jax.experimental import pallas as pl
from jax.experimental.pallas import tpu as pltpu
from jax.sharding import PartitionSpec as P


H = 64
KVH = 4
HD = 128
REQ_TOK = 16
GROUP = H // KVH
LANES = 128

HIGHEST = lax.Precision.HIGHEST
NEG_FILL = -1e30


VMEM = pltpu.VMEM


def reverse_bits(value, bits):
    out = 0
    for b in range(bits):
        out |= ((value >> b) & 1) << (bits - 1 - b)
    return out


def swap_rows(x, size):
    blocks = [x[i * size : (i + 1) * size] for i in range(x.shape[0] // size)]
    return jnp.concatenate([blocks[i ^ 1] for i in range(len(blocks))], axis=0)


def lanes_of(columns, rows):
    lane = lax.broadcasted_iota(jnp.int32, (rows, LANES), 1)
    out = jnp.zeros((rows, LANES), jnp.float32)
    for i, column in enumerate(columns):
        out = jnp.where(lane == i, column, out)
    return out


def pieces_of(x, count):
    out = []
    for _ in range(count):
        out.append(x.astype(jnp.bfloat16))
        x = x - out[-1].astype(jnp.float32)
    return out


def times(a, b, dims=(((1,), (0,)), ((), ()))):
    return lax.dot_general(a, b, dims, preferred_element_type=jnp.float32)


def limit(mib):
    return pltpu.CompilerParams(vmem_limit_bytes=mib << 20)


IN_VMEM = pl.BlockSpec(memory_space=VMEM)
IN_PLACE = pl.BlockSpec(memory_space=pl.ANY)


def in_hbm(x):
    return pltpu.with_memory_space_constraint(x, pltpu.HBM)


def pack_kernel(sub, q_hbm, k_hbm, v_hbm, *refs):
    outs, sems = refs[:-1], refs[-1]
    plane = lax.axis_index("blk") // sub
    keys, wide = k_hbm.shape[0], GROUP * HD
    copies = []
    for step in (2, 3, 1, 0) if KVH == 4 else range(KVH):
        other = plane ^ step
        lanes = pl.ds(pl.multiple_of(other * HD, HD), HD)
        q_lanes = pl.ds(pl.multiple_of(other * wide, wide), wide)
        copies += [
            (k_hbm.at[:, lanes], outs[step].at[pl.ds(0, keys), :]),
            (v_hbm.at[:, lanes], outs[step].at[pl.ds(keys, keys), :]),
            (q_hbm.at[:, q_lanes], outs[KVH + step]),
        ]
    copies = [pltpu.make_async_copy(src, dst, sems.at[i]) for i, (src, dst) in enumerate(copies)]
    for copy in copies:
        copy.start()
    for copy in copies:
        copy.wait()


def pack(sub, queries, keys, values):
    kv = jax.ShapeDtypeStruct((2 * keys.shape[0], HD), jnp.float32)
    q = jax.ShapeDtypeStruct((queries.shape[0], GROUP * HD), jnp.float32)
    out = pl.pallas_call(
        functools.partial(pack_kernel, sub),
        out_shape=[kv] * KVH + [q] * KVH,
        in_specs=[IN_PLACE] * 3,
        out_specs=[IN_VMEM] * (2 * KVH),
        scratch_shapes=[pltpu.SemaphoreType.DMA((3 * KVH,))],
        compiler_params=limit(4),
        name="pack",
    )(in_hbm(queries), in_hbm(keys), in_hbm(values))
    return out[:KVH], out[KVH:]


def split_kernel(tile, w_hbm, high_ref, low_ref, buf, sems):
    chunks = w_hbm.shape[0] // tile
    copies = [
        pltpu.make_async_copy(w_hbm.at[pl.ds(c * tile, tile), :], buf.at[c], sems.at[c])
        for c in range(chunks)
    ]
    for copy in copies:
        copy.start()
    for c in range(chunks):
        copies[c].wait()
        rows = slice(c * tile, (c + 1) * tile)
        high_ref[rows, :], low_ref[rows, :] = pieces_of(buf[c], 2)


def split_weight(weight):
    features, width = weight.shape
    tile = min(features, 64)
    out = jax.ShapeDtypeStruct((features, width), jnp.bfloat16)
    return pl.pallas_call(
        functools.partial(split_kernel, tile),
        out_shape=[out, out],
        in_specs=[IN_PLACE],
        out_specs=[IN_VMEM] * 2,
        scratch_shapes=[
            pltpu.VMEM((features // tile, tile, width), jnp.float32),
            pltpu.SemaphoreType.DMA((features // tile,)),
        ],
        compiler_params=limit(20),
        cost_estimate=pl.CostEstimate(
            flops=8 * features * width, bytes_accessed=8 * features * width, transcendentals=0
        ),
        name="split",
    )(in_hbm(weight))


def attend_kernel(bits, local_rows, key_count, len_ref, *refs):
    sub = 1 << bits
    q_refs, kv_refs = refs[:sub], refs[sub : sub + KVH]
    send_ref, keep_ref = refs[sub + KVH :]
    position = lax.axis_index("blk")
    plane, place = position // sub, position % sub
    part = KVH * local_rows
    rows = part * sub
    per_owner = GROUP // sub
    held = key_count * KVH

    row = lax.broadcasted_iota(jnp.int32, (rows, 1), 0)
    order = row // part
    within = row % part
    rel = (within // local_rows) * sub
    for b in range(bits):
        rel = rel + ((order >> (bits - 1 - b)) & 1) * (1 << b)
    token = (position ^ rel) * local_rows + within % local_rows
    request = token // REQ_TOK
    limits = jnp.zeros((rows, 1), jnp.int32)
    for i in range(len_ref.shape[0]):
        limits = jnp.where(request == i, len_ref[i], limits)
    at = lax.broadcasted_iota(jnp.int32, (1, held), 1)
    source = (plane ^ (at // key_count)) * sub + place
    visible = (source * key_count + at % key_count) < limits

    keys = jnp.concatenate([r[:key_count, :] for r in kv_refs], axis=0)
    values = jnp.concatenate([r[key_count:, :] for r in kv_refs], axis=0)
    k1, k2, k3 = pieces_of(keys, 3)
    k12, k31 = jnp.concatenate([k1, k2], axis=1), jnp.concatenate([k3, k1], axis=1)
    v1, v2 = pieces_of(values, 2)
    v12 = jnp.concatenate([v1, v2], axis=1)
    both = (((1,), (1,)), ((), ()))
    scale = 1.0 / math.sqrt(HD)

    half = GROUP // 2
    for ref, start in ((send_ref, half), (keep_ref, 0)):
        peaks, totals = [], []
        for i in range(half):
            head = start + i
            owner = place ^ reverse_bits(head // per_owner, bits)
            lanes = pl.ds(pl.multiple_of((owner * per_owner + head % per_owner) * HD, HD), HD)
            q = jnp.concatenate([q_ref[:, lanes] for q_ref in q_refs], axis=0)
            q1, q2, q3 = pieces_of(q, 3)
            q11, q22 = jnp.concatenate([q1, q1], axis=1), jnp.concatenate([q2, q2], axis=1)
            q13 = jnp.concatenate([q1, q3], axis=1)
            top = times(jnp.concatenate([q11, q22], axis=0), k12, both)
            scores = (top[:rows] + (top[rows:] + times(q13, k31, both))) * scale
            masked = jnp.where(visible, scores, NEG_FILL)
            peak = jnp.max(masked, axis=1, keepdims=True)
            weights = jnp.where(visible, jnp.exp(masked - peak), 0.0)
            w1, w2 = pieces_of(weights, 2)
            wide = times(w1, v12)
            ref[:, i * HD : (i + 1) * HD] = wide[:, :HD] + (wide[:, HD:] + times(w2, v1))
            peaks.append(peak)
            totals.append(jnp.sum(weights, axis=1, keepdims=True))
        ref[:, half * HD :] = lanes_of(peaks + totals, rows)


def attend(bits, local_rows, lengths, q_parts, kv_held):
    sub = 1 << bits
    rows = KVH * local_rows * sub
    out = jax.ShapeDtypeStruct((rows, GROUP // 2 * HD + LANES), jnp.float32)
    return pl.pallas_call(
        functools.partial(attend_kernel, bits, local_rows, kv_held[0].shape[0] // 2),
        out_shape=[out, out],
        in_specs=[pl.BlockSpec(memory_space=pltpu.SMEM)] + [IN_VMEM] * (sub + KVH),
        out_specs=[IN_VMEM] * 2,
        compiler_params=limit(16),
        name="attend",
    )(lengths, *q_parts, *kv_held)


def merged(keep_ref, recv_ref, swap):
    heads = (keep_ref.shape[1] - LANES) // HD
    mine, other = keep_ref[:, heads * HD :], swap_rows(recv_ref[:, heads * HD :], swap)
    sums, peaks, totals = [], [], []
    for i in range(heads):
        peak_a, peak_b = mine[:, i : i + 1], other[:, i : i + 1]
        peak = jnp.maximum(peak_a, peak_b)
        factor_a, factor_b = jnp.exp(peak_a - peak), jnp.exp(peak_b - peak)
        cols = slice(i * HD, (i + 1) * HD)
        sums.append(keep_ref[:, cols] * factor_a + swap_rows(recv_ref[:, cols], swap) * factor_b)
        peaks.append(peak)
        totals.append(
            mine[:, heads + i : heads + i + 1] * factor_a + other[:, heads + i : heads + i + 1] * factor_b
        )
    return sums, peaks, totals


def merge_kernel(swap, keep_ref, recv_ref, send_out, keep_out):
    sums, peaks, totals = merged(keep_ref, recv_ref, swap)
    half = len(sums) // 2
    for start, ref in ((0, keep_out), (half, send_out)):
        for i in range(half):
            ref[:, i * HD : (i + 1) * HD] = sums[start + i]
        stats = peaks[start : start + half] + totals[start : start + half]
        ref[:, half * HD :] = lanes_of(stats, keep_ref.shape[0])


def merge(swap, keep, recv):
    rows, width = keep.shape
    half = (width - LANES) // HD // 2
    out = jax.ShapeDtypeStruct((rows, half * HD + LANES), jnp.float32)
    return pl.pallas_call(
        functools.partial(merge_kernel, swap),
        out_shape=[out, out],
        in_specs=[IN_VMEM] * 2,
        out_specs=[IN_VMEM] * 2,
        compiler_params=limit(4),
        name="merge",
    )(keep, recv)


def project_kernel(swap, tile, keep_ref, recv_ref, high_ref, low_ref, send_out, keep_out):
    sums, _, totals = merged(keep_ref, recv_ref, swap)
    attended = jnp.concatenate([a / t for a, t in zip(sums, totals)], axis=1)
    rows = attended.shape[0]
    half = rows // 2
    a1, a2 = pieces_of(attended, 2)
    a12 = jnp.concatenate([a1, a2], axis=0)
    for c in range(high_ref.shape[1] // tile):
        cols = slice(c * tile, (c + 1) * tile)
        top = times(a12, high_ref[:, cols])
        out = top[:rows] + (top[rows:] + times(a1, low_ref[:, cols]))
        keep_out[:, cols] = out[:half]
        send_out[:, cols] = out[half:]


def project(swap, keep, recv, high, low):
    width = high.shape[1]
    out = jax.ShapeDtypeStruct((keep.shape[0] // 2, width), jnp.float32)
    return pl.pallas_call(
        functools.partial(project_kernel, swap, min(width, 512)),
        out_shape=[out, out],
        in_specs=[IN_VMEM] * 4,
        out_specs=[IN_VMEM] * 2,
        compiler_params=limit(16),
        name="project",
    )(keep, recv, high, low)


def by_planes(bits, queries, keys, values, weight, lengths):
    blocks = lax.axis_size("blk")
    sub = 1 << bits
    local_rows = queries.shape[0]
    part = KVH * local_rows

    def swap(x, mask):
        return lax.ppermute(x, "blk", [(i, i ^ mask) for i in range(blocks)])

    kv_send, q_send = pack(sub, queries, keys, values)
    kv_held = [kv_send[0]] + [swap(kv_send[k], k * sub) for k in range(1, KVH)]
    q_rows = [q_send[0]] + [swap(q_send[k], k * sub) for k in range(1, KVH)]
    q_parts = [jnp.concatenate(q_rows, axis=0)]
    for b in reversed(range(bits)):
        q_parts = q_parts + [swap(x, 1 << b) for x in q_parts]
    high, low = split_weight(weight)

    send, keep = attend(bits, local_rows, lengths, q_parts, kv_held)
    for b in range(bits - 1):
        send, keep = merge(part << (bits - 1 - b), keep, swap(send, 1 << b))
    send, keep = project(part, keep, swap(send, 1 << (bits - 1)), high, low)

    recv = swap(send, 1)
    for b in range(1, bits):
        half = keep.shape[0] // 2
        send = keep[half:] + recv[half:]
        keep = keep[:half] + recv[:half]
        recv = swap(send, 1 << b)
    total = keep + recv
    out = total[:local_rows]
    for k in range(1, KVH):
        out = out + swap(total[k * local_rows : (k + 1) * local_rows], k * sub)
    return out


def head_partials(query_rows, keys_held, values_held, key_pos, lengths):
    row_count = query_rows.shape[0]
    grouped = query_rows.reshape(row_count, GROUP, HD)
    scores = jnp.einsum(
        "tje,pe->tjp", grouped, keys_held, precision=HIGHEST, preferred_element_type=jnp.float32
    ) * (1.0 / math.sqrt(HD))
    request_ids = jnp.arange(row_count, dtype=jnp.int32) // REQ_TOK
    request_table = jnp.arange(lengths.shape[0], dtype=jnp.int32)
    limits = jnp.sum(
        jnp.where(request_ids[:, None] == request_table[None, :], lengths[None, :], 0), axis=1
    )
    visible = (key_pos[None, :] < limits[:, None])[:, None, :]
    masked = jnp.where(visible, scores, NEG_FILL)
    peak_vals = jnp.max(masked, axis=2)
    weights = jnp.where(visible, jnp.exp(masked - peak_vals[..., None]), 0.0)
    totals = jnp.sum(weights, axis=2)
    mixed_values = jnp.einsum(
        "tjp,pe->tje", weights, values_held, precision=HIGHEST, preferred_element_type=jnp.float32
    )
    return mixed_values.reshape(row_count, GROUP * HD), peak_vals, totals


def by_all_to_all(queries, keys, values, weight, lengths):
    blocks = lax.axis_size("blk")
    position = lax.axis_index("blk")
    local_rows = queries.shape[0]
    total_rows = local_rows * blocks
    key_count = keys.shape[0]
    sub_count = blocks // KVH
    sub_len = key_count // sub_count

    def exchange(x, split, concat):
        return lax.all_to_all(x, "blk", split_axis=split, concat_axis=concat, tiled=True)

    def spread(x):
        split = x.reshape(sub_count, sub_len, KVH, HD).transpose(0, 2, 1, 3)
        return exchange(split.reshape(blocks, sub_len, HD), 0, 0).reshape(blocks * sub_len, HD)

    held_pos = (
        jnp.arange(blocks, dtype=jnp.int32)[:, None] * key_count
        + position // KVH * sub_len
        + jnp.arange(sub_len, dtype=jnp.int32)[None, :]
    ).reshape(blocks * sub_len)
    query_heads = queries.reshape(local_rows, KVH, GROUP * HD).transpose(1, 0, 2)
    query_send = jnp.broadcast_to(query_heads[None], (sub_count, KVH, local_rows, GROUP * HD))
    query_held = exchange(query_send.reshape(blocks, local_rows, GROUP * HD), 0, 0)
    sums, peaks, totals = head_partials(
        query_held.reshape(total_rows, GROUP * HD), spread(keys), spread(values), held_pos, lengths
    )
    sums = exchange(sums, 0, 0).reshape(sub_count, KVH, local_rows, GROUP, HD)
    peaks = exchange(peaks, 0, 0).reshape(sub_count, KVH, local_rows, GROUP)
    totals = exchange(totals, 0, 0).reshape(sub_count, KVH, local_rows, GROUP)
    factor = jnp.exp(peaks - jnp.max(peaks, axis=0)[None])
    numerator = jnp.sum(sums * factor[..., None], axis=0)
    denominator = jnp.sum(totals * factor, axis=0)
    attended = (numerator / denominator[..., None]).transpose(1, 0, 2, 3).reshape(local_rows, H * HD)
    feature_rows = exchange(attended, 1, 0)
    parts = jnp.dot(feature_rows, weight, precision=HIGHEST, preferred_element_type=jnp.float32)
    return jnp.sum(exchange(parts, 0, 0).reshape(blocks, local_rows, weight.shape[1]), axis=0)


def per_device(queries, prefix_keys, prefix_values, out_weight, lengths):
    blocks = lax.axis_size("blk")
    sub = blocks // KVH
    bits = sub.bit_length() - 1
    fits = (
        blocks == KVH << bits
        and bits >= 1
        and GROUP % sub == 0
        and (KVH * queries.shape[0]) % 8 == 0
        and prefix_keys.shape[0] % LANES == 0
    )
    if fits:
        return by_planes(bits, queries, prefix_keys, prefix_values, out_weight, lengths)
    return by_all_to_all(queries, prefix_keys, prefix_values, out_weight, lengths)


def solution(mesh):
    in_specs = (
        P(("groups", "blk"), None),
        P(("groups", "blk"), None),
        P(("groups", "blk"), None),
        P("blk", None),
        P("groups"),
    )
    out_specs = P(("groups", "blk"), None)
    return jax.shard_map(
        per_device, mesh=mesh, in_specs=in_specs, out_specs=out_specs, check_vma=False
    )
```

profile of v0, /device:TPU:0, one launch (start us, length us, event | category | flops | bytes accessed | tf_op | source)
XLA Modules:
  0.0 53.9 jit_solution(13225399444293089316)
XLA Ops:
  0.0 1.2 %pack.1 = (f32[256,128]{1,0:T(8,128)S(1)}, f32[256,128]{1,0:T(8,128)S(1)}, f32[256,128]{1,0:T(8,128)S(1)}, f32[256,128]{1,0:T(8,128)S(1)}, f32[2,2048]{1,0:T(2,1...) custom-call(f32[2,8192]{1,0:T(2,128)} %q_hbm.1, f32[128,512]{1,0:T(8,128)} %k_hbm.1, ...), custom_call_target="tpu_custom_call" | custom-call | tf_op jit(solution)/shard_map/pack/pallas_call | solution.py:94
  1.2 3.1 %collective-permute-start = (f32[2,2048]{1,0:T(2,128)S(1)}, f32[2,2048]{1,0:T(2,128)S(1)}, u32[]{:S(2)}, u32[]{:S(2)}) collective-permute-start(f32[2,2048]{1,0:T(2,128)S(1)} %get-tuple-element.22), channel_id=1, source_target_pairs={{0,4},{1,5},{2,6},{3,7},{4,0},{5,1},{6,2},{7,3},{8,12},{9,13},{10,... | collective-permute-start | bytes 49160 | tf_op jit(solution)/shard_map/ppermute | solution.py:290
  4.3 2.6 %collective-permute-start.1 = (f32[2,2048]{1,0:T(2,128)S(1)}, f32[2,2048]{1,0:T(2,128)S(1)}, u32[]{:S(2)}, u32[]{:S(2)}) collective-permute-start(f32[2,2048]{1,0:T(2,128)S(1)} %get-tuple-element.23), channel_id=1, source_target_pairs={{0,8},{1,9},{2,10},{3,11},{4,12},{5,13},{6,14},{7,15},{8,0},{9,1},... | collective-permute-start | bytes 49160 | tf_op jit(solution)/shard_map/ppermute | solution.py:290
  6.9 0.0 collective-permute-start.2
  6.9 0.9 %collective-permute-start.6 = (f32[256,128]{1,0:T(8,128)S(1)}, f32[256,128]{1,0:T(8,128)S(1)}, u32[]{:S(2)}, u32[]{:S(2)}) collective-permute-start(f32[256,128]{1,0:T(8,128)S(1)} %get-tuple-element.26), channel_id=1, source_target_pairs={{0,4},{1,5},{2,6},{3,7},{4,0},{5,1},{6,2},{7,3},{8,12},{9,13},{10,... | collective-permute-start | bytes 393224 | tf_op jit(solution)/shard_map/ppermute | solution.py:290
  7.8 3.5 %collective-permute-start.7 = (f32[256,128]{1,0:T(8,128)S(1)}, f32[256,128]{1,0:T(8,128)S(1)}, u32[]{:S(2)}, u32[]{:S(2)}) collective-permute-start(f32[256,128]{1,0:T(8,128)S(1)} %get-tuple-element.27), channel_id=1, source_target_pairs={{0,8},{1,9},{2,10},{3,11},{4,12},{5,13},{6,14},{7,15},{8,0},{9,1},... | collective-permute-start | bytes 393224 | tf_op jit(solution)/shard_map/ppermute | solution.py:290
  11.3 0.0 collective-permute-done
  11.3 1.4 %collective-permute-done.2 = f32[2,2048]{1,0:T(2,128)S(1)} collective-permute-done((f32[2,2048]{1,0:T(2,128)S(1)}, f32[2,2048]{1,0:T(2,128)S(1)}, u32[]{:S(2)}, u32[]{:S(2)}) %collective-permute-start.2) | collective-permute-done | bytes 16416 | tf_op jit(solution)/shard_map/ppermute | solution.py:290
  12.8 1.6 %collective-permute-start.3 = (f32[8,2048]{1,0:T(8,128)S(1)}, f32[8,2048]{1,0:T(8,128)S(1)}, u32[]{:S(2)}, u32[]{:S(2)}) collective-permute-start(f32[8,2048]{1,0:T(8,128)S(1)} %pad_maximum_fusion.refs_0_), channel_id=1, source_target_pairs={{0,2},{1,3},{2,0},{3,1},{4,6},{5,7},{6,4},{7,5},{8,10},{9,11},{10,... | collective-permute-start | bytes 196616 | tf_op jit(solution)/shard_map/ppermute | solution.py:290
  14.4 2.7 %collective-permute-done.3.refs_1_ = f32[8,2048]{1,0:T(8,128)S(1)} collective-permute-done((f32[8,2048]{1,0:T(8,128)S(1)}, f32[8,2048]{1,0:T(8,128)S(1)}, u32[]{:S(2)}, u32[]{:S(2)}) %collective-permute-start.3) | collective-permute-done | bytes 65568 | tf_op jit(solution)/shard_map/ppermute | solution.py:290
  17.1 0.0 collective-permute-start.5
  17.1 0.0 collective-permute-done.4.refs_2_
  17.1 3.8 %collective-permute-done.7.refs_6_ = f32[256,128]{1,0:T(8,128)S(1)} collective-permute-done((f32[256,128]{1,0:T(8,128)S(1)}, f32[256,128]{1,0:T(8,128)S(1)}, u32[]{:S(2)}, u32[]{:S(2)}) %collective-permute-start.7) | collective-permute-done | bytes 131104 | tf_op jit(solution)/shard_map/ppermute | solution.py:290
  20.9 0.0 collective-permute-done.8.refs_7_
  20.9 0.0 collective-permute-done.5.refs_3_
  20.9 0.7 %copy-done = s32[2]{0:T(128)S(1)} copy-done((s32[2]{0:T(128)S(1)}, s32[2]{0:T(128)}, u32[]{:S(2)}) %copy-start) | copy-done | bytes 32
  21.5 6.8 %attend.1 = (f32[32,1152]{1,0:T(8,128)S(1)}, f32[32,1152]{1,0:T(8,128)S(1)}) custom-call(s32[2]{0:T(128)S(1)} %copy-done, f32[8,2048]{1,0:T(8,128)S(1)} %pad_maximum_fusion.refs_0_, f32[8,2048]{1,0:T(8,128)S(1)} %collective-permute-done.3.refs_1_, f32[8,2048]{1,0:T(8,128)S(1)} %collective-permute-done.4.refs_2_, ...), custom_call_target="tpu_custom_call" | custom-call | tf_op jit(solution)/shard_map/attend/pallas_call | solution.py:204
  28.4 0.1 collective-permute-start.9
  28.5 1.4 %collective-permute-done.9.recv_ref = f32[32,1152]{1,0:T(8,128)S(1)} collective-permute-done((f32[32,1152]{1,0:T(8,128)S(1)}, f32[32,1152]{1,0:T(8,128)S(1)}, u32[]{:S(2)}, u32[]{:S(2)}) %collective-permute-start.9) | collective-permute-done | bytes 147488 | tf_op jit(solution)/shard_map/ppermute | solution.py:290
  29.8 0.3 merge.1
  30.1 1.6 %collective-permute-start.10 = (f32[32,640]{1,0:T(8,128)S(1)}, f32[32,640]{1,0:T(8,128)S(1)}, u32[]{:S(2)}, u32[]{:S(2)}) collective-permute-start(f32[32,640]{1,0:T(8,128)S(1)} %get-tuple-element.32), channel_id=1, source_target_pairs={{0,2},{1,3},{2,0},{3,1},{4,6},{5,7},{6,4},{7,5},{8,10},{9,11},{10,... | collective-permute-start | bytes 245768 | tf_op jit(solution)/shard_map/ppermute | solution.py:290
  31.7 3.6 %split.1 = (bf16[512,4096]{1,0:T(8,128)(2,1)S(1)}, bf16[512,4096]{1,0:T(8,128)(2,1)S(1)}) custom-call(f32[512,4096]{1,0:T(8,128)} %w_hbm.1), custom_call_target="tpu_custom_call" | custom-call | flops 16777216 | bytes 16777216 | tf_op jit(solution)/shard_map/split/pallas_call | solution.py:124
  35.3 0.0 collective-permute-done.10.recv_ref
  35.3 1.7 %project.1 = (f32[16,4096]{1,0:T(8,128)S(1)}, f32[16,4096]{1,0:T(8,128)S(1)}) custom-call(f32[32,640]{1,0:T(8,128)S(1)} %get-tuple-element.31.keep_ref, f32[32,640]{1,0:T(8,128)S(1)} %collective-permute-done.10.recv_ref, bf16[512,4096]{1,0:T(8,128)(2,1)S(1)} %get-tuple-element.33.high_ref, bf16[512,4096]{1,0:T(8,128)(2,1)S(1)} %get-tuple-element.34.low_ref), custom_call_target="tpu_custom_call" | custom-call | tf_op jit(solution)/shard_map/project/pallas_call | solution.py:273
  37.0 1.5 %collective-permute-done.11 = f32[16,4096]{1,0:T(8,128)S(1)} collective-permute-done((f32[16,4096]{1,0:T(8,128)S(1)}, f32[16,4096]{1,0:T(8,128)S(1)}, u32[]{:S(2)}, u32[]{:S(2)}) %collective-permute-start.11) | collective-permute-done | bytes 262176 | tf_op jit(solution)/shard_map/ppermute | solution.py:290
  38.6 0.9 %collective-permute-start.12 = (f32[8,4096]{1,0:T(8,128)S(1)}, f32[8,4096]{1,0:T(8,128)S(1)}, u32[]{:S(2)}, u32[]{:S(2)}) collective-permute-start(f32[8,4096]{1,0:T(8,128)S(1)} %slice_add_fusion), channel_id=1, source_target_pairs={{0,2},{1,3},{2,0},{3,1},{4,6},{5,7},{6,4},{7,5},{8,10},{9,11},{10,... | collective-permute-start | bytes 393224 | tf_op jit(solution)/shard_map/ppermute | solution.py:290
  39.5 4.7 %collective-permute-done.12 = f32[8,4096]{1,0:T(8,128)S(1)} collective-permute-done((f32[8,4096]{1,0:T(8,128)S(1)}, f32[8,4096]{1,0:T(8,128)S(1)}, u32[]{:S(2)}, u32[]{:S(2)}) %collective-permute-start.12) | collective-permute-done | bytes 131104 | tf_op jit(solution)/shard_map/ppermute | solution.py:290
  44.2 2.0 %collective-permute-start.13 = (f32[2,4096]{1,0:T(2,128)S(1)}, f32[2,4096]{1,0:T(2,128)S(1)}, u32[]{:S(2)}, u32[]{:S(2)}) collective-permute-start(f32[2,4096]{1,0:T(2,128)S(1)} %get-tuple-element.37), channel_id=1, source_target_pairs={{0,4},{1,5},{2,6},{3,7},{4,0},{5,1},{6,2},{7,3},{8,12},{9,13},{10,... | collective-permute-start | bytes 98312 | tf_op jit(solution)/shard_map/ppermute | solution.py:290
  46.3 2.2 %collective-permute-start.15 = (f32[2,4096]{1,0:T(2,128)S(1)}, f32[2,4096]{1,0:T(2,128)S(1)}, u32[]{:S(2)}, u32[]{:S(2)}) collective-permute-start(f32[2,4096]{1,0:T(2,128)S(1)} %get-tuple-element.38), channel_id=1, source_target_pairs={{0,12},{1,13},{2,14},{3,15},{4,8},{5,9},{6,10},{7,11},{8,4},{9,5},... | collective-permute-start | bytes 98312 | tf_op jit(solution)/shard_map/ppermute | solution.py:290
  48.5 3.5 %collective-permute-done.15 = f32[2,4096]{1,0:T(2,128)S(1)} collective-permute-done((f32[2,4096]{1,0:T(2,128)S(1)}, f32[2,4096]{1,0:T(2,128)S(1)}, u32[]{:S(2)}, u32[]{:S(2)}) %collective-permute-start.15) | collective-permute-done | bytes 32800 | tf_op jit(solution)/shard_map/ppermute | solution.py:290
  52.0 1.3 %collective-permute-done.14 = f32[2,4096]{1,0:T(2,128)S(1)} collective-permute-done((f32[2,4096]{1,0:T(2,128)S(1)}, f32[2,4096]{1,0:T(2,128)S(1)}, u32[]{:S(2)}, u32[]{:S(2)}) %collective-permute-start.14) | collective-permute-done | bytes 32800 | tf_op jit(solution)/shard_map/ppermute | solution.py:290
  53.3 0.6 %fusion.2 = f32[2,4096]{1,0:T(2,128)} fusion(f32[2,4096]{1,0:T(2,128)S(1)} %collective-permute-done.15, f32[2,4096]{1,0:T(2,128)S(1)} %collective-permute-done.14, f32[2,4096]{1,0:T(2,128)S(1)} %collective-permute-done.13, f32[8,4096]{1,0:T(8,128)S(1)} %fusion), kind=kLoop, calls=%fused_computation.6 | loop fusion | flops 24576 | bytes 163840 | tf_op jit(solution)/shard_map/add | solution.py:314
  (12 shorter events, 0.1 us)
Async XLA Ops:
  1.2 10.1 %collective-permute-start = (f32[2,2048]{1,0:T(2,128)S(1)}, f32[2,2048]{1,0:T(2,128)S(1)}, u32[]{:S(2)}, u32[]{:S(2)}) collective-permute-start(f32[2,2048]{1,0:T(2,128)S(1)} %get-tuple-element.22), channel_id=1, source_target_pairs={{0,4},{1,5},{2,6},{3,7},{4,0},{5,1},{6,2},{7,3},{8,12},{9,13},{10,... | collective-permute-start | bytes 49160 | tf_op jit(solution)/shard_map/ppermute | solution.py:290
  4.3 7.0 %collective-permute-start.1 = (f32[2,2048]{1,0:T(2,128)S(1)}, f32[2,2048]{1,0:T(2,128)S(1)}, u32[]{:S(2)}, u32[]{:S(2)}) collective-permute-start(f32[2,2048]{1,0:T(2,128)S(1)} %get-tuple-element.23), channel_id=1, source_target_pairs={{0,8},{1,9},{2,10},{3,11},{4,12},{5,13},{6,14},{7,15},{8,0},{9,1},... | collective-permute-start | bytes 49160 | tf_op jit(solution)/shard_map/ppermute | solution.py:290
  6.9 5.8 %collective-permute-start.2 = (f32[2,2048]{1,0:T(2,128)S(1)}, f32[2,2048]{1,0:T(2,128)S(1)}, u32[]{:S(2)}, u32[]{:S(2)}) collective-permute-start(f32[2,2048]{1,0:T(2,128)S(1)} %get-tuple-element.24), channel_id=1, source_target_pairs={{0,12},{1,13},{2,14},{3,15},{4,8},{5,9},{6,10},{7,11},{8,4},{9,5},... | collective-permute-start | bytes 49160 | tf_op jit(solution)/shard_map/ppermute | solution.py:290
  6.9 10.2 %collective-permute-start.6 = (f32[256,128]{1,0:T(8,128)S(1)}, f32[256,128]{1,0:T(8,128)S(1)}, u32[]{:S(2)}, u32[]{:S(2)}) collective-permute-start(f32[256,128]{1,0:T(8,128)S(1)} %get-tuple-element.26), channel_id=1, source_target_pairs={{0,4},{1,5},{2,6},{3,7},{4,0},{5,1},{6,2},{7,3},{8,12},{9,13},{10,... | collective-permute-start | bytes 393224 | tf_op jit(solution)/shard_map/ppermute | solution.py:290
  7.8 13.1 %collective-permute-start.7 = (f32[256,128]{1,0:T(8,128)S(1)}, f32[256,128]{1,0:T(8,128)S(1)}, u32[]{:S(2)}, u32[]{:S(2)}) collective-permute-start(f32[256,128]{1,0:T(8,128)S(1)} %get-tuple-element.27), channel_id=1, source_target_pairs={{0,8},{1,9},{2,10},{3,11},{4,12},{5,13},{6,14},{7,15},{8,0},{9,1},... | collective-permute-start | bytes 393224 | tf_op jit(solution)/shard_map/ppermute | solution.py:290
  11.3 9.6 %collective-permute-start.8 = (f32[256,128]{1,0:T(8,128)S(1)}, f32[256,128]{1,0:T(8,128)S(1)}, u32[]{:S(2)}, u32[]{:S(2)}) collective-permute-start(f32[256,128]{1,0:T(8,128)S(1)} %get-tuple-element.28), channel_id=1, source_target_pairs={{0,12},{1,13},{2,14},{3,15},{4,8},{5,9},{6,10},{7,11},{8,4},{9,5},... | collective-permute-start | bytes 393224 | tf_op jit(solution)/shard_map/ppermute | solution.py:290
  12.8 4.3 %collective-permute-start.3 = (f32[8,2048]{1,0:T(8,128)S(1)}, f32[8,2048]{1,0:T(8,128)S(1)}, u32[]{:S(2)}, u32[]{:S(2)}) collective-permute-start(f32[8,2048]{1,0:T(8,128)S(1)} %pad_maximum_fusion.refs_0_), channel_id=1, source_target_pairs={{0,2},{1,3},{2,0},{3,1},{4,6},{5,7},{6,4},{7,5},{8,10},{9,11},{10,... | collective-permute-start | bytes 196616 | tf_op jit(solution)/shard_map/ppermute | solution.py:290
  14.4 2.8 %collective-permute-start.4 = (f32[8,2048]{1,0:T(8,128)S(1)}, f32[8,2048]{1,0:T(8,128)S(1)}, u32[]{:S(2)}, u32[]{:S(2)}) collective-permute-start(f32[8,2048]{1,0:T(8,128)S(1)} %pad_maximum_fusion.refs_0_), channel_id=1, source_target_pairs={{0,1},{1,0},{2,3},{3,2},{4,5},{5,4},{6,7},{7,6},{8,9},{9,8},{10,11... | collective-permute-start | bytes 196616 | tf_op jit(solution)/shard_map/ppermute | solution.py:290
  17.1 3.8 %collective-permute-start.5 = (f32[8,2048]{1,0:T(8,128)S(1)}, f32[8,2048]{1,0:T(8,128)S(1)}, u32[]{:S(2)}, u32[]{:S(2)}) collective-permute-start(f32[8,2048]{1,0:T(8,128)S(1)} %collective-permute-done.3.refs_1_), channel_id=1, source_target_pairs={{0,1},{1,0},{2,3},{3,2},{4,5},{5,4},{6,7},{7,6},{8,9},{9,8},{10,11... | collective-permute-start | bytes 196616 | tf_op jit(solution)/shard_map/ppermute | solution.py:290
  20.9 0.7 %copy-start = (s32[2]{0:T(128)S(1)}, s32[2]{0:T(128)}, u32[]{:S(2)}) copy-start(s32[2]{0:T(128)} %len_ref.1) | copy-start | bytes 28
  28.4 1.4 %collective-permute-start.9 = (f32[32,1152]{1,0:T(8,128)S(1)}, f32[32,1152]{1,0:T(8,128)S(1)}, u32[]{:S(2)}, u32[]{:S(2)}) collective-permute-start(f32[32,1152]{1,0:T(8,128)S(1)} %get-tuple-element.30), channel_id=1, source_target_pairs={{0,1},{1,0},{2,3},{3,2},{4,5},{5,4},{6,7},{7,6},{8,9},{9,8},{10,11... | collective-permute-start | bytes 442376 | tf_op jit(solution)/shard_map/ppermute | solution.py:290
  30.1 5.2 %collective-permute-start.10 = (f32[32,640]{1,0:T(8,128)S(1)}, f32[32,640]{1,0:T(8,128)S(1)}, u32[]{:S(2)}, u32[]{:S(2)}) collective-permute-start(f32[32,640]{1,0:T(8,128)S(1)} %get-tuple-element.32), channel_id=1, source_target_pairs={{0,2},{1,3},{2,0},{3,1},{4,6},{5,7},{6,4},{7,5},{8,10},{9,11},{10,... | collective-permute-start | bytes 245768 | tf_op jit(solution)/shard_map/ppermute | solution.py:290
  37.0 1.5 %collective-permute-start.11 = (f32[16,4096]{1,0:T(8,128)S(1)}, f32[16,4096]{1,0:T(8,128)S(1)}, u32[]{:S(2)}, u32[]{:S(2)}) collective-permute-start(f32[16,4096]{1,0:T(8,128)S(1)} %get-tuple-element.36), channel_id=1, source_target_pairs={{0,1},{1,0},{2,3},{3,2},{4,5},{5,4},{6,7},{7,6},{8,9},{9,8},{10,11... | collective-permute-start | bytes 786440 | tf_op jit(solution)/shard_map/ppermute | solution.py:290
  38.6 5.6 %collective-permute-start.12 = (f32[8,4096]{1,0:T(8,128)S(1)}, f32[8,4096]{1,0:T(8,128)S(1)}, u32[]{:S(2)}, u32[]{:S(2)}) collective-permute-start(f32[8,4096]{1,0:T(8,128)S(1)} %slice_add_fusion), channel_id=1, source_target_pairs={{0,2},{1,3},{2,0},{3,1},{4,6},{5,7},{6,4},{7,5},{8,10},{9,11},{10,... | collective-permute-start | bytes 393224 | tf_op jit(solution)/shard_map/ppermute | solution.py:290
  44.2 4.2 %collective-permute-start.13 = (f32[2,4096]{1,0:T(2,128)S(1)}, f32[2,4096]{1,0:T(2,128)S(1)}, u32[]{:S(2)}, u32[]{:S(2)}) collective-permute-start(f32[2,4096]{1,0:T(2,128)S(1)} %get-tuple-element.37), channel_id=1, source_target_pairs={{0,4},{1,5},{2,6},{3,7},{4,0},{5,1},{6,2},{7,3},{8,12},{9,13},{10,... | collective-permute-start | bytes 98312 | tf_op jit(solution)/shard_map/ppermute | solution.py:290
  46.3 5.7 %collective-permute-start.15 = (f32[2,4096]{1,0:T(2,128)S(1)}, f32[2,4096]{1,0:T(2,128)S(1)}, u32[]{:S(2)}, u32[]{:S(2)}) collective-permute-start(f32[2,4096]{1,0:T(2,128)S(1)} %get-tuple-element.38), channel_id=1, source_target_pairs={{0,12},{1,13},{2,14},{3,15},{4,8},{5,9},{6,10},{7,11},{8,4},{9,5},... | collective-permute-start | bytes 98312 | tf_op jit(solution)/shard_map/ppermute | solution.py:290
  48.5 4.8 %collective-permute-start.14 = (f32[2,4096]{1,0:T(2,128)S(1)}, f32[2,4096]{1,0:T(2,128)S(1)}, u32[]{:S(2)}, u32[]{:S(2)}) collective-permute-start(f32[2,4096]{1,0:T(2,128)S(1)} %get-tuple-element.39), channel_id=1, source_target_pairs={{0,8},{1,9},{2,10},{3,11},{4,12},{5,13},{6,14},{7,15},{8,0},{9,1},... | collective-permute-start | bytes 98312 | tf_op jit(solution)/shard_map/ppermute | solution.py:290
where the time goes:
time: 54.1 us; the launch traced here: 53.9 us
  waiting for transfers between devices  20.3 us (38%)
  starting transfers between devices  18.5 us (34%)
  Pallas kernels  13.6 us (25%)
  other arithmetic  0.72 us (1%)
  local copies, waits for them, and re-layouts  0.7 us (1%)
    ppermute x16, waiting for transfers between devices, swap(): return lax.ppermute(x, 'blk', [(i, i ^ mask) for i in range(blocks)])  20.3 us
    ppermute x16, starting transfers between devices, swap(): return lax.ppermute(x, 'blk', [(i, i ^ mask) for i in range(blocks)])  18.5 us
    pallas_call x1, Pallas kernels, attend(): pl.pallas_call(functools.partial(attend_kernel, bits, local_rows, kv_held...  6.84 us
    pallas_call x1, Pallas kernels, split_weight(): pl.pallas_call(functools.partial(split_kernel, tile), out_shape=[out, out...  3.62 us
    pallas_call x1, Pallas kernels, project(): pl.pallas_call(functools.partial(project_kernel, swap, min(width, 512)),...  1.68 us
    pallas_call x1, Pallas kernels, pack(): pl.pallas_call(functools.partial(pack_kernel, sub), out_shape=[kv] * KVH...  1.21 us
  transfers between devices with their start and end apart: 16, of which 8 were waited for; matrix products, arithmetic and copies ran while one was open for 0% of the time, Pallas kernels for 7%

commit v1 on v0

--- a/solution.py
+++ b/solution.py
@@ -174,27 +174,29 @@
     scale = 1.0 / math.sqrt(HD)
 
     half = GROUP // 2
+    cross = jnp.broadcast_to(visible[None], (half, rows, held))
     for ref, start in ((send_ref, half), (keep_ref, 0)):
-        peaks, totals = [], []
-        for i in range(half):
-            head = start + i
+        heads = []
+        for head in range(start, start + half):
             owner = place ^ reverse_bits(head // per_owner, bits)
             lanes = pl.ds(pl.multiple_of((owner * per_owner + head % per_owner) * HD, HD), HD)
-            q = jnp.concatenate([q_ref[:, lanes] for q_ref in q_refs], axis=0)
-            q1, q2, q3 = pieces_of(q, 3)
-            q11, q22 = jnp.concatenate([q1, q1], axis=1), jnp.concatenate([q2, q2], axis=1)
-            q13 = jnp.concatenate([q1, q3], axis=1)
-            top = times(jnp.concatenate([q11, q22], axis=0), k12, both)
-            scores = (top[:rows] + (top[rows:] + times(q13, k31, both))) * scale
-            masked = jnp.where(visible, scores, NEG_FILL)
-            peak = jnp.max(masked, axis=1, keepdims=True)
-            weights = jnp.where(visible, jnp.exp(masked - peak), 0.0)
-            w1, w2 = pieces_of(weights, 2)
-            wide = times(w1, v12)
-            ref[:, i * HD : (i + 1) * HD] = wide[:, :HD] + (wide[:, HD:] + times(w2, v1))
-            peaks.append(peak)
-            totals.append(jnp.sum(weights, axis=1, keepdims=True))
-        ref[:, half * HD :] = lanes_of(peaks + totals, rows)
+            heads += [q_ref[:, lanes] for q_ref in q_refs]
+        q1, q2, q3 = pieces_of(jnp.concatenate(heads, axis=0), 3)
+        q11, q22 = jnp.concatenate([q1, q1], axis=1), jnp.concatenate([q2, q2], axis=1)
+        q13 = jnp.concatenate([q1, q3], axis=1)
+        scores = times(q11, k12, both) + (times(q22, k12, both) + times(q13, k31, both))
+        scores = scores.reshape(half, rows, held) * scale
+        masked = jnp.where(cross, scores, NEG_FILL)
+        peak = jnp.max(masked, axis=2, keepdims=True)
+        weights = jnp.where(cross, jnp.exp(masked - peak), 0.0)
+        total = jnp.sum(weights, axis=2, keepdims=True)
+        w1, w2 = pieces_of(weights.reshape(half * rows, held), 2)
+        wide = times(w1, v12)
+        sums = wide[:, :HD] + (wide[:, HD:] + times(w2, v1))
+        for i in range(half):
+            ref[:, i * HD : (i + 1) * HD] = sums[i * rows : (i + 1) * rows]
+        stats = [peak[i] for i in range(half)] + [total[i] for i in range(half)]
+        ref[:, half * HD :] = lanes_of(stats, rows)
 
 
 def attend(bits, local_rows, lengths, q_parts, kv_held):

time: 54.1 us -> 49.1 us (0.908)
  Pallas kernels: 13.6 us -> 8.59 us
    pallas_call x1, Pallas kernels: 6.84 us -> 1.83 us  [attend(): pl.pallas_call(functools.partial(attend_kernel, bits, local_rows, kv_held...]
where the time goes in v1:
time: 49.1 us; the launch traced here: 48.9 us
  waiting for transfers between devices  20.3 us (41%)
  starting transfers between devices  18.5 us (38%)
  Pallas kernels  8.59 us (17%)
  other arithmetic  0.72 us (1%)
  local copies, waits for them, and re-layouts  0.7 us (1%)
    ppermute x16, waiting for transfers between devices, swap(): return lax.ppermute(x, 'blk', [(i, i ^ mask) for i in range(blocks)])  20.3 us
    ppermute x16, starting transfers between devices, swap(): return lax.ppermute(x, 'blk', [(i, i ^ mask) for i in range(blocks)])  18.5 us
    pallas_call x1, Pallas kernels, split_weight(): pl.pallas_call(functools.partial(split_kernel, tile), out_shape=[out, out...  3.62 us
    pallas_call x1, Pallas kernels, attend(): pl.pallas_call(functools.partial(attend_kernel, bits, local_rows, kv_held...  1.83 us
    pallas_call x1, Pallas kernels, project(): pl.pallas_call(functools.partial(project_kernel, swap, min(width, 512)),...  1.68 us
    pallas_call x1, Pallas kernels, pack(): pl.pallas_call(functools.partial(pack_kernel, sub), out_shape=[kv] * KVH...  1.21 us
  transfers between devices with their start and end apart: 16, of which 8 were waited for; matrix products, arithmetic and copies ran while one was open for 0% of the time, Pallas kernels for 7%

profile of v1, /device:TPU:0, one launch (start us, length us, event | category | flops | bytes accessed | tf_op | source)
XLA Modules:
  0.0 48.9 jit_solution(6390503475270882420)
XLA Ops:
  0.0 1.2 %pack.1 = (f32[256,128]{1,0:T(8,128)S(1)}, f32[256,128]{1,0:T(8,128)S(1)}, f32[256,128]{1,0:T(8,128)S(1)}, f32[256,128]{1,0:T(8,128)S(1)}, f32[2,2048]{1,0:T(2,1...) custom-call(f32[2,8192]{1,0:T(2,128)} %q_hbm.1, f32[128,512]{1,0:T(8,128)} %k_hbm.1, ...), custom_call_target="tpu_custom_call" | custom-call | tf_op jit(solution)/shard_map/pack/pallas_call | solution.py:94
  1.2 3.1 %collective-permute-start = (f32[2,2048]{1,0:T(2,128)S(1)}, f32[2,2048]{1,0:T(2,128)S(1)}, u32[]{:S(2)}, u32[]{:S(2)}) collective-permute-start(f32[2,2048]{1,0:T(2,128)S(1)} %get-tuple-element.22), channel_id=1, source_target_pairs={{0,4},{1,5},{2,6},{3,7},{4,0},{5,1},{6,2},{7,3},{8,12},{9,13},{10,... | collective-permute-start | bytes 49160 | tf_op jit(solution)/shard_map/ppermute | solution.py:292
  4.3 2.6 %collective-permute-start.1 = (f32[2,2048]{1,0:T(2,128)S(1)}, f32[2,2048]{1,0:T(2,128)S(1)}, u32[]{:S(2)}, u32[]{:S(2)}) collective-permute-start(f32[2,2048]{1,0:T(2,128)S(1)} %get-tuple-element.23), channel_id=1, source_target_pairs={{0,8},{1,9},{2,10},{3,11},{4,12},{5,13},{6,14},{7,15},{8,0},{9,1},... | collective-permute-start | bytes 49160 | tf_op jit(solution)/shard_map/ppermute | solution.py:292
  6.9 0.0 collective-permute-start.2
  6.9 0.9 %collective-permute-start.6 = (f32[256,128]{1,0:T(8,128)S(1)}, f32[256,128]{1,0:T(8,128)S(1)}, u32[]{:S(2)}, u32[]{:S(2)}) collective-permute-start(f32[256,128]{1,0:T(8,128)S(1)} %get-tuple-element.26), channel_id=1, source_target_pairs={{0,4},{1,5},{2,6},{3,7},{4,0},{5,1},{6,2},{7,3},{8,12},{9,13},{10,... | collective-permute-start | bytes 393224 | tf_op jit(solution)/shard_map/ppermute | solution.py:292
  7.8 3.5 %collective-permute-start.7 = (f32[256,128]{1,0:T(8,128)S(1)}, f32[256,128]{1,0:T(8,128)S(1)}, u32[]{:S(2)}, u32[]{:S(2)}) collective-permute-start(f32[256,128]{1,0:T(8,128)S(1)} %get-tuple-element.27), channel_id=1, source_target_pairs={{0,8},{1,9},{2,10},{3,11},{4,12},{5,13},{6,14},{7,15},{8,0},{9,1},... | collective-permute-start | bytes 393224 | tf_op jit(solution)/shard_map/ppermute | solution.py:292
  11.3 0.0 collective-permute-done
  11.3 1.4 %collective-permute-done.2 = f32[2,2048]{1,0:T(2,128)S(1)} collective-permute-done((f32[2,2048]{1,0:T(2,128)S(1)}, f32[2,2048]{1,0:T(2,128)S(1)}, u32[]{:S(2)}, u32[]{:S(2)}) %collective-permute-start.2) | collective-permute-done | bytes 16416 | tf_op jit(solution)/shard_map/ppermute | solution.py:292
  12.8 1.6 %collective-permute-start.3 = (f32[8,2048]{1,0:T(8,128)S(1)}, f32[8,2048]{1,0:T(8,128)S(1)}, u32[]{:S(2)}, u32[]{:S(2)}) collective-permute-start(f32[8,2048]{1,0:T(8,128)S(1)} %pad_maximum_fusion.refs_0_), channel_id=1, source_target_pairs={{0,2},{1,3},{2,0},{3,1},{4,6},{5,7},{6,4},{7,5},{8,10},{9,11},{10,... | collective-permute-start | bytes 196616 | tf_op jit(solution)/shard_map/ppermute | solution.py:292
  14.4 2.7 %collective-permute-done.3.refs_1_ = f32[8,2048]{1,0:T(8,128)S(1)} collective-permute-done((f32[8,2048]{1,0:T(8,128)S(1)}, f32[8,2048]{1,0:T(8,128)S(1)}, u32[]{:S(2)}, u32[]{:S(2)}) %collective-permute-start.3) | collective-permute-done | bytes 65568 | tf_op jit(solution)/shard_map/ppermute | solution.py:292
  17.1 0.0 collective-permute-start.5
  17.1 0.0 collective-permute-done.4.refs_2_
  17.1 3.8 %collective-permute-done.7.refs_6_ = f32[256,128]{1,0:T(8,128)S(1)} collective-permute-done((f32[256,128]{1,0:T(8,128)S(1)}, f32[256,128]{1,0:T(8,128)S(1)}, u32[]{:S(2)}, u32[]{:S(2)}) %collective-permute-start.7) | collective-permute-done | bytes 131104 | tf_op jit(solution)/shard_map/ppermute | solution.py:292
  20.9 0.0 collective-permute-done.8.refs_7_
  20.9 0.0 collective-permute-done.5.refs_3_
  20.9 0.7 %copy-done = s32[2]{0:T(128)S(1)} copy-done((s32[2]{0:T(128)S(1)}, s32[2]{0:T(128)}, u32[]{:S(2)}) %copy-start) | copy-done | bytes 32
  21.5 1.8 %attend.1 = (f32[32,1152]{1,0:T(8,128)S(1)}, f32[32,1152]{1,0:T(8,128)S(1)}) custom-call(s32[2]{0:T(128)S(1)} %copy-done, f32[8,2048]{1,0:T(8,128)S(1)} %pad_maximum_fusion.refs_0_, f32[8,2048]{1,0:T(8,128)S(1)} %collective-permute-done.3.refs_1_, f32[8,2048]{1,0:T(8,128)S(1)} %collective-permute-done.4.refs_2_, ...), custom_call_target="tpu_custom_call" | custom-call | tf_op jit(solution)/shard_map/attend/pallas_call | solution.py:206
  23.4 0.1 collective-permute-start.9
  23.5 1.4 %collective-permute-done.9.recv_ref = f32[32,1152]{1,0:T(8,128)S(1)} collective-permute-done((f32[32,1152]{1,0:T(8,128)S(1)}, f32[32,1152]{1,0:T(8,128)S(1)}, u32[]{:S(2)}, u32[]{:S(2)}) %collective-permute-start.9) | collective-permute-done | bytes 147488 | tf_op jit(solution)/shard_map/ppermute | solution.py:292
  24.8 0.3 merge.1
  25.1 1.6 %collective-permute-start.10 = (f32[32,640]{1,0:T(8,128)S(1)}, f32[32,640]{1,0:T(8,128)S(1)}, u32[]{:S(2)}, u32[]{:S(2)}) collective-permute-start(f32[32,640]{1,0:T(8,128)S(1)} %get-tuple-element.32), channel_id=1, source_target_pairs={{0,2},{1,3},{2,0},{3,1},{4,6},{5,7},{6,4},{7,5},{8,10},{9,11},{10,... | collective-permute-start | bytes 245768 | tf_op jit(solution)/shard_map/ppermute | solution.py:292
  26.7 3.6 %split.1 = (bf16[512,4096]{1,0:T(8,128)(2,1)S(1)}, bf16[512,4096]{1,0:T(8,128)(2,1)S(1)}) custom-call(f32[512,4096]{1,0:T(8,128)} %w_hbm.1), custom_call_target="tpu_custom_call" | custom-call | flops 16777216 | bytes 16777216 | tf_op jit(solution)/shard_map/split/pallas_call | solution.py:124
  30.3 1.7 %project.1 = (f32[16,4096]{1,0:T(8,128)S(1)}, f32[16,4096]{1,0:T(8,128)S(1)}) custom-call(f32[32,640]{1,0:T(8,128)S(1)} %get-tuple-element.31.keep_ref, f32[32,640]{1,0:T(8,128)S(1)} %collective-permute-done.10.recv_ref, bf16[512,4096]{1,0:T(8,128)(2,1)S(1)} %get-tuple-element.33.high_ref, bf16[512,4096]{1,0:T(8,128)(2,1)S(1)} %get-tuple-element.34.low_ref), custom_call_target="tpu_custom_call" | custom-call | tf_op jit(solution)/shard_map/project/pallas_call | solution.py:275
  32.0 1.5 %collective-permute-done.11 = f32[16,4096]{1,0:T(8,128)S(1)} collective-permute-done((f32[16,4096]{1,0:T(8,128)S(1)}, f32[16,4096]{1,0:T(8,128)S(1)}, u32[]{:S(2)}, u32[]{:S(2)}) %collective-permute-start.11) | collective-permute-done | bytes 262176 | tf_op jit(solution)/shard_map/ppermute | solution.py:292
  33.5 0.9 %collective-permute-start.12 = (f32[8,4096]{1,0:T(8,128)S(1)}, f32[8,4096]{1,0:T(8,128)S(1)}, u32[]{:S(2)}, u32[]{:S(2)}) collective-permute-start(f32[8,4096]{1,0:T(8,128)S(1)} %slice_add_fusion), channel_id=1, source_target_pairs={{0,2},{1,3},{2,0},{3,1},{4,6},{5,7},{6,4},{7,5},{8,10},{9,11},{10,... | collective-permute-start | bytes 393224 | tf_op jit(solution)/shard_map/ppermute | solution.py:292
  34.5 4.7 %collective-permute-done.12 = f32[8,4096]{1,0:T(8,128)S(1)} collective-permute-done((f32[8,4096]{1,0:T(8,128)S(1)}, f32[8,4096]{1,0:T(8,128)S(1)}, u32[]{:S(2)}, u32[]{:S(2)}) %collective-permute-start.12) | collective-permute-done | bytes 131104 | tf_op jit(solution)/shard_map/ppermute | solution.py:292
  39.2 2.0 %collective-permute-start.13 = (f32[2,4096]{1,0:T(2,128)S(1)}, f32[2,4096]{1,0:T(2,128)S(1)}, u32[]{:S(2)}, u32[]{:S(2)}) collective-permute-start(f32[2,4096]{1,0:T(2,128)S(1)} %get-tuple-element.37), channel_id=1, source_target_pairs={{0,4},{1,5},{2,6},{3,7},{4,0},{5,1},{6,2},{7,3},{8,12},{9,13},{10,... | collective-permute-start | bytes 98312 | tf_op jit(solution)/shard_map/ppermute | solution.py:292
  41.3 2.2 %collective-permute-start.15 = (f32[2,4096]{1,0:T(2,128)S(1)}, f32[2,4096]{1,0:T(2,128)S(1)}, u32[]{:S(2)}, u32[]{:S(2)}) collective-permute-start(f32[2,4096]{1,0:T(2,128)S(1)} %get-tuple-element.38), channel_id=1, source_target_pairs={{0,12},{1,13},{2,14},{3,15},{4,8},{5,9},{6,10},{7,11},{8,4},{9,5},... | collective-permute-start | bytes 98312 | tf_op jit(solution)/shard_map/ppermute | solution.py:292
  43.4 0.0 collective-permute-start.14
  43.5 3.5 %collective-permute-done.15 = f32[2,4096]{1,0:T(2,128)S(1)} collective-permute-done((f32[2,4096]{1,0:T(2,128)S(1)}, f32[2,4096]{1,0:T(2,128)S(1)}, u32[]{:S(2)}, u32[]{:S(2)}) %collective-permute-start.15) | collective-permute-done | bytes 32800 | tf_op jit(solution)/shard_map/ppermute | solution.py:292
  47.0 1.3 %collective-permute-done.14 = f32[2,4096]{1,0:T(2,128)S(1)} collective-permute-done((f32[2,4096]{1,0:T(2,128)S(1)}, f32[2,4096]{1,0:T(2,128)S(1)}, u32[]{:S(2)}, u32[]{:S(2)}) %collective-permute-start.14) | collective-permute-done | bytes 32800 | tf_op jit(solution)/shard_map/ppermute | solution.py:292
  48.3 0.6 %fusion.2 = f32[2,4096]{1,0:T(2,128)} fusion(f32[2,4096]{1,0:T(2,128)S(1)} %collective-permute-done.15, f32[2,4096]{1,0:T(2,128)S(1)} %collective-permute-done.14, f32[2,4096]{1,0:T(2,128)S(1)} %collective-permute-done.13, f32[8,4096]{1,0:T(8,128)S(1)} %fusion), kind=kLoop, calls=%fused_computation.6 | loop fusion | flops 24576 | bytes 163840 | tf_op jit(solution)/shard_map/add | solution.py:316
  (12 shorter events, 0.1 us)
Async XLA Ops:
  1.2 10.1 %collective-permute-start = (f32[2,2048]{1,0:T(2,128)S(1)}, f32[2,2048]{1,0:T(2,128)S(1)}, u32[]{:S(2)}, u32[]{:S(2)}) collective-permute-start(f32[2,2048]{1,0:T(2,128)S(1)} %get-tuple-element.22), channel_id=1, source_target_pairs={{0,4},{1,5},{2,6},{3,7},{4,0},{5,1},{6,2},{7,3},{8,12},{9,13},{10,... | collective-permute-start | bytes 49160 | tf_op jit(solution)/shard_map/ppermute | solution.py:292
  4.3 7.0 %collective-permute-start.1 = (f32[2,2048]{1,0:T(2,128)S(1)}, f32[2,2048]{1,0:T(2,128)S(1)}, u32[]{:S(2)}, u32[]{:S(2)}) collective-permute-start(f32[2,2048]{1,0:T(2,128)S(1)} %get-tuple-element.23), channel_id=1, source_target_pairs={{0,8},{1,9},{2,10},{3,11},{4,12},{5,13},{6,14},{7,15},{8,0},{9,1},... | collective-permute-start | bytes 49160 | tf_op jit(solution)/shard_map/ppermute | solution.py:292
  6.9 5.8 %collective-permute-start.2 = (f32[2,2048]{1,0:T(2,128)S(1)}, f32[2,2048]{1,0:T(2,128)S(1)}, u32[]{:S(2)}, u32[]{:S(2)}) collective-permute-start(f32[2,2048]{1,0:T(2,128)S(1)} %get-tuple-element.24), channel_id=1, source_target_pairs={{0,12},{1,13},{2,14},{3,15},{4,8},{5,9},{6,10},{7,11},{8,4},{9,5},... | collective-permute-start | bytes 49160 | tf_op jit(solution)/shard_map/ppermute | solution.py:292
  6.9 10.2 %collective-permute-start.6 = (f32[256,128]{1,0:T(8,128)S(1)}, f32[256,128]{1,0:T(8,128)S(1)}, u32[]{:S(2)}, u32[]{:S(2)}) collective-permute-start(f32[256,128]{1,0:T(8,128)S(1)} %get-tuple-element.26), channel_id=1, source_target_pairs={{0,4},{1,5},{2,6},{3,7},{4,0},{5,1},{6,2},{7,3},{8,12},{9,13},{10,... | collective-permute-start | bytes 393224 | tf_op jit(solution)/shard_map/ppermute | solution.py:292
  7.8 13.1 %collective-permute-start.7 = (f32[256,128]{1,0:T(8,128)S(1)}, f32[256,128]{1,0:T(8,128)S(1)}, u32[]{:S(2)}, u32[]{:S(2)}) collective-permute-start(f32[256,128]{1,0:T(8,128)S(1)} %get-tuple-element.27), channel_id=1, source_target_pairs={{0,8},{1,9},{2,10},{3,11},{4,12},{5,13},{6,14},{7,15},{8,0},{9,1},... | collective-permute-start | bytes 393224 | tf_op jit(solution)/shard_map/ppermute | solution.py:292
  11.3 9.6 %collective-permute-start.8 = (f32[256,128]{1,0:T(8,128)S(1)}, f32[256,128]{1,0:T(8,128)S(1)}, u32[]{:S(2)}, u32[]{:S(2)}) collective-permute-start(f32[256,128]{1,0:T(8,128)S(1)} %get-tuple-element.28), channel_id=1, source_target_pairs={{0,12},{1,13},{2,14},{3,15},{4,8},{5,9},{6,10},{7,11},{8,4},{9,5},... | collective-permute-start | bytes 393224 | tf_op jit(solution)/shard_map/ppermute | solution.py:292
  12.8 4.3 %collective-permute-start.3 = (f32[8,2048]{1,0:T(8,128)S(1)}, f32[8,2048]{1,0:T(8,128)S(1)}, u32[]{:S(2)}, u32[]{:S(2)}) collective-permute-start(f32[8,2048]{1,0:T(8,128)S(1)} %pad_maximum_fusion.refs_0_), channel_id=1, source_target_pairs={{0,2},{1,3},{2,0},{3,1},{4,6},{5,7},{6,4},{7,5},{8,10},{9,11},{10,... | collective-permute-start | bytes 196616 | tf_op jit(solution)/shard_map/ppermute | solution.py:292
  14.4 2.8 %collective-permute-start.4 = (f32[8,2048]{1,0:T(8,128)S(1)}, f32[8,2048]{1,0:T(8,128)S(1)}, u32[]{:S(2)}, u32[]{:S(2)}) collective-permute-start(f32[8,2048]{1,0:T(8,128)S(1)} %pad_maximum_fusion.refs_0_), channel_id=1, source_target_pairs={{0,1},{1,0},{2,3},{3,2},{4,5},{5,4},{6,7},{7,6},{8,9},{9,8},{10,11... | collective-permute-start | bytes 196616 | tf_op jit(solution)/shard_map/ppermute | solution.py:292
  17.1 3.8 %collective-permute-start.5 = (f32[8,2048]{1,0:T(8,128)S(1)}, f32[8,2048]{1,0:T(8,128)S(1)}, u32[]{:S(2)}, u32[]{:S(2)}) collective-permute-start(f32[8,2048]{1,0:T(8,128)S(1)} %collective-permute-done.3.refs_1_), channel_id=1, source_target_pairs={{0,1},{1,0},{2,3},{3,2},{4,5},{5,4},{6,7},{7,6},{8,9},{9,8},{10,11... | collective-permute-start | bytes 196616 | tf_op jit(solution)/shard_map/ppermute | solution.py:292
  20.9 0.7 %copy-start = (s32[2]{0:T(128)S(1)}, s32[2]{0:T(128)}, u32[]{:S(2)}) copy-start(s32[2]{0:T(128)} %len_ref.1) | copy-start | bytes 28
  23.4 1.4 %collective-permute-start.9 = (f32[32,1152]{1,0:T(8,128)S(1)}, f32[32,1152]{1,0:T(8,128)S(1)}, u32[]{:S(2)}, u32[]{:S(2)}) collective-permute-start(f32[32,1152]{1,0:T(8,128)S(1)} %get-tuple-element.30), channel_id=1, source_target_pairs={{0,1},{1,0},{2,3},{3,2},{4,5},{5,4},{6,7},{7,6},{8,9},{9,8},{10,11... | collective-permute-start | bytes 442376 | tf_op jit(solution)/shard_map/ppermute | solution.py:292
  25.1 5.2 %collective-permute-start.10 = (f32[32,640]{1,0:T(8,128)S(1)}, f32[32,640]{1,0:T(8,128)S(1)}, u32[]{:S(2)}, u32[]{:S(2)}) collective-permute-start(f32[32,640]{1,0:T(8,128)S(1)} %get-tuple-element.32), channel_id=1, source_target_pairs={{0,2},{1,3},{2,0},{3,1},{4,6},{5,7},{6,4},{7,5},{8,10},{9,11},{10,... | collective-permute-start | bytes 245768 | tf_op jit(solution)/shard_map/ppermute | solution.py:292
  32.0 1.5 %collective-permute-start.11 = (f32[16,4096]{1,0:T(8,128)S(1)}, f32[16,4096]{1,0:T(8,128)S(1)}, u32[]{:S(2)}, u32[]{:S(2)}) collective-permute-start(f32[16,4096]{1,0:T(8,128)S(1)} %get-tuple-element.36), channel_id=1, source_target_pairs={{0,1},{1,0},{2,3},{3,2},{4,5},{5,4},{6,7},{7,6},{8,9},{9,8},{10,11... | collective-permute-start | bytes 786440 | tf_op jit(solution)/shard_map/ppermute | solution.py:292
  33.5 5.6 %collective-permute-start.12 = (f32[8,4096]{1,0:T(8,128)S(1)}, f32[8,4096]{1,0:T(8,128)S(1)}, u32[]{:S(2)}, u32[]{:S(2)}) collective-permute-start(f32[8,4096]{1,0:T(8,128)S(1)} %slice_add_fusion), channel_id=1, source_target_pairs={{0,2},{1,3},{2,0},{3,1},{4,6},{5,7},{6,4},{7,5},{8,10},{9,11},{10,... | collective-permute-start | bytes 393224 | tf_op jit(solution)/shard_map/ppermute | solution.py:292
  39.2 4.2 %collective-permute-start.13 = (f32[2,4096]{1,0:T(2,128)S(1)}, f32[2,4096]{1,0:T(2,128)S(1)}, u32[]{:S(2)}, u32[]{:S(2)}) collective-permute-start(f32[2,4096]{1,0:T(2,128)S(1)} %get-tuple-element.37), channel_id=1, source_target_pairs={{0,4},{1,5},{2,6},{3,7},{4,0},{5,1},{6,2},{7,3},{8,12},{9,13},{10,... | collective-permute-start | bytes 98312 | tf_op jit(solution)/shard_map/ppermute | solution.py:292
  41.3 5.7 %collective-permute-start.15 = (f32[2,4096]{1,0:T(2,128)S(1)}, f32[2,4096]{1,0:T(2,128)S(1)}, u32[]{:S(2)}, u32[]{:S(2)}) collective-permute-start(f32[2,4096]{1,0:T(2,128)S(1)} %get-tuple-element.38), channel_id=1, source_target_pairs={{0,12},{1,13},{2,14},{3,15},{4,8},{5,9},{6,10},{7,11},{8,4},{9,5},... | collective-permute-start | bytes 98312 | tf_op jit(solution)/shard_map/ppermute | solution.py:292
  43.4 4.8 %collective-permute-start.14 = (f32[2,4096]{1,0:T(2,128)S(1)}, f32[2,4096]{1,0:T(2,128)S(1)}, u32[]{:S(2)}, u32[]{:S(2)}) collective-permute-start(f32[2,4096]{1,0:T(2,128)S(1)} %get-tuple-element.39), channel_id=1, source_target_pairs={{0,8},{1,9},{2,10},{3,11},{4,12},{5,13},{6,14},{7,15},{8,0},{9,1},... | collective-permute-start | bytes 98312 | tf_op jit(solution)/shard_map/ppermute | solution.py:292

commit v2 on v1

--- a/solution.py
+++ b/solution.py
@@ -14,6 +14,7 @@
 HD = 128
 REQ_TOK = 16
 GROUP = H // KVH
+PLANE_BITS = KVH.bit_length() - 1
 LANES = 128
 
 HIGHEST = lax.Precision.HIGHEST
@@ -27,6 +28,15 @@
     out = 0
     for b in range(bits):
         out |= ((value >> b) & 1) << (bits - 1 - b)
+    return out
+
+
+def relative(order, bits):
+    out = 0
+    for b in range(PLANE_BITS):
+        out = out + (((order >> (PLANE_BITS - 1 - b)) & 1) << (bits + b))
+    for b in range(bits):
+        out = out + (((order >> (PLANE_BITS + bits - 1 - b)) & 1) << b)
     return out
 
 
@@ -67,46 +77,61 @@
     return pltpu.with_memory_space_constraint(x, pltpu.HBM)
 
 
-def pack_kernel(sub, q_hbm, k_hbm, v_hbm, *refs):
-    outs, sems = refs[:-1], refs[-1]
-    plane = lax.axis_index("blk") // sub
-    keys, wide = k_hbm.shape[0], GROUP * HD
-    copies = []
-    for step in (2, 3, 1, 0) if KVH == 4 else range(KVH):
+def pack_kernel(bits, len_hbm, q_hbm, k_hbm, v_hbm, *refs):
+    kv_outs, q_outs, (limit_out, len_ref, sems) = refs[:KVH], refs[KVH:-3], refs[-3:]
+    position = lax.axis_index("blk")
+    plane = position >> bits
+    keys, wide, half = k_hbm.shape[0], GROUP * HD, KVH // 2
+    copies = [(len_hbm, len_ref)]
+    for step in reversed(range(KVH)):
         other = plane ^ step
-        lanes = pl.ds(pl.multiple_of(other * HD, HD), HD)
-        q_lanes = pl.ds(pl.multiple_of(other * wide, wide), wide)
-        copies += [
-            (k_hbm.at[:, lanes], outs[step].at[pl.ds(0, keys), :]),
-            (v_hbm.at[:, lanes], outs[step].at[pl.ds(keys, keys), :]),
-            (q_hbm.at[:, q_lanes], outs[KVH + step]),
-        ]
+        q_out = q_outs[0].at[:, pl.ds((step - half) * wide, wide)] if step >= half else q_outs[1 + step]
+        copies.append((q_hbm.at[:, pl.ds(pl.multiple_of(other * wide, wide), wide)], q_out))
+    for step in reversed(range(KVH)):
+        lanes = pl.ds(pl.multiple_of((plane ^ step) * HD, HD), HD)
+        copies.append((k_hbm.at[:, lanes], kv_outs[step].at[pl.ds(0, keys), :]))
+        copies.append((v_hbm.at[:, lanes], kv_outs[step].at[pl.ds(keys, keys), :]))
     copies = [pltpu.make_async_copy(src, dst, sems.at[i]) for i, (src, dst) in enumerate(copies)]
     for copy in copies:
         copy.start()
-    for copy in copies:
+    local_rows = q_hbm.shape[0]
+    row = lax.broadcasted_iota(jnp.int32, limit_out.shape, 0)
+    token = (position ^ relative(row // local_rows, bits)) * local_rows + row % local_rows
+    request = token // REQ_TOK
+    copies[0].wait()
+    limits = jnp.zeros(limit_out.shape, jnp.int32)
+    for i in range(len_ref.shape[0]):
+        limits = jnp.where(request == i, len_ref[i], limits)
+    limit_out[...] = limits
+    for copy in copies[1:]:
         copy.wait()
 
 
-def pack(sub, queries, keys, values):
+def pack(bits, lengths, queries, keys, values):
+    local_rows = queries.shape[0]
     kv = jax.ShapeDtypeStruct((2 * keys.shape[0], HD), jnp.float32)
-    q = jax.ShapeDtypeStruct((queries.shape[0], GROUP * HD), jnp.float32)
+    q = jax.ShapeDtypeStruct((local_rows, GROUP * HD), jnp.float32)
+    q_high = jax.ShapeDtypeStruct((local_rows, KVH // 2 * GROUP * HD), jnp.float32)
+    limits = jax.ShapeDtypeStruct(((KVH << bits) * local_rows, LANES), jnp.int32)
     out = pl.pallas_call(
-        functools.partial(pack_kernel, sub),
-        out_shape=[kv] * KVH + [q] * KVH,
-        in_specs=[IN_PLACE] * 3,
-        out_specs=[IN_VMEM] * (2 * KVH),
-        scratch_shapes=[pltpu.SemaphoreType.DMA((3 * KVH,))],
+        functools.partial(pack_kernel, bits),
+        out_shape=[kv] * KVH + [q_high] + [q] * (KVH // 2) + [limits],
+        in_specs=[IN_PLACE] * 4,
+        out_specs=[IN_VMEM] * (KVH + KVH // 2 + 2),
+        scratch_shapes=[
+            pltpu.SMEM(lengths.shape, jnp.int32),
+            pltpu.SemaphoreType.DMA((1 + 3 * KVH,)),
+        ],
         compiler_params=limit(4),
         name="pack",
-    )(in_hbm(queries), in_hbm(keys), in_hbm(values))
-    return out[:KVH], out[KVH:]
-
-
-def split_kernel(tile, w_hbm, high_ref, low_ref, buf, sems):
-    chunks = w_hbm.shape[0] // tile
+    )(*map(in_hbm, (lengths, queries, keys, values)))
+    return out[:KVH], out[KVH:-1], out[-1]
+
+
+def split_kernel(first, tile, w_hbm, high_ref, low_ref, buf, sems):
+    chunks = buf.shape[0]
     copies = [
-        pltpu.make_async_copy(w_hbm.at[pl.ds(c * tile, tile), :], buf.at[c], sems.at[c])
+        pltpu.make_async_copy(w_hbm.at[pl.ds(first + c * tile, tile), :], buf.at[c], sems.at[c])
         for c in range(chunks)
     ]
     for copy in copies:
@@ -117,52 +142,40 @@
         high_ref[rows, :], low_ref[rows, :] = pieces_of(buf[c], 2)
 
 
-def split_weight(weight):
-    features, width = weight.shape
-    tile = min(features, 64)
-    out = jax.ShapeDtypeStruct((features, width), jnp.bfloat16)
+def split_weight(weight, first, count):
+    width = weight.shape[1]
+    tile = min(count, 64)
+    out = jax.ShapeDtypeStruct((count, width), jnp.bfloat16)
     return pl.pallas_call(
-        functools.partial(split_kernel, tile),
+        functools.partial(split_kernel, first, tile),
         out_shape=[out, out],
         in_specs=[IN_PLACE],
         out_specs=[IN_VMEM] * 2,
         scratch_shapes=[
-            pltpu.VMEM((features // tile, tile, width), jnp.float32),
-            pltpu.SemaphoreType.DMA((features // tile,)),
+            pltpu.VMEM((count // tile, tile, width), jnp.float32),
+            pltpu.SemaphoreType.DMA((count // tile,)),
         ],
-        compiler_params=limit(20),
+        compiler_params=limit(12),
         cost_estimate=pl.CostEstimate(
-            flops=8 * features * width, bytes_accessed=8 * features * width, transcendentals=0
+            flops=8 * count * width, bytes_accessed=8 * count * width, transcendentals=0
         ),
         name="split",
     )(in_hbm(weight))
 
 
-def attend_kernel(bits, local_rows, key_count, len_ref, *refs):
+def attend_kernel(bits, key_count, limit_ref, *refs):
     sub = 1 << bits
     q_refs, kv_refs = refs[:sub], refs[sub : sub + KVH]
     send_ref, keep_ref = refs[sub + KVH :]
     position = lax.axis_index("blk")
     plane, place = position // sub, position % sub
-    part = KVH * local_rows
-    rows = part * sub
+    rows = limit_ref.shape[0]
     per_owner = GROUP // sub
     held = key_count * KVH
 
-    row = lax.broadcasted_iota(jnp.int32, (rows, 1), 0)
-    order = row // part
-    within = row % part
-    rel = (within // local_rows) * sub
-    for b in range(bits):
-        rel = rel + ((order >> (bits - 1 - b)) & 1) * (1 << b)
-    token = (position ^ rel) * local_rows + within % local_rows
-    request = token // REQ_TOK
-    limits = jnp.zeros((rows, 1), jnp.int32)
-    for i in range(len_ref.shape[0]):
-        limits = jnp.where(request == i, len_ref[i], limits)
     at = lax.broadcasted_iota(jnp.int32, (1, held), 1)
     source = (plane ^ (at // key_count)) * sub + place
-    visible = (source * key_count + at % key_count) < limits
+    visible = (source * key_count + at % key_count) < limit_ref[:, :1]
 
     keys = jnp.concatenate([r[:key_count, :] for r in kv_refs], axis=0)
     values = jnp.concatenate([r[key_count:, :] for r in kv_refs], axis=0)
@@ -199,18 +212,16 @@
         ref[:, half * HD :] = lanes_of(stats, rows)
 
 
-def attend(bits, local_rows, lengths, q_parts, kv_held):
-    sub = 1 << bits
-    rows = KVH * local_rows * sub
-    out = jax.ShapeDtypeStruct((rows, GROUP // 2 * HD + LANES), jnp.float32)
+def attend(bits, limits, q_parts, kv_held):
+    out = jax.ShapeDtypeStruct((limits.shape[0], GROUP // 2 * HD + LANES), jnp.float32)
     return pl.pallas_call(
-        functools.partial(attend_kernel, bits, local_rows, kv_held[0].shape[0] // 2),
+        functools.partial(attend_kernel, bits, kv_held[0].shape[0] // 2),
         out_shape=[out, out],
-        in_specs=[pl.BlockSpec(memory_space=pltpu.SMEM)] + [IN_VMEM] * (sub + KVH),
+        in_specs=[IN_VMEM] * (1 + len(q_parts) + KVH),
         out_specs=[IN_VMEM] * 2,
         compiler_params=limit(16),
         name="attend",
-    )(lengths, *q_parts, *kv_held)
+    )(limits, *q_parts, *kv_held)
 
 
 def merged(keep_ref, recv_ref, swap):
@@ -254,32 +265,37 @@
     )(keep, recv)
 
 
-def project_kernel(swap, tile, keep_ref, recv_ref, high_ref, low_ref, send_out, keep_out):
+def project_kernel(swap, tile, keep_ref, recv_ref, *refs):
+    piece_refs, (send_out, keep_out) = refs[:-2], refs[-2:]
     sums, _, totals = merged(keep_ref, recv_ref, swap)
     attended = jnp.concatenate([a / t for a, t in zip(sums, totals)], axis=1)
     rows = attended.shape[0]
     half = rows // 2
     a1, a2 = pieces_of(attended, 2)
     a12 = jnp.concatenate([a1, a2], axis=0)
-    for c in range(high_ref.shape[1] // tile):
+    for c in range(keep_out.shape[1] // tile):
         cols = slice(c * tile, (c + 1) * tile)
-        top = times(a12, high_ref[:, cols])
-        out = top[:rows] + (top[rows:] + times(a1, low_ref[:, cols]))
+        out, first = 0.0, 0
+        for high_ref, low_ref in zip(piece_refs[::2], piece_refs[1::2]):
+            used = slice(first, first + high_ref.shape[0])
+            first = used.stop
+            top = times(a12[:, used], high_ref[:, cols])
+            out = out + (top[:rows] + (top[rows:] + times(a1[:, used], low_ref[:, cols])))
         keep_out[:, cols] = out[:half]
         send_out[:, cols] = out[half:]
 
 
-def project(swap, keep, recv, high, low):
-    width = high.shape[1]
+def project(swap, keep, recv, pieces):
+    width = pieces[0].shape[1]
     out = jax.ShapeDtypeStruct((keep.shape[0] // 2, width), jnp.float32)
     return pl.pallas_call(
         functools.partial(project_kernel, swap, min(width, 512)),
         out_shape=[out, out],
-        in_specs=[IN_VMEM] * 4,
+        in_specs=[IN_VMEM] * (2 + len(pieces)),
         out_specs=[IN_VMEM] * 2,
         compiler_params=limit(16),
         name="project",
-    )(keep, recv, high, low)
+    )(keep, recv, *pieces)
 
 
 def by_planes(bits, queries, keys, values, weight, lengths):
@@ -291,18 +307,32 @@
     def swap(x, mask):
         return lax.ppermute(x, "blk", [(i, i ^ mask) for i in range(blocks)])
 
-    kv_send, q_send = pack(sub, queries, keys, values)
+    kv_send, q_send, limits = pack(bits, lengths, queries, keys, values)
     kv_held = [kv_send[0]] + [swap(kv_send[k], k * sub) for k in range(1, KVH)]
-    q_rows = [q_send[0]] + [swap(q_send[k], k * sub) for k in range(1, KVH)]
-    q_parts = [jnp.concatenate(q_rows, axis=0)]
+    wide = GROUP * HD
+    q_rows = [[q] for q in q_send[1:]]
+    q_out = q_send[0]
+    for b in reversed(range(PLANE_BITS)):
+        q_in = swap(q_out, sub << b)
+        count = len(q_rows[0])
+        got = [q_in[:, i * wide : (i + 1) * wide] for i in range(q_in.shape[1] // wide)]
+        q_rows = [rows + got[t * count : (t + 1) * count] for t, rows in enumerate(q_rows)]
+        high = q_rows[len(q_rows) // 2 :]
+        if b:
+            q_out = jnp.concatenate([piece for rows in high for piece in rows], axis=1)
+            q_rows = q_rows[: len(q_rows) // 2]
+    q_parts = [jnp.concatenate(q_rows[0], axis=0)]
     for b in reversed(range(bits)):
         q_parts = q_parts + [swap(x, 1 << b) for x in q_parts]
-    high, low = split_weight(weight)
-
-    send, keep = attend(bits, local_rows, lengths, q_parts, kv_held)
+    features = weight.shape[0]
+    pieces = []
+    for i in range(2):
+        pieces += split_weight(weight, i * features // 2, features // 2)
+
+    send, keep = attend(bits, limits, q_parts, kv_held)
     for b in range(bits - 1):
         send, keep = merge(part << (bits - 1 - b), keep, swap(send, 1 << b))
-    send, keep = project(part, keep, swap(send, 1 << (bits - 1)), high, low)
+    send, keep = project(part, keep, swap(send, 1 << (bits - 1)), pieces)
 
     recv = swap(send, 1)
     for b in range(1, bits):
@@ -312,8 +342,9 @@
         recv = swap(send, 1 << b)
     total = keep + recv
     out = total[:local_rows]
-    for k in range(1, KVH):
-        out = out + swap(total[k * local_rows : (k + 1) * local_rows], k * sub)
+    for order in range(1, KVH):
+        k = relative(order, 0)
+        out = out + swap(total[order * local_rows : (order + 1) * local_rows], k * sub)
     return out
 
 

time: 49.1 us -> 50.1 us (1.020)
  waiting for transfers between devices: 20.3 us -> 21.6 us
  local copies, waits for them, and re-layouts: 0.7 us -> 0.05 us
    ppermute x16 -> x15, waiting for transfers between devices: 20.3 us -> 21.6 us  [swap(): return lax.ppermute(x, 'blk', [(i, i ^ mask) for i in range(blocks)])]
    unnamed x2 -> x0, local copies, waits for them, and re-layouts: 0.65 us -> none
    pallas_call x3 -> x4, Pallas kernels: 6.66 us -> 7.26 us  [the longest x2 4.71 us: split_weight(): pl.pallas_call(functools.partial(split_kernel, first, tile), out_shape=[o...]
    ppermute x16 -> x15, starting transfers between devices: 18.5 us -> 18.3 us  [swap(): return lax.ppermute(x, 'blk', [(i, i ^ mask) for i in range(blocks)])]
  transfers between devices with their start and end apart: 16 -> 15, of which waited for: 8 -> 8; matrix products, arithmetic and copies ran while one was open for 0% -> 0% of each run, Pallas kernels for 7% -> 9%
where the time goes in v2:
time: 50.1 us; the launch traced here: 49.9 us
  waiting for transfers between devices  21.6 us (43%)
  starting transfers between devices  18.3 us (37%)
  Pallas kernels  9.07 us (18%)
  other arithmetic  0.74 us (1%)
    ppermute x15, waiting for transfers between devices, swap(): return lax.ppermute(x, 'blk', [(i, i ^ mask) for i in range(blocks)])  21.6 us
    ppermute x15, starting transfers between devices, swap(): return lax.ppermute(x, 'blk', [(i, i ^ mask) for i in range(blocks)])  18.3 us
    pallas_call x2, Pallas kernels, split_weight(): pl.pallas_call(functools.partial(split_kernel, first, tile), out_shape=[o...  4.71 us
    pallas_call x1, Pallas kernels, project(): pl.pallas_call(functools.partial(project_kernel, swap, min(width, 512)),...  1.56 us
    pallas_call x1, Pallas kernels, attend(): pl.pallas_call(functools.partial(attend_kernel, bits, kv_held[0].shape[0]...  1.29 us
    pallas_call x1, Pallas kernels, pack(): pl.pallas_call(functools.partial(pack_kernel, bits), out_shape=[kv] * KVH...  1.26 us
  transfers between devices with their start and end apart: 15, of which 8 were waited for; matrix products, arithmetic and copies ran while one was open for 0% of the time, Pallas kernels for 9%

profile of v2, /device:TPU:0, one launch (start us, length us, event | category | flops | bytes accessed | tf_op | source)
XLA Modules:
  0.0 49.9 jit_solution(6989639815501437490)
XLA Ops:
  0.0 1.3 %pack.1 = (f32[256,128]{1,0:T(8,128)S(1)}, f32[256,128]{1,0:T(8,128)S(1)}, f32[256,128]{1,0:T(8,128)S(1)}, f32[256,128]{1,0:T(8,128)S(1)}, f32[2,4096]{1,0:T(2,1...) custom-call(s32[2]{0:T(128)} %len_hbm.1, f32[2,8192]{1,0:T(2,128)} %q_hbm.1, ...), custom_call_target="tpu_custom_call" | custom-call | tf_op jit(solution)/shard_map/pack/pallas_call | solution.py:116
  1.3 4.1 %collective-permute-start = (f32[2,4096]{1,0:T(2,128)S(1)}, f32[2,4096]{1,0:T(2,128)S(1)}, u32[]{:S(2)}, u32[]{:S(2)}) collective-permute-start(f32[2,4096]{1,0:T(2,128)S(1)} %get-tuple-element.25), channel_id=1, source_target_pairs={{0,8},{1,9},{2,10},{3,11},{4,12},{5,13},{6,14},{7,15},{8,0},{9,1},... | collective-permute-start | bytes 98312 | tf_op jit(solution)/shard_map/ppermute | solution.py:308
  5.4 2.2 %collective-permute-done = f32[2,4096]{1,0:T(2,128)S(1)} collective-permute-done((f32[2,4096]{1,0:T(2,128)S(1)}, f32[2,4096]{1,0:T(2,128)S(1)}, u32[]{:S(2)}, u32[]{:S(2)}) %collective-permute-start) | collective-permute-done | bytes 32800 | tf_op jit(solution)/shard_map/ppermute | solution.py:308
  7.7 1.6 %collective-permute-start.1 = (f32[2,4096]{1,0:T(2,128)S(1)}, f32[2,4096]{1,0:T(2,128)S(1)}, u32[]{:S(2)}, u32[]{:S(2)}) collective-permute-start(f32[2,4096]{1,0:T(2,128)S(1)} %pad_maximum_fusion.1), channel_id=1, source_target_pairs={{0,4},{1,5},{2,6},{3,7},{4,0},{5,1},{6,2},{7,3},{8,12},{9,13},{10,... | collective-permute-start | bytes 98312 | tf_op jit(solution)/shard_map/ppermute | solution.py:308
  9.3 0.5 collective-permute-start.5
  9.8 2.6 %collective-permute-start.6 = (f32[256,128]{1,0:T(8,128)S(1)}, f32[256,128]{1,0:T(8,128)S(1)}, u32[]{:S(2)}, u32[]{:S(2)}) collective-permute-start(f32[256,128]{1,0:T(8,128)S(1)} %get-tuple-element.29), channel_id=1, source_target_pairs={{0,8},{1,9},{2,10},{3,11},{4,12},{5,13},{6,14},{7,15},{8,0},{9,1},... | collective-permute-start | bytes 393224 | tf_op jit(solution)/shard_map/ppermute | solution.py:308
  12.3 1.3 %collective-permute-start.7 = (f32[256,128]{1,0:T(8,128)S(1)}, f32[256,128]{1,0:T(8,128)S(1)}, u32[]{:S(2)}, u32[]{:S(2)}) collective-permute-start(f32[256,128]{1,0:T(8,128)S(1)} %get-tuple-element.30), channel_id=1, source_target_pairs={{0,12},{1,13},{2,14},{3,15},{4,8},{5,9},{6,10},{7,11},{8,4},{9,5},... | collective-permute-start | bytes 393224 | tf_op jit(solution)/shard_map/ppermute | solution.py:308
  13.7 1.6 %collective-permute-start.2 = (f32[8,2048]{1,0:T(8,128)S(1)}, f32[8,2048]{1,0:T(8,128)S(1)}, u32[]{:S(2)}, u32[]{:S(2)}) collective-permute-start(f32[8,2048]{1,0:T(8,128)S(1)} %pad_maximum_fusion.refs_0_), channel_id=1, source_target_pairs={{0,2},{1,3},{2,0},{3,1},{4,6},{5,7},{6,4},{7,5},{8,10},{9,11},{10,... | collective-permute-start | bytes 196616 | tf_op jit(solution)/shard_map/ppermute | solution.py:308
  15.3 0.0 collective-permute-start.3
  15.3 2.7 %collective-permute-done.2.refs_1_ = f32[8,2048]{1,0:T(8,128)S(1)} collective-permute-done((f32[8,2048]{1,0:T(8,128)S(1)}, f32[8,2048]{1,0:T(8,128)S(1)}, u32[]{:S(2)}, u32[]{:S(2)}) %collective-permute-start.2) | collective-permute-done | bytes 65568 | tf_op jit(solution)/shard_map/ppermute | solution.py:308
  18.1 0.0 collective-permute-start.4
  18.1 0.0 collective-permute-done.3.refs_2_
  18.1 4.4 %collective-permute-done.6.refs_6_ = f32[256,128]{1,0:T(8,128)S(1)} collective-permute-done((f32[256,128]{1,0:T(8,128)S(1)}, f32[256,128]{1,0:T(8,128)S(1)}, u32[]{:S(2)}, u32[]{:S(2)}) %collective-permute-start.6) | collective-permute-done | bytes 131104 | tf_op jit(solution)/shard_map/ppermute | solution.py:308
  22.4 1.3 %attend.1 = (f32[32,1152]{1,0:T(8,128)S(1)}, f32[32,1152]{1,0:T(8,128)S(1)}) custom-call(s32[32,128]{1,0:T(8,128)S(1)} %get-tuple-element.23.limit_ref, f32[8,2048]{1,0:T(8,128)S(1)} %pad_maximum_fusion.refs_0_, f32[8,2048]{1,0:T(8,128)S(1)} %collective-permute-done.2.refs_1_, f32[8,2048]{1,0:T(8,128)S(1)} %collective-permute-done.3.refs_2_, ...), custom_call_target="tpu_custom_call" | custom-call | tf_op jit(solution)/shard_map/attend/pallas_call | solution.py:217
  23.7 0.1 collective-permute-start.8
  23.8 1.4 %collective-permute-done.8.recv_ref = f32[32,1152]{1,0:T(8,128)S(1)} collective-permute-done((f32[32,1152]{1,0:T(8,128)S(1)}, f32[32,1152]{1,0:T(8,128)S(1)}, u32[]{:S(2)}, u32[]{:S(2)}) %collective-permute-start.8) | collective-permute-done | bytes 147488 | tf_op jit(solution)/shard_map/ppermute | solution.py:308
  25.2 0.3 merge.1
  25.4 1.6 %collective-permute-start.9 = (f32[32,640]{1,0:T(8,128)S(1)}, f32[32,640]{1,0:T(8,128)S(1)}, u32[]{:S(2)}, u32[]{:S(2)}) collective-permute-start(f32[32,640]{1,0:T(8,128)S(1)} %get-tuple-element.34), channel_id=1, source_target_pairs={{0,2},{1,3},{2,0},{3,1},{4,6},{5,7},{6,4},{7,5},{8,10},{9,11},{10,... | collective-permute-start | bytes 245768 | tf_op jit(solution)/shard_map/ppermute | solution.py:308
  27.0 2.4 %split.3 = (bf16[256,4096]{1,0:T(8,128)(2,1)S(1)}, bf16[256,4096]{1,0:T(8,128)(2,1)S(1)}) custom-call(f32[512,4096]{1,0:T(8,128)} %w_hbm.3), custom_call_target="tpu_custom_call" | custom-call | flops 8388608 | bytes 8388608 | tf_op jit(solution)/shard_map/split/pallas_call | solution.py:149
  29.4 2.4 %split.2 = (bf16[256,4096]{1,0:T(8,128)(2,1)S(1)}, bf16[256,4096]{1,0:T(8,128)(2,1)S(1)}) custom-call(f32[512,4096]{1,0:T(8,128)} %w_hbm.3), custom_call_target="tpu_custom_call" | custom-call | flops 8388608 | bytes 8388608 | tf_op jit(solution)/shard_map/split/pallas_call | solution.py:149
  31.8 0.0 collective-permute-done.9.recv_ref
  31.8 1.6 %project.1 = (f32[16,4096]{1,0:T(8,128)S(1)}, f32[16,4096]{1,0:T(8,128)S(1)}) custom-call(f32[32,640]{1,0:T(8,128)S(1)} %get-tuple-element.33.keep_ref, f32[32,640]{1,0:T(8,128)S(1)} %collective-permute-done.9.recv_ref, bf16[256,4096]{1,0:T(8,128)(2,1)S(1)} %get-tuple-element.35.refs_0_, bf16[256,4096]{1,0:T(8,128)(2,1)S(1)} %get-tuple-element.36.refs_1_, ...), custom_call_target="tpu_custom_call" | custom-call | tf_op jit(solution)/shard_map/project/pallas_call | solution.py:291
  33.3 0.0 collective-permute-start.10
  33.3 1.5 %collective-permute-done.10 = f32[16,4096]{1,0:T(8,128)S(1)} collective-permute-done((f32[16,4096]{1,0:T(8,128)S(1)}, f32[16,4096]{1,0:T(8,128)S(1)}, u32[]{:S(2)}, u32[]{:S(2)}) %collective-permute-start.10) | collective-permute-done | bytes 262176 | tf_op jit(solution)/shard_map/ppermute | solution.py:308
  34.9 0.6 %collective-permute-start.11 = (f32[8,4096]{1,0:T(8,128)S(1)}, f32[8,4096]{1,0:T(8,128)S(1)}, u32[]{:S(2)}, u32[]{:S(2)}) collective-permute-start(f32[8,4096]{1,0:T(8,128)S(1)} %slice_add_fusion), channel_id=1, source_target_pairs={{0,2},{1,3},{2,0},{3,1},{4,6},{5,7},{6,4},{7,5},{8,10},{9,11},{10,... | collective-permute-start | bytes 393224 | tf_op jit(solution)/shard_map/ppermute | solution.py:308
  35.5 5.0 %collective-permute-done.11 = f32[8,4096]{1,0:T(8,128)S(1)} collective-permute-done((f32[8,4096]{1,0:T(8,128)S(1)}, f32[8,4096]{1,0:T(8,128)S(1)}, u32[]{:S(2)}, u32[]{:S(2)}) %collective-permute-start.11) | collective-permute-done | bytes 131104 | tf_op jit(solution)/shard_map/ppermute | solution.py:308
  40.6 2.9 %collective-permute-start.12 = (f32[2,4096]{1,0:T(2,128)S(1)}, f32[2,4096]{1,0:T(2,128)S(1)}, u32[]{:S(2)}, u32[]{:S(2)}) collective-permute-start(f32[2,4096]{1,0:T(2,128)S(1)} %get-tuple-element.41), channel_id=1, source_target_pairs={{0,8},{1,9},{2,10},{3,11},{4,12},{5,13},{6,14},{7,15},{8,0},{9,1},... | collective-permute-start | bytes 98312 | tf_op jit(solution)/shard_map/ppermute | solution.py:308
  43.5 1.4 %collective-permute-start.14 = (f32[2,4096]{1,0:T(2,128)S(1)}, f32[2,4096]{1,0:T(2,128)S(1)}, u32[]{:S(2)}, u32[]{:S(2)}) collective-permute-start(f32[2,4096]{1,0:T(2,128)S(1)} %get-tuple-element.42), channel_id=1, source_target_pairs={{0,12},{1,13},{2,14},{3,15},{4,8},{5,9},{6,10},{7,11},{8,4},{9,5},... | collective-permute-start | bytes 98312 | tf_op jit(solution)/shard_map/ppermute | solution.py:308
  45.0 0.0 collective-permute-start.13
  45.0 0.7 %collective-permute-done.12 = f32[2,4096]{1,0:T(2,128)S(1)} collective-permute-done((f32[2,4096]{1,0:T(2,128)S(1)}, f32[2,4096]{1,0:T(2,128)S(1)}, u32[]{:S(2)}, u32[]{:S(2)}) %collective-permute-start.12) | collective-permute-done | bytes 32800 | tf_op jit(solution)/shard_map/ppermute | solution.py:308
  45.6 3.6 %collective-permute-done.14 = f32[2,4096]{1,0:T(2,128)S(1)} collective-permute-done((f32[2,4096]{1,0:T(2,128)S(1)}, f32[2,4096]{1,0:T(2,128)S(1)}, u32[]{:S(2)}, u32[]{:S(2)}) %collective-permute-start.14) | collective-permute-done | bytes 32800 | tf_op jit(solution)/shard_map/ppermute | solution.py:308
  49.2 0.6 %fusion.2 = f32[2,4096]{1,0:T(2,128)} fusion(f32[2,4096]{1,0:T(2,128)S(1)} %collective-permute-done.14, f32[2,4096]{1,0:T(2,128)S(1)} %collective-permute-done.13, f32[2,4096]{1,0:T(2,128)S(1)} %collective-permute-done.12, f32[8,4096]{1,0:T(8,128)S(1)} %fusion), kind=kLoop, calls=%fused_computation.6 | loop fusion | flops 24576 | bytes 163840 | tf_op jit(solution)/shard_map/add | solution.py:347
  (12 shorter events, 0.2 us)
Async XLA Ops:
  1.3 6.4 %collective-permute-start = (f32[2,4096]{1,0:T(2,128)S(1)}, f32[2,4096]{1,0:T(2,128)S(1)}, u32[]{:S(2)}, u32[]{:S(2)}) collective-permute-start(f32[2,4096]{1,0:T(2,128)S(1)} %get-tuple-element.25), channel_id=1, source_target_pairs={{0,8},{1,9},{2,10},{3,11},{4,12},{5,13},{6,14},{7,15},{8,0},{9,1},... | collective-permute-start | bytes 98312 | tf_op jit(solution)/shard_map/ppermute | solution.py:308
  7.7 6.0 %collective-permute-start.1 = (f32[2,4096]{1,0:T(2,128)S(1)}, f32[2,4096]{1,0:T(2,128)S(1)}, u32[]{:S(2)}, u32[]{:S(2)}) collective-permute-start(f32[2,4096]{1,0:T(2,128)S(1)} %pad_maximum_fusion.1), channel_id=1, source_target_pairs={{0,4},{1,5},{2,6},{3,7},{4,0},{5,1},{6,2},{7,3},{8,12},{9,13},{10,... | collective-permute-start | bytes 98312 | tf_op jit(solution)/shard_map/ppermute | solution.py:308
  9.3 8.8 %collective-permute-start.5 = (f32[256,128]{1,0:T(8,128)S(1)}, f32[256,128]{1,0:T(8,128)S(1)}, u32[]{:S(2)}, u32[]{:S(2)}) collective-permute-start(f32[256,128]{1,0:T(8,128)S(1)} %get-tuple-element.28), channel_id=1, source_target_pairs={{0,4},{1,5},{2,6},{3,7},{4,0},{5,1},{6,2},{7,3},{8,12},{9,13},{10,... | collective-permute-start | bytes 393224 | tf_op jit(solution)/shard_map/ppermute | solution.py:308
  9.8 12.7 %collective-permute-start.6 = (f32[256,128]{1,0:T(8,128)S(1)}, f32[256,128]{1,0:T(8,128)S(1)}, u32[]{:S(2)}, u32[]{:S(2)}) collective-permute-start(f32[256,128]{1,0:T(8,128)S(1)} %get-tuple-element.29), channel_id=1, source_target_pairs={{0,8},{1,9},{2,10},{3,11},{4,12},{5,13},{6,14},{7,15},{8,0},{9,1},... | collective-permute-start | bytes 393224 | tf_op jit(solution)/shard_map/ppermute | solution.py:308
  12.3 10.1 %collective-permute-start.7 = (f32[256,128]{1,0:T(8,128)S(1)}, f32[256,128]{1,0:T(8,128)S(1)}, u32[]{:S(2)}, u32[]{:S(2)}) collective-permute-start(f32[256,128]{1,0:T(8,128)S(1)} %get-tuple-element.30), channel_id=1, source_target_pairs={{0,12},{1,13},{2,14},{3,15},{4,8},{5,9},{6,10},{7,11},{8,4},{9,5},... | collective-permute-start | bytes 393224 | tf_op jit(solution)/shard_map/ppermute | solution.py:308
  13.7 4.3 %collective-permute-start.2 = (f32[8,2048]{1,0:T(8,128)S(1)}, f32[8,2048]{1,0:T(8,128)S(1)}, u32[]{:S(2)}, u32[]{:S(2)}) collective-permute-start(f32[8,2048]{1,0:T(8,128)S(1)} %pad_maximum_fusion.refs_0_), channel_id=1, source_target_pairs={{0,2},{1,3},{2,0},{3,1},{4,6},{5,7},{6,4},{7,5},{8,10},{9,11},{10,... | collective-permute-start | bytes 196616 | tf_op jit(solution)/shard_map/ppermute | solution.py:308
  15.3 2.8 %collective-permute-start.3 = (f32[8,2048]{1,0:T(8,128)S(1)}, f32[8,2048]{1,0:T(8,128)S(1)}, u32[]{:S(2)}, u32[]{:S(2)}) collective-permute-start(f32[8,2048]{1,0:T(8,128)S(1)} %pad_maximum_fusion.refs_0_), channel_id=1, source_target_pairs={{0,1},{1,0},{2,3},{3,2},{4,5},{5,4},{6,7},{7,6},{8,9},{9,8},{10,11... | collective-permute-start | bytes 196616 | tf_op jit(solution)/shard_map/ppermute | solution.py:308
  18.1 4.4 %collective-permute-start.4 = (f32[8,2048]{1,0:T(8,128)S(1)}, f32[8,2048]{1,0:T(8,128)S(1)}, u32[]{:S(2)}, u32[]{:S(2)}) collective-permute-start(f32[8,2048]{1,0:T(8,128)S(1)} %collective-permute-done.2.refs_1_), channel_id=1, source_target_pairs={{0,1},{1,0},{2,3},{3,2},{4,5},{5,4},{6,7},{7,6},{8,9},{9,8},{10,11... | collective-permute-start | bytes 196616 | tf_op jit(solution)/shard_map/ppermute | solution.py:308
  23.7 1.4 %collective-permute-start.8 = (f32[32,1152]{1,0:T(8,128)S(1)}, f32[32,1152]{1,0:T(8,128)S(1)}, u32[]{:S(2)}, u32[]{:S(2)}) collective-permute-start(f32[32,1152]{1,0:T(8,128)S(1)} %get-tuple-element.32), channel_id=1, source_target_pairs={{0,1},{1,0},{2,3},{3,2},{4,5},{5,4},{6,7},{7,6},{8,9},{9,8},{10,11... | collective-permute-start | bytes 442376 | tf_op jit(solution)/shard_map/ppermute | solution.py:308
  25.4 6.3 %collective-permute-start.9 = (f32[32,640]{1,0:T(8,128)S(1)}, f32[32,640]{1,0:T(8,128)S(1)}, u32[]{:S(2)}, u32[]{:S(2)}) collective-permute-start(f32[32,640]{1,0:T(8,128)S(1)} %get-tuple-element.34), channel_id=1, source_target_pairs={{0,2},{1,3},{2,0},{3,1},{4,6},{5,7},{6,4},{7,5},{8,10},{9,11},{10,... | collective-permute-start | bytes 245768 | tf_op jit(solution)/shard_map/ppermute | solution.py:308
  33.3 1.6 %collective-permute-start.10 = (f32[16,4096]{1,0:T(8,128)S(1)}, f32[16,4096]{1,0:T(8,128)S(1)}, u32[]{:S(2)}, u32[]{:S(2)}) collective-permute-start(f32[16,4096]{1,0:T(8,128)S(1)} %get-tuple-element.40), channel_id=1, source_target_pairs={{0,1},{1,0},{2,3},{3,2},{4,5},{5,4},{6,7},{7,6},{8,9},{9,8},{10,11... | collective-permute-start | bytes 786440 | tf_op jit(solution)/shard_map/ppermute | solution.py:308
  34.9 5.6 %collective-permute-start.11 = (f32[8,4096]{1,0:T(8,128)S(1)}, f32[8,4096]{1,0:T(8,128)S(1)}, u32[]{:S(2)}, u32[]{:S(2)}) collective-permute-start(f32[8,4096]{1,0:T(8,128)S(1)} %slice_add_fusion), channel_id=1, source_target_pairs={{0,2},{1,3},{2,0},{3,1},{4,6},{5,7},{6,4},{7,5},{8,10},{9,11},{10,... | collective-permute-start | bytes 393224 | tf_op jit(solution)/shard_map/ppermute | solution.py:308
  40.6 5.0 %collective-permute-start.12 = (f32[2,4096]{1,0:T(2,128)S(1)}, f32[2,4096]{1,0:T(2,128)S(1)}, u32[]{:S(2)}, u32[]{:S(2)}) collective-permute-start(f32[2,4096]{1,0:T(2,128)S(1)} %get-tuple-element.41), channel_id=1, source_target_pairs={{0,8},{1,9},{2,10},{3,11},{4,12},{5,13},{6,14},{7,15},{8,0},{9,1},... | collective-permute-start | bytes 98312 | tf_op jit(solution)/shard_map/ppermute | solution.py:308
  43.5 5.7 %collective-permute-start.14 = (f32[2,4096]{1,0:T(2,128)S(1)}, f32[2,4096]{1,0:T(2,128)S(1)}, u32[]{:S(2)}, u32[]{:S(2)}) collective-permute-start(f32[2,4096]{1,0:T(2,128)S(1)} %get-tuple-element.42), channel_id=1, source_target_pairs={{0,12},{1,13},{2,14},{3,15},{4,8},{5,9},{6,10},{7,11},{8,4},{9,5},... | collective-permute-start | bytes 98312 | tf_op jit(solution)/shard_map/ppermute | solution.py:308
  45.0 4.3 %collective-permute-start.13 = (f32[2,4096]{1,0:T(2,128)S(1)}, f32[2,4096]{1,0:T(2,128)S(1)}, u32[]{:S(2)}, u32[]{:S(2)}) collective-permute-start(f32[2,4096]{1,0:T(2,128)S(1)} %get-tuple-element.43), channel_id=1, source_target_pairs={{0,4},{1,5},{2,6},{3,7},{4,0},{5,1},{6,2},{7,3},{8,12},{9,13},{10,... | collective-permute-start | bytes 98312 | tf_op jit(solution)/shard_map/ppermute | solution.py:308

commit v3 on v2

--- a/solution.py
+++ b/solution.py
@@ -77,23 +77,23 @@
     return pltpu.with_memory_space_constraint(x, pltpu.HBM)
 
 
-def pack_kernel(bits, len_hbm, q_hbm, k_hbm, v_hbm, *refs):
-    kv_outs, q_outs, (limit_out, len_ref, sems) = refs[:KVH], refs[KVH:-3], refs[-3:]
-    position = lax.axis_index("blk")
-    plane = position >> bits
-    keys, wide, half = k_hbm.shape[0], GROUP * HD, KVH // 2
-    copies = [(len_hbm, len_ref)]
-    for step in reversed(range(KVH)):
-        other = plane ^ step
-        q_out = q_outs[0].at[:, pl.ds((step - half) * wide, wide)] if step >= half else q_outs[1 + step]
-        copies.append((q_hbm.at[:, pl.ds(pl.multiple_of(other * wide, wide), wide)], q_out))
-    for step in reversed(range(KVH)):
-        lanes = pl.ds(pl.multiple_of((plane ^ step) * HD, HD), HD)
-        copies.append((k_hbm.at[:, lanes], kv_outs[step].at[pl.ds(0, keys), :]))
-        copies.append((v_hbm.at[:, lanes], kv_outs[step].at[pl.ds(keys, keys), :]))
-    copies = [pltpu.make_async_copy(src, dst, sems.at[i]) for i, (src, dst) in enumerate(copies)]
+def run_copies(pairs, sems):
+    copies = [pltpu.make_async_copy(src, dst, sems.at[i]) for i, (src, dst) in enumerate(pairs)]
     for copy in copies:
         copy.start()
+    return copies
+
+
+def pack_q_kernel(bits, len_hbm, q_hbm, *refs):
+    q_outs, (limit_out, len_ref, sems) = refs[:-3], refs[-3:]
+    position = lax.axis_index("blk")
+    wide, half = GROUP * HD, KVH // 2
+    pairs = [(len_hbm, len_ref)]
+    for step in reversed(range(KVH)):
+        lanes = pl.ds(pl.multiple_of(((position >> bits) ^ step) * wide, wide), wide)
+        q_out = q_outs[0].at[:, pl.ds((step - half) * wide, wide)] if step >= half else q_outs[1 + step]
+        pairs.append((q_hbm.at[:, lanes], q_out))
+    copies = run_copies(pairs, sems)
     local_rows = q_hbm.shape[0]
     row = lax.broadcasted_iota(jnp.int32, limit_out.shape, 0)
     token = (position ^ relative(row // local_rows, bits)) * local_rows + row % local_rows
@@ -107,25 +107,48 @@
         copy.wait()
 
 
-def pack(bits, lengths, queries, keys, values):
-    local_rows = queries.shape[0]
-    kv = jax.ShapeDtypeStruct((2 * keys.shape[0], HD), jnp.float32)
-    q = jax.ShapeDtypeStruct((local_rows, GROUP * HD), jnp.float32)
-    q_high = jax.ShapeDtypeStruct((local_rows, KVH // 2 * GROUP * HD), jnp.float32)
+def pack_q(bits, lengths, queries):
+    local_rows, wide = queries.shape[0], GROUP * HD
+    q_high = jax.ShapeDtypeStruct((local_rows, KVH // 2 * wide), jnp.float32)
+    q = jax.ShapeDtypeStruct((local_rows, wide), jnp.float32)
     limits = jax.ShapeDtypeStruct(((KVH << bits) * local_rows, LANES), jnp.int32)
     out = pl.pallas_call(
-        functools.partial(pack_kernel, bits),
-        out_shape=[kv] * KVH + [q_high] + [q] * (KVH // 2) + [limits],
-        in_specs=[IN_PLACE] * 4,
-        out_specs=[IN_VMEM] * (KVH + KVH // 2 + 2),
-        scratch_shapes=[
-            pltpu.SMEM(lengths.shape, jnp.int32),
-            pltpu.SemaphoreType.DMA((1 + 3 * KVH,)),
-        ],
+        functools.partial(pack_q_kernel, bits),
+        out_shape=[q_high] + [q] * (KVH // 2) + [limits],
+        in_specs=[IN_PLACE] * 2,
+        out_specs=[IN_VMEM] * (KVH // 2 + 2),
+        scratch_shapes=[pltpu.SMEM(lengths.shape, jnp.int32), pltpu.SemaphoreType.DMA((1 + KVH,))],
         compiler_params=limit(4),
-        name="pack",
-    )(*map(in_hbm, (lengths, queries, keys, values)))
-    return out[:KVH], out[KVH:-1], out[-1]
+        name="pack_q",
+    )(in_hbm(lengths), in_hbm(queries))
+    return out[:-1], out[-1]
+
+
+def pack_kv_kernel(bits, k_hbm, v_hbm, *refs):
+    kv_outs, sems = refs[:-1], refs[-1]
+    plane = lax.axis_index("blk") >> bits
+    keys = k_hbm.shape[0]
+    pairs = []
+    for step in reversed(range(KVH)):
+        lanes = pl.ds(pl.multiple_of((plane ^ step) * HD, HD), HD)
+        pairs.append((k_hbm.at[:, lanes], kv_outs[step].at[pl.ds(0, keys), :]))
+        pairs.append((v_hbm.at[:, lanes], kv_outs[step].at[pl.ds(keys, keys), :]))
+    for copy in run_copies(pairs, sems):
+        copy.wait()
+
+
+def pack_kv(bits, keys, values):
+    kv = jax.ShapeDtypeStruct((2 * keys.shape[0], HD), jnp.float32)
+    return pl.pallas_call(
+        functools.partial(pack_kv_kernel, bits),
+        out_shape=[kv] * KVH,
+        in_specs=[IN_PLACE] * 2,
+        out_specs=[IN_VMEM] * KVH,
+        scratch_shapes=[pltpu.SemaphoreType.DMA((2 * KVH,))],
+        compiler_params=limit(4),
+        cost_estimate=pl.CostEstimate(flops=0, bytes_accessed=16 * keys.size, transcendentals=0),
+        name="pack_kv",
+    )(in_hbm(keys), in_hbm(values))
 
 
 def split_kernel(first, tile, w_hbm, high_ref, low_ref, buf, sems):
@@ -163,10 +186,9 @@
     )(in_hbm(weight))
 
 
-def attend_kernel(bits, key_count, limit_ref, *refs):
+def attend_kernel(bits, key_count, start, limit_ref, *refs):
     sub = 1 << bits
-    q_refs, kv_refs = refs[:sub], refs[sub : sub + KVH]
-    send_ref, keep_ref = refs[sub + KVH :]
+    q_refs, kv_refs, ref = refs[: -KVH - 1], refs[-KVH - 1 : -1], refs[-1]
     position = lax.axis_index("blk")
     plane, place = position // sub, position % sub
     rows = limit_ref.shape[0]
@@ -188,38 +210,41 @@
 
     half = GROUP // 2
     cross = jnp.broadcast_to(visible[None], (half, rows, held))
-    for ref, start in ((send_ref, half), (keep_ref, 0)):
-        heads = []
-        for head in range(start, start + half):
-            owner = place ^ reverse_bits(head // per_owner, bits)
-            lanes = pl.ds(pl.multiple_of((owner * per_owner + head % per_owner) * HD, HD), HD)
-            heads += [q_ref[:, lanes] for q_ref in q_refs]
-        q1, q2, q3 = pieces_of(jnp.concatenate(heads, axis=0), 3)
-        q11, q22 = jnp.concatenate([q1, q1], axis=1), jnp.concatenate([q2, q2], axis=1)
-        q13 = jnp.concatenate([q1, q3], axis=1)
-        scores = times(q11, k12, both) + (times(q22, k12, both) + times(q13, k31, both))
-        scores = scores.reshape(half, rows, held) * scale
-        masked = jnp.where(cross, scores, NEG_FILL)
-        peak = jnp.max(masked, axis=2, keepdims=True)
-        weights = jnp.where(cross, jnp.exp(masked - peak), 0.0)
-        total = jnp.sum(weights, axis=2, keepdims=True)
-        w1, w2 = pieces_of(weights.reshape(half * rows, held), 2)
-        wide = times(w1, v12)
-        sums = wide[:, :HD] + (wide[:, HD:] + times(w2, v1))
-        for i in range(half):
-            ref[:, i * HD : (i + 1) * HD] = sums[i * rows : (i + 1) * rows]
-        stats = [peak[i] for i in range(half)] + [total[i] for i in range(half)]
-        ref[:, half * HD :] = lanes_of(stats, rows)
-
-
-def attend(bits, limits, q_parts, kv_held):
-    out = jax.ShapeDtypeStruct((limits.shape[0], GROUP // 2 * HD + LANES), jnp.float32)
+    heads = []
+    for head in range(start, start + half):
+        owner = place ^ reverse_bits(head // per_owner, bits)
+        lanes = pl.ds(pl.multiple_of((owner * per_owner + head % per_owner) * HD, HD), HD)
+        heads += [q_ref[:, lanes] for q_ref in q_refs]
+    q1, q2, q3 = pieces_of(jnp.concatenate(heads, axis=0), 3)
+    q11, q22 = jnp.concatenate([q1, q1], axis=1), jnp.concatenate([q2, q2], axis=1)
+    q13 = jnp.concatenate([q1, q3], axis=1)
+    scores = times(q11, k12, both) + (times(q22, k12, both) + times(q13, k31, both))
+    scores = scores.reshape(half, rows, held) * scale
+    masked = jnp.where(cross, scores, NEG_FILL)
+    peak = jnp.max(masked, axis=2, keepdims=True)
+    weights = jnp.where(cross, jnp.exp(masked - peak), 0.0)
+    total = jnp.sum(weights, axis=2, keepdims=True)
+    w1, w2 = pieces_of(weights.reshape(half * rows, held), 2)
+    wide = times(w1, v12)
+    sums = wide[:, :HD] + (wide[:, HD:] + times(w2, v1))
+    for i in range(half):
+        ref[:, i * HD : (i + 1) * HD] = sums[i * rows : (i + 1) * rows]
+    stats = [peak[i] for i in range(half)] + [total[i] for i in range(half)]
+    ref[:, half * HD :] = lanes_of(stats, rows)
+
+
+def attend(bits, start, limits, q_parts, kv_held):
+    rows, width, key_count = limits.shape[0], GROUP // 2 * HD, kv_held[0].shape[0] // 2
+    pairs = rows * GROUP // 2 * key_count * KVH
     return pl.pallas_call(
-        functools.partial(attend_kernel, bits, kv_held[0].shape[0] // 2),
-        out_shape=[out, out],
+        functools.partial(attend_kernel, bits, key_count, start),
+        out_shape=jax.ShapeDtypeStruct((rows, width + LANES), jnp.float32),
         in_specs=[IN_VMEM] * (1 + len(q_parts) + KVH),
-        out_specs=[IN_VMEM] * 2,
+        out_specs=IN_VMEM,
         compiler_params=limit(16),
+        cost_estimate=pl.CostEstimate(
+            flops=12 * pairs * HD, bytes_accessed=4 * rows * width, transcendentals=pairs
+        ),
         name="attend",
     )(limits, *q_parts, *kv_held)
 
@@ -307,7 +332,8 @@
     def swap(x, mask):
         return lax.ppermute(x, "blk", [(i, i ^ mask) for i in range(blocks)])
 
-    kv_send, q_send, limits = pack(bits, lengths, queries, keys, values)
+    q_send, limits = pack_q(bits, lengths, queries)
+    kv_send = pack_kv(bits, keys, values)
     kv_held = [kv_send[0]] + [swap(kv_send[k], k * sub) for k in range(1, KVH)]
     wide = GROUP * HD
     q_rows = [[q] for q in q_send[1:]]
@@ -329,7 +355,8 @@
     for i in range(2):
         pieces += split_weight(weight, i * features // 2, features // 2)
 
-    send, keep = attend(bits, limits, q_parts, kv_held)
+    send = attend(bits, GROUP // 2, limits, q_parts, kv_held)
+    keep = attend(bits, 0, limits, q_parts, kv_held)
     for b in range(bits - 1):
         send, keep = merge(part << (bits - 1 - b), keep, swap(send, 1 << b))
     send, keep = project(part, keep, swap(send, 1 << (bits - 1)), pieces)

time: 50.1 us -> 50.4 us (level)
  Pallas kernels: 9.07 us -> 9.96 us
  waiting for transfers between devices: 21.6 us -> 20.8 us
    pallas_call x2 -> x4, Pallas kernels: 2.55 us -> 3.44 us  [the longest x2 1.49 us: attend(): pl.pallas_call(functools.partial(attend_kernel, bits, key_count, start),...]
    ppermute x15, waiting for transfers between devices: 21.6 us -> 20.8 us  [swap(): return lax.ppermute(x, 'blk', [(i, i ^ mask) for i in range(blocks)])]
  transfers between devices with their start and end apart: 15 -> 15, of which waited for: 8 -> 8; matrix products, arithmetic and copies ran while one was open for 0% -> 0% of each run, Pallas kernels for 9% -> 13%
where the time goes in v3:
time: 50.4 us; the launch traced here: 50.1 us
  waiting for transfers between devices  20.8 us (41%)
  starting transfers between devices  18.4 us (37%)
  Pallas kernels  9.96 us (20%)
  other arithmetic  0.74 us (1%)
    ppermute x15, waiting for transfers between devices, swap(): return lax.ppermute(x, 'blk', [(i, i ^ mask) for i in range(blocks)])  20.8 us
    ppermute x15, starting transfers between devices, swap(): return lax.ppermute(x, 'blk', [(i, i ^ mask) for i in range(blocks)])  18.4 us
    pallas_call x2, Pallas kernels, split_weight(): pl.pallas_call(functools.partial(split_kernel, first, tile), out_shape=[o...  4.71 us
    pallas_call x1, Pallas kernels, project(): pl.pallas_call(functools.partial(project_kernel, swap, min(width, 512)),...  1.56 us
    pallas_call x2, Pallas kernels, attend(): pl.pallas_call(functools.partial(attend_kernel, bits, key_count, start),...  1.49 us
    pallas_call x1, Pallas kernels, pack_kv(): pl.pallas_call(functools.partial(pack_kv_kernel, bits), out_shape=[kv] *...  1.13 us
  transfers between devices with their start and end apart: 15, of which 8 were waited for; matrix products, arithmetic and copies ran while one was open for 0% of the time, Pallas kernels for 13%

profile of v3, /device:TPU:0, one launch (start us, length us, event | category | flops | bytes accessed | tf_op | source)
XLA Modules:
  0.0 50.1 jit_solution(7822328213406567863)
XLA Ops:
  0.0 0.8 %pack_q.1 = (f32[2,4096]{1,0:T(2,128)S(1)}, f32[2,2048]{1,0:T(2,128)S(1)}, f32[2,2048]{1,0:T(2,128)S(1)}, s32[32,128]{1,0:T(8,128)S(1)}) custom-call(s32[2]{0:T(128)} %len_hbm.1, f32[2,8192]{1,0:T(2,128)} %q_hbm.1), custom_call_target="tpu_custom_call" | custom-call | tf_op jit(solution)/shard_map/pack_q/pallas_call | solution.py:115
  0.8 4.1 %collective-permute-start = (f32[2,4096]{1,0:T(2,128)S(1)}, f32[2,4096]{1,0:T(2,128)S(1)}, u32[]{:S(2)}, u32[]{:S(2)}) collective-permute-start(f32[2,4096]{1,0:T(2,128)S(1)} %get-tuple-element.23), channel_id=1, source_target_pairs={{0,8},{1,9},{2,10},{3,11},{4,12},{5,13},{6,14},{7,15},{8,0},{9,1},... | collective-permute-start | bytes 98312 | tf_op jit(solution)/shard_map/ppermute | solution.py:333
  5.0 2.2 %collective-permute-done = f32[2,4096]{1,0:T(2,128)S(1)} collective-permute-done((f32[2,4096]{1,0:T(2,128)S(1)}, f32[2,4096]{1,0:T(2,128)S(1)}, u32[]{:S(2)}, u32[]{:S(2)}) %collective-permute-start) | collective-permute-done | bytes 32800 | tf_op jit(solution)/shard_map/ppermute | solution.py:333
  7.2 1.6 %collective-permute-start.1 = (f32[2,4096]{1,0:T(2,128)S(1)}, f32[2,4096]{1,0:T(2,128)S(1)}, u32[]{:S(2)}, u32[]{:S(2)}) collective-permute-start(f32[2,4096]{1,0:T(2,128)S(1)} %pad_maximum_fusion.1), channel_id=1, source_target_pairs={{0,4},{1,5},{2,6},{3,7},{4,0},{5,1},{6,2},{7,3},{8,12},{9,13},{10,... | collective-permute-start | bytes 98312 | tf_op jit(solution)/shard_map/ppermute | solution.py:333
  8.9 1.1 %pack_kv.1 = (f32[256,128]{1,0:T(8,128)S(1)}, f32[256,128]{1,0:T(8,128)S(1)}, f32[256,128]{1,0:T(8,128)S(1)}, f32[256,128]{1,0:T(8,128)S(1)}) custom-call(f32[128,512]{1,0:T(8,128)} %k_hbm.1, f32[128,512]{1,0:T(8,128)} %v_hbm.1), custom_call_target="tpu_custom_call" | custom-call | bytes 1048576 | tf_op jit(solution)/shard_map/pack_kv/pallas_call | solution.py:142
  10.0 0.5 %collective-permute-start.5 = (f32[256,128]{1,0:T(8,128)S(1)}, f32[256,128]{1,0:T(8,128)S(1)}, u32[]{:S(2)}, u32[]{:S(2)}) collective-permute-start(f32[256,128]{1,0:T(8,128)S(1)} %get-tuple-element.26), channel_id=1, source_target_pairs={{0,4},{1,5},{2,6},{3,7},{4,0},{5,1},{6,2},{7,3},{8,12},{9,13},{10,... | collective-permute-start | bytes 393224 | tf_op jit(solution)/shard_map/ppermute | solution.py:333
  10.5 2.6 %collective-permute-start.6 = (f32[256,128]{1,0:T(8,128)S(1)}, f32[256,128]{1,0:T(8,128)S(1)}, u32[]{:S(2)}, u32[]{:S(2)}) collective-permute-start(f32[256,128]{1,0:T(8,128)S(1)} %get-tuple-element.27), channel_id=1, source_target_pairs={{0,8},{1,9},{2,10},{3,11},{4,12},{5,13},{6,14},{7,15},{8,0},{9,1},... | collective-permute-start | bytes 393224 | tf_op jit(solution)/shard_map/ppermute | solution.py:333
  13.1 1.3 %collective-permute-start.7 = (f32[256,128]{1,0:T(8,128)S(1)}, f32[256,128]{1,0:T(8,128)S(1)}, u32[]{:S(2)}, u32[]{:S(2)}) collective-permute-start(f32[256,128]{1,0:T(8,128)S(1)} %get-tuple-element.28), channel_id=1, source_target_pairs={{0,12},{1,13},{2,14},{3,15},{4,8},{5,9},{6,10},{7,11},{8,4},{9,5},... | collective-permute-start | bytes 393224 | tf_op jit(solution)/shard_map/ppermute | solution.py:333
  14.5 1.6 %collective-permute-start.2 = (f32[8,2048]{1,0:T(8,128)S(1)}, f32[8,2048]{1,0:T(8,128)S(1)}, u32[]{:S(2)}, u32[]{:S(2)}) collective-permute-start(f32[8,2048]{1,0:T(8,128)S(1)} %pad_maximum_fusion.refs_0_), channel_id=1, source_target_pairs={{0,2},{1,3},{2,0},{3,1},{4,6},{5,7},{6,4},{7,5},{8,10},{9,11},{10,... | collective-permute-start | bytes 196616 | tf_op jit(solution)/shard_map/ppermute | solution.py:333
  16.1 0.0 collective-permute-start.3
  16.1 2.7 %collective-permute-done.2.refs_1_ = f32[8,2048]{1,0:T(8,128)S(1)} collective-permute-done((f32[8,2048]{1,0:T(8,128)S(1)}, f32[8,2048]{1,0:T(8,128)S(1)}, u32[]{:S(2)}, u32[]{:S(2)}) %collective-permute-start.2) | collective-permute-done | bytes 65568 | tf_op jit(solution)/shard_map/ppermute | solution.py:333
  18.8 0.0 collective-permute-start.4
  18.8 4.3 %collective-permute-done.6.refs_6_ = f32[256,128]{1,0:T(8,128)S(1)} collective-permute-done((f32[256,128]{1,0:T(8,128)S(1)}, f32[256,128]{1,0:T(8,128)S(1)}, u32[]{:S(2)}, u32[]{:S(2)}) %collective-permute-start.6) | collective-permute-done | bytes 131104 | tf_op jit(solution)/shard_map/ppermute | solution.py:333
  23.2 0.0 collective-permute-done.7.refs_7_
  23.2 0.0 collective-permute-done.4.refs_3_
  23.2 0.7 %attend.3 = f32[32,1152]{1,0:T(8,128)S(1)} custom-call(s32[32,128]{1,0:T(8,128)S(1)} %get-tuple-element.21.limit_ref, f32[8,2048]{1,0:T(8,128)S(1)} %pad_maximum_fusion.refs_0_, f32[8,2048]{1,0:T(8,128)S(1)} %collective-permute-done.2.refs_1_, f32[8,2048]{1,0:T(8,128)S(1)} %collective-permute-done.3.refs_2_, f32[8,2048]{1,0:T(8,128)S(1)} %collective-permute-done.4.refs_3_, ...), custom_call_target="tpu_custom_call" | custom-call | flops 201326592 | bytes 131072 | tf_op jit(solution)/shard_map/attend/pallas_call | solution.py:239
  23.9 0.1 collective-permute-start.8
  24.0 0.7 %attend.2.keep_ref = f32[32,1152]{1,0:T(8,128)S(1)} custom-call(s32[32,128]{1,0:T(8,128)S(1)} %get-tuple-element.21.limit_ref, f32[8,2048]{1,0:T(8,128)S(1)} %pad_maximum_fusion.refs_0_, f32[8,2048]{1,0:T(8,128)S(1)} %collective-permute-done.2.refs_1_, f32[8,2048]{1,0:T(8,128)S(1)} %collective-permute-done.3.refs_2_, ...), custom_call_target="tpu_custom_call" | custom-call | flops 201326592 | bytes 131072 | tf_op jit(solution)/shard_map/attend/pallas_call | solution.py:239
  24.7 0.6 %collective-permute-done.8.recv_ref = f32[32,1152]{1,0:T(8,128)S(1)} collective-permute-done((f32[32,1152]{1,0:T(8,128)S(1)}, f32[32,1152]{1,0:T(8,128)S(1)}, u32[]{:S(2)}, u32[]{:S(2)}) %collective-permute-start.8) | collective-permute-done | bytes 147488 | tf_op jit(solution)/shard_map/ppermute | solution.py:333
  25.3 0.3 merge.1
  25.6 1.6 %collective-permute-start.9 = (f32[32,640]{1,0:T(8,128)S(1)}, f32[32,640]{1,0:T(8,128)S(1)}, u32[]{:S(2)}, u32[]{:S(2)}) collective-permute-start(f32[32,640]{1,0:T(8,128)S(1)} %get-tuple-element.30), channel_id=1, source_target_pairs={{0,2},{1,3},{2,0},{3,1},{4,6},{5,7},{6,4},{7,5},{8,10},{9,11},{10,... | collective-permute-start | bytes 245768 | tf_op jit(solution)/shard_map/ppermute | solution.py:333
  27.2 2.4 %split.3 = (bf16[256,4096]{1,0:T(8,128)(2,1)S(1)}, bf16[256,4096]{1,0:T(8,128)(2,1)S(1)}) custom-call(f32[512,4096]{1,0:T(8,128)} %w_hbm.3), custom_call_target="tpu_custom_call" | custom-call | flops 8388608 | bytes 8388608 | tf_op jit(solution)/shard_map/split/pallas_call | solution.py:172
  29.5 2.4 %split.2 = (bf16[256,4096]{1,0:T(8,128)(2,1)S(1)}, bf16[256,4096]{1,0:T(8,128)(2,1)S(1)}) custom-call(f32[512,4096]{1,0:T(8,128)} %w_hbm.3), custom_call_target="tpu_custom_call" | custom-call | flops 8388608 | bytes 8388608 | tf_op jit(solution)/shard_map/split/pallas_call | solution.py:172
  31.9 1.6 %project.1 = (f32[16,4096]{1,0:T(8,128)S(1)}, f32[16,4096]{1,0:T(8,128)S(1)}) custom-call(f32[32,640]{1,0:T(8,128)S(1)} %get-tuple-element.29.keep_ref, f32[32,640]{1,0:T(8,128)S(1)} %collective-permute-done.9.recv_ref, bf16[256,4096]{1,0:T(8,128)(2,1)S(1)} %get-tuple-element.31.refs_0_, bf16[256,4096]{1,0:T(8,128)(2,1)S(1)} %get-tuple-element.32.refs_1_, ...), custom_call_target="tpu_custom_call" | custom-call | tf_op jit(solution)/shard_map/project/pallas_call | solution.py:316
  33.5 1.5 %collective-permute-done.10 = f32[16,4096]{1,0:T(8,128)S(1)} collective-permute-done((f32[16,4096]{1,0:T(8,128)S(1)}, f32[16,4096]{1,0:T(8,128)S(1)}, u32[]{:S(2)}, u32[]{:S(2)}) %collective-permute-start.10) | collective-permute-done | bytes 262176 | tf_op jit(solution)/shard_map/ppermute | solution.py:333
  35.1 0.6 %collective-permute-start.11 = (f32[8,4096]{1,0:T(8,128)S(1)}, f32[8,4096]{1,0:T(8,128)S(1)}, u32[]{:S(2)}, u32[]{:S(2)}) collective-permute-start(f32[8,4096]{1,0:T(8,128)S(1)} %slice_add_fusion), channel_id=1, source_target_pairs={{0,2},{1,3},{2,0},{3,1},{4,6},{5,7},{6,4},{7,5},{8,10},{9,11},{10,... | collective-permute-start | bytes 393224 | tf_op jit(solution)/shard_map/ppermute | solution.py:333
  35.6 5.0 %collective-permute-done.11 = f32[8,4096]{1,0:T(8,128)S(1)} collective-permute-done((f32[8,4096]{1,0:T(8,128)S(1)}, f32[8,4096]{1,0:T(8,128)S(1)}, u32[]{:S(2)}, u32[]{:S(2)}) %collective-permute-start.11) | collective-permute-done | bytes 131104 | tf_op jit(solution)/shard_map/ppermute | solution.py:333
  40.7 3.0 %collective-permute-start.12 = (f32[2,4096]{1,0:T(2,128)S(1)}, f32[2,4096]{1,0:T(2,128)S(1)}, u32[]{:S(2)}, u32[]{:S(2)}) collective-permute-start(f32[2,4096]{1,0:T(2,128)S(1)} %get-tuple-element.37), channel_id=1, source_target_pairs={{0,8},{1,9},{2,10},{3,11},{4,12},{5,13},{6,14},{7,15},{8,0},{9,1},... | collective-permute-start | bytes 98312 | tf_op jit(solution)/shard_map/ppermute | solution.py:333
  43.7 1.4 %collective-permute-start.14 = (f32[2,4096]{1,0:T(2,128)S(1)}, f32[2,4096]{1,0:T(2,128)S(1)}, u32[]{:S(2)}, u32[]{:S(2)}) collective-permute-start(f32[2,4096]{1,0:T(2,128)S(1)} %get-tuple-element.38), channel_id=1, source_target_pairs={{0,12},{1,13},{2,14},{3,15},{4,8},{5,9},{6,10},{7,11},{8,4},{9,5},... | collective-permute-start | bytes 98312 | tf_op jit(solution)/shard_map/ppermute | solution.py:333
  45.1 0.7 %collective-permute-done.12 = f32[2,4096]{1,0:T(2,128)S(1)} collective-permute-done((f32[2,4096]{1,0:T(2,128)S(1)}, f32[2,4096]{1,0:T(2,128)S(1)}, u32[]{:S(2)}, u32[]{:S(2)}) %collective-permute-start.12) | collective-permute-done | bytes 32800 | tf_op jit(solution)/shard_map/ppermute | solution.py:333
  45.8 3.6 %collective-permute-done.14 = f32[2,4096]{1,0:T(2,128)S(1)} collective-permute-done((f32[2,4096]{1,0:T(2,128)S(1)}, f32[2,4096]{1,0:T(2,128)S(1)}, u32[]{:S(2)}, u32[]{:S(2)}) %collective-permute-start.14) | collective-permute-done | bytes 32800 | tf_op jit(solution)/shard_map/ppermute | solution.py:333
  49.5 0.6 %fusion.2 = f32[2,4096]{1,0:T(2,128)} fusion(f32[2,4096]{1,0:T(2,128)S(1)} %collective-permute-done.14, f32[2,4096]{1,0:T(2,128)S(1)} %collective-permute-done.13, f32[2,4096]{1,0:T(2,128)S(1)} %collective-permute-done.12, f32[8,4096]{1,0:T(8,128)S(1)} %fusion), kind=kLoop, calls=%fused_computation.6 | loop fusion | flops 24576 | bytes 163840 | tf_op jit(solution)/shard_map/add | solution.py:374
  (14 shorter events, 0.2 us)
Async XLA Ops:
  0.8 6.4 %collective-permute-start = (f32[2,4096]{1,0:T(2,128)S(1)}, f32[2,4096]{1,0:T(2,128)S(1)}, u32[]{:S(2)}, u32[]{:S(2)}) collective-permute-start(f32[2,4096]{1,0:T(2,128)S(1)} %get-tuple-element.23), channel_id=1, source_target_pairs={{0,8},{1,9},{2,10},{3,11},{4,12},{5,13},{6,14},{7,15},{8,0},{9,1},... | collective-permute-start | bytes 98312 | tf_op jit(solution)/shard_map/ppermute | solution.py:333
  7.2 7.2 %collective-permute-start.1 = (f32[2,4096]{1,0:T(2,128)S(1)}, f32[2,4096]{1,0:T(2,128)S(1)}, u32[]{:S(2)}, u32[]{:S(2)}) collective-permute-start(f32[2,4096]{1,0:T(2,128)S(1)} %pad_maximum_fusion.1), channel_id=1, source_target_pairs={{0,4},{1,5},{2,6},{3,7},{4,0},{5,1},{6,2},{7,3},{8,12},{9,13},{10,... | collective-permute-start | bytes 98312 | tf_op jit(solution)/shard_map/ppermute | solution.py:333
  10.0 8.8 %collective-permute-start.5 = (f32[256,128]{1,0:T(8,128)S(1)}, f32[256,128]{1,0:T(8,128)S(1)}, u32[]{:S(2)}, u32[]{:S(2)}) collective-permute-start(f32[256,128]{1,0:T(8,128)S(1)} %get-tuple-element.26), channel_id=1, source_target_pairs={{0,4},{1,5},{2,6},{3,7},{4,0},{5,1},{6,2},{7,3},{8,12},{9,13},{10,... | collective-permute-start | bytes 393224 | tf_op jit(solution)/shard_map/ppermute | solution.py:333
  10.5 12.6 %collective-permute-start.6 = (f32[256,128]{1,0:T(8,128)S(1)}, f32[256,128]{1,0:T(8,128)S(1)}, u32[]{:S(2)}, u32[]{:S(2)}) collective-permute-start(f32[256,128]{1,0:T(8,128)S(1)} %get-tuple-element.27), channel_id=1, source_target_pairs={{0,8},{1,9},{2,10},{3,11},{4,12},{5,13},{6,14},{7,15},{8,0},{9,1},... | collective-permute-start | bytes 393224 | tf_op jit(solution)/shard_map/ppermute | solution.py:333
  13.1 10.0 %collective-permute-start.7 = (f32[256,128]{1,0:T(8,128)S(1)}, f32[256,128]{1,0:T(8,128)S(1)}, u32[]{:S(2)}, u32[]{:S(2)}) collective-permute-start(f32[256,128]{1,0:T(8,128)S(1)} %get-tuple-element.28), channel_id=1, source_target_pairs={{0,12},{1,13},{2,14},{3,15},{4,8},{5,9},{6,10},{7,11},{8,4},{9,5},... | collective-permute-start | bytes 393224 | tf_op jit(solution)/shard_map/ppermute | solution.py:333
  14.5 4.3 %collective-permute-start.2 = (f32[8,2048]{1,0:T(8,128)S(1)}, f32[8,2048]{1,0:T(8,128)S(1)}, u32[]{:S(2)}, u32[]{:S(2)}) collective-permute-start(f32[8,2048]{1,0:T(8,128)S(1)} %pad_maximum_fusion.refs_0_), channel_id=1, source_target_pairs={{0,2},{1,3},{2,0},{3,1},{4,6},{5,7},{6,4},{7,5},{8,10},{9,11},{10,... | collective-permute-start | bytes 196616 | tf_op jit(solution)/shard_map/ppermute | solution.py:333
  16.1 2.8 %collective-permute-start.3 = (f32[8,2048]{1,0:T(8,128)S(1)}, f32[8,2048]{1,0:T(8,128)S(1)}, u32[]{:S(2)}, u32[]{:S(2)}) collective-permute-start(f32[8,2048]{1,0:T(8,128)S(1)} %pad_maximum_fusion.refs_0_), channel_id=1, source_target_pairs={{0,1},{1,0},{2,3},{3,2},{4,5},{5,4},{6,7},{7,6},{8,9},{9,8},{10,11... | collective-permute-start | bytes 196616 | tf_op jit(solution)/shard_map/ppermute | solution.py:333
  18.8 4.3 %collective-permute-start.4 = (f32[8,2048]{1,0:T(8,128)S(1)}, f32[8,2048]{1,0:T(8,128)S(1)}, u32[]{:S(2)}, u32[]{:S(2)}) collective-permute-start(f32[8,2048]{1,0:T(8,128)S(1)} %collective-permute-done.2.refs_1_), channel_id=1, source_target_pairs={{0,1},{1,0},{2,3},{3,2},{4,5},{5,4},{6,7},{7,6},{8,9},{9,8},{10,11... | collective-permute-start | bytes 196616 | tf_op jit(solution)/shard_map/ppermute | solution.py:333
  23.9 1.4 %collective-permute-start.8 = (f32[32,1152]{1,0:T(8,128)S(1)}, f32[32,1152]{1,0:T(8,128)S(1)}, u32[]{:S(2)}, u32[]{:S(2)}) collective-permute-start(f32[32,1152]{1,0:T(8,128)S(1)} %attend.3), channel_id=1, source_target_pairs={{0,1},{1,0},{2,3},{3,2},{4,5},{5,4},{6,7},{7,6},{8,9},{9,8},{10,11... | collective-permute-start | bytes 442376 | tf_op jit(solution)/shard_map/ppermute | solution.py:333
  25.6 6.3 %collective-permute-start.9 = (f32[32,640]{1,0:T(8,128)S(1)}, f32[32,640]{1,0:T(8,128)S(1)}, u32[]{:S(2)}, u32[]{:S(2)}) collective-permute-start(f32[32,640]{1,0:T(8,128)S(1)} %get-tuple-element.30), channel_id=1, source_target_pairs={{0,2},{1,3},{2,0},{3,1},{4,6},{5,7},{6,4},{7,5},{8,10},{9,11},{10,... | collective-permute-start | bytes 245768 | tf_op jit(solution)/shard_map/ppermute | solution.py:333
  33.5 1.6 %collective-permute-start.10 = (f32[16,4096]{1,0:T(8,128)S(1)}, f32[16,4096]{1,0:T(8,128)S(1)}, u32[]{:S(2)}, u32[]{:S(2)}) collective-permute-start(f32[16,4096]{1,0:T(8,128)S(1)} %get-tuple-element.36), channel_id=1, source_target_pairs={{0,1},{1,0},{2,3},{3,2},{4,5},{5,4},{6,7},{7,6},{8,9},{9,8},{10,11... | collective-permute-start | bytes 786440 | tf_op jit(solution)/shard_map/ppermute | solution.py:333
  35.1 5.6 %collective-permute-start.11 = (f32[8,4096]{1,0:T(8,128)S(1)}, f32[8,4096]{1,0:T(8,128)S(1)}, u32[]{:S(2)}, u32[]{:S(2)}) collective-permute-start(f32[8,4096]{1,0:T(8,128)S(1)} %slice_add_fusion), channel_id=1, source_target_pairs={{0,2},{1,3},{2,0},{3,1},{4,6},{5,7},{6,4},{7,5},{8,10},{9,11},{10,... | collective-permute-start | bytes 393224 | tf_op jit(solution)/shard_map/ppermute | solution.py:333
  40.7 5.1 %collective-permute-start.12 = (f32[2,4096]{1,0:T(2,128)S(1)}, f32[2,4096]{1,0:T(2,128)S(1)}, u32[]{:S(2)}, u32[]{:S(2)}) collective-permute-start(f32[2,4096]{1,0:T(2,128)S(1)} %get-tuple-element.37), channel_id=1, source_target_pairs={{0,8},{1,9},{2,10},{3,11},{4,12},{5,13},{6,14},{7,15},{8,0},{9,1},... | collective-permute-start | bytes 98312 | tf_op jit(solution)/shard_map/ppermute | solution.py:333
  43.7 5.7 %collective-permute-start.14 = (f32[2,4096]{1,0:T(2,128)S(1)}, f32[2,4096]{1,0:T(2,128)S(1)}, u32[]{:S(2)}, u32[]{:S(2)}) collective-permute-start(f32[2,4096]{1,0:T(2,128)S(1)} %get-tuple-element.38), channel_id=1, source_target_pairs={{0,12},{1,13},{2,14},{3,15},{4,8},{5,9},{6,10},{7,11},{8,4},{9,5},... | collective-permute-start | bytes 98312 | tf_op jit(solution)/shard_map/ppermute | solution.py:333
  45.1 4.3 %collective-permute-start.13 = (f32[2,4096]{1,0:T(2,128)S(1)}, f32[2,4096]{1,0:T(2,128)S(1)}, u32[]{:S(2)}, u32[]{:S(2)}) collective-permute-start(f32[2,4096]{1,0:T(2,128)S(1)} %get-tuple-element.39), channel_id=1, source_target_pairs={{0,4},{1,5},{2,6},{3,7},{4,0},{5,1},{6,2},{7,3},{8,12},{9,13},{10,... | collective-permute-start | bytes 98312 | tf_op jit(solution)/shard_map/ppermute | solution.py:333

commit v4 on v3

--- a/solution.py
+++ b/solution.py
@@ -362,16 +362,12 @@
     send, keep = project(part, keep, swap(send, 1 << (bits - 1)), pieces)
 
     recv = swap(send, 1)
-    for b in range(1, bits):
-        half = keep.shape[0] // 2
-        send = keep[half:] + recv[half:]
-        keep = keep[:half] + recv[:half]
-        recv = swap(send, 1 << b)
-    total = keep + recv
-    out = total[:local_rows]
-    for order in range(1, KVH):
-        k = relative(order, 0)
-        out = out + swap(total[order * local_rows : (order + 1) * local_rows], k * sub)
+    quarter = keep.shape[0] // 4
+    rows = [slice(i * quarter, (i + 1) * quarter) for i in range(4)]
+    total = keep[rows[0]] + recv[rows[0]]
+    for i, mask in ((1, sub), (2, 2), (3, 2 + sub)):
+        total = total + swap(keep[rows[i]] + recv[rows[i]], mask)
+    out = total[:local_rows] + swap(total[local_rows:], 2 * sub)
     return out
 
 

time: 50.4 us -> 48.4 us (0.960)
  waiting for transfers between devices: 20.8 us -> 17.9 us
  starting transfers between devices: 18.4 us -> 19.4 us
    ppermute x15, waiting for transfers between devices: 20.8 us -> 17.9 us  [swap(): return lax.ppermute(x, 'blk', [(i, i ^ mask) for i in range(blocks)])]
    ppermute x15, starting transfers between devices: 18.4 us -> 19.4 us  [swap(): return lax.ppermute(x, 'blk', [(i, i ^ mask) for i in range(blocks)])]
  transfers between devices with their start and end apart: 15 -> 15, of which waited for: 8 -> 9; matrix products, arithmetic and copies ran while one was open for 0% -> 0% of each run, Pallas kernels for 13% -> 14%
where the time goes in v4:
time: 48.4 us; the launch traced here: 48.2 us
  starting transfers between devices  19.4 us (40%)
  waiting for transfers between devices  17.9 us (37%)
  Pallas kernels  9.96 us (21%)
  other arithmetic  0.79 us (2%)
    ppermute x15, starting transfers between devices, swap(): return lax.ppermute(x, 'blk', [(i, i ^ mask) for i in range(blocks)])  19.4 us
    ppermute x15, waiting for transfers between devices, swap(): return lax.ppermute(x, 'blk', [(i, i ^ mask) for i in range(blocks)])  17.9 us
    pallas_call x2, Pallas kernels, split_weight(): pl.pallas_call(functools.partial(split_kernel, first, tile), out_shape=[o...  4.71 us
    pallas_call x1, Pallas kernels, project(): pl.pallas_call(functools.partial(project_kernel, swap, min(width, 512)),...  1.56 us
    pallas_call x2, Pallas kernels, attend(): pl.pallas_call(functools.partial(attend_kernel, bits, key_count, start),...  1.49 us
    pallas_call x1, Pallas kernels, pack_kv(): pl.pallas_call(functools.partial(pack_kv_kernel, bits), out_shape=[kv] *...  1.13 us
  transfers between devices with their start and end apart: 15, of which 9 were waited for; matrix products, arithmetic and copies ran while one was open for 0% of the time, Pallas kernels for 14%

profile of v4, /device:TPU:0, one launch (start us, length us, event | category | flops | bytes accessed | tf_op | source)
XLA Modules:
  0.0 48.2 jit_solution(2714197623175428638)
XLA Ops:
  0.0 0.8 %pack_q.1 = (f32[2,4096]{1,0:T(2,128)S(1)}, f32[2,2048]{1,0:T(2,128)S(1)}, f32[2,2048]{1,0:T(2,128)S(1)}, s32[32,128]{1,0:T(8,128)S(1)}) custom-call(s32[2]{0:T(128)} %len_hbm.1, f32[2,8192]{1,0:T(2,128)} %q_hbm.1), custom_call_target="tpu_custom_call" | custom-call | tf_op jit(solution)/shard_map/pack_q/pallas_call | solution.py:115
  0.8 4.1 %collective-permute-start = (f32[2,4096]{1,0:T(2,128)S(1)}, f32[2,4096]{1,0:T(2,128)S(1)}, u32[]{:S(2)}, u32[]{:S(2)}) collective-permute-start(f32[2,4096]{1,0:T(2,128)S(1)} %get-tuple-element.23), channel_id=1, source_target_pairs={{0,8},{1,9},{2,10},{3,11},{4,12},{5,13},{6,14},{7,15},{8,0},{9,1},... | collective-permute-start | bytes 98312 | tf_op jit(solution)/shard_map/ppermute | solution.py:333
  5.0 2.2 %collective-permute-done = f32[2,4096]{1,0:T(2,128)S(1)} collective-permute-done((f32[2,4096]{1,0:T(2,128)S(1)}, f32[2,4096]{1,0:T(2,128)S(1)}, u32[]{:S(2)}, u32[]{:S(2)}) %collective-permute-start) | collective-permute-done | bytes 32800 | tf_op jit(solution)/shard_map/ppermute | solution.py:333
  7.2 1.6 %collective-permute-start.1 = (f32[2,4096]{1,0:T(2,128)S(1)}, f32[2,4096]{1,0:T(2,128)S(1)}, u32[]{:S(2)}, u32[]{:S(2)}) collective-permute-start(f32[2,4096]{1,0:T(2,128)S(1)} %pad_maximum_fusion.1), channel_id=1, source_target_pairs={{0,4},{1,5},{2,6},{3,7},{4,0},{5,1},{6,2},{7,3},{8,12},{9,13},{10,... | collective-permute-start | bytes 98312 | tf_op jit(solution)/shard_map/ppermute | solution.py:333
  8.9 1.1 %pack_kv.1 = (f32[256,128]{1,0:T(8,128)S(1)}, f32[256,128]{1,0:T(8,128)S(1)}, f32[256,128]{1,0:T(8,128)S(1)}, f32[256,128]{1,0:T(8,128)S(1)}) custom-call(f32[128,512]{1,0:T(8,128)} %k_hbm.1, f32[128,512]{1,0:T(8,128)} %v_hbm.1), custom_call_target="tpu_custom_call" | custom-call | bytes 1048576 | tf_op jit(solution)/shard_map/pack_kv/pallas_call | solution.py:142
  10.0 0.5 %collective-permute-start.5 = (f32[256,128]{1,0:T(8,128)S(1)}, f32[256,128]{1,0:T(8,128)S(1)}, u32[]{:S(2)}, u32[]{:S(2)}) collective-permute-start(f32[256,128]{1,0:T(8,128)S(1)} %get-tuple-element.26), channel_id=1, source_target_pairs={{0,4},{1,5},{2,6},{3,7},{4,0},{5,1},{6,2},{7,3},{8,12},{9,13},{10,... | collective-permute-start | bytes 393224 | tf_op jit(solution)/shard_map/ppermute | solution.py:333
  10.5 2.6 %collective-permute-start.6 = (f32[256,128]{1,0:T(8,128)S(1)}, f32[256,128]{1,0:T(8,128)S(1)}, u32[]{:S(2)}, u32[]{:S(2)}) collective-permute-start(f32[256,128]{1,0:T(8,128)S(1)} %get-tuple-element.27), channel_id=1, source_target_pairs={{0,8},{1,9},{2,10},{3,11},{4,12},{5,13},{6,14},{7,15},{8,0},{9,1},... | collective-permute-start | bytes 393224 | tf_op jit(solution)/shard_map/ppermute | solution.py:333
  13.1 1.3 %collective-permute-start.7 = (f32[256,128]{1,0:T(8,128)S(1)}, f32[256,128]{1,0:T(8,128)S(1)}, u32[]{:S(2)}, u32[]{:S(2)}) collective-permute-start(f32[256,128]{1,0:T(8,128)S(1)} %get-tuple-element.28), channel_id=1, source_target_pairs={{0,12},{1,13},{2,14},{3,15},{4,8},{5,9},{6,10},{7,11},{8,4},{9,5},... | collective-permute-start | bytes 393224 | tf_op jit(solution)/shard_map/ppermute | solution.py:333
  14.5 1.6 %collective-permute-start.2 = (f32[8,2048]{1,0:T(8,128)S(1)}, f32[8,2048]{1,0:T(8,128)S(1)}, u32[]{:S(2)}, u32[]{:S(2)}) collective-permute-start(f32[8,2048]{1,0:T(8,128)S(1)} %pad_maximum_fusion.refs_0_), channel_id=1, source_target_pairs={{0,2},{1,3},{2,0},{3,1},{4,6},{5,7},{6,4},{7,5},{8,10},{9,11},{10,... | collective-permute-start | bytes 196616 | tf_op jit(solution)/shard_map/ppermute | solution.py:333
  16.1 0.0 collective-permute-start.3
  16.1 2.7 %collective-permute-done.2.refs_1_ = f32[8,2048]{1,0:T(8,128)S(1)} collective-permute-done((f32[8,2048]{1,0:T(8,128)S(1)}, f32[8,2048]{1,0:T(8,128)S(1)}, u32[]{:S(2)}, u32[]{:S(2)}) %collective-permute-start.2) | collective-permute-done | bytes 65568 | tf_op jit(solution)/shard_map/ppermute | solution.py:333
  18.8 4.3 %collective-permute-done.6.refs_6_ = f32[256,128]{1,0:T(8,128)S(1)} collective-permute-done((f32[256,128]{1,0:T(8,128)S(1)}, f32[256,128]{1,0:T(8,128)S(1)}, u32[]{:S(2)}, u32[]{:S(2)}) %collective-permute-start.6) | collective-permute-done | bytes 131104 | tf_op jit(solution)/shard_map/ppermute | solution.py:333
  23.2 0.7 %attend.3 = f32[32,1152]{1,0:T(8,128)S(1)} custom-call(s32[32,128]{1,0:T(8,128)S(1)} %get-tuple-element.21.limit_ref, f32[8,2048]{1,0:T(8,128)S(1)} %pad_maximum_fusion.refs_0_, f32[8,2048]{1,0:T(8,128)S(1)} %collective-permute-done.2.refs_1_, f32[8,2048]{1,0:T(8,128)S(1)} %collective-permute-done.3.refs_2_, f32[8,2048]{1,0:T(8,128)S(1)} %collective-permute-done.4.refs_3_, ...), custom_call_target="tpu_custom_call" | custom-call | flops 201326592 | bytes 131072 | tf_op jit(solution)/shard_map/attend/pallas_call | solution.py:239
  23.9 0.1 collective-permute-start.8
  24.0 0.7 %attend.2.keep_ref = f32[32,1152]{1,0:T(8,128)S(1)} custom-call(s32[32,128]{1,0:T(8,128)S(1)} %get-tuple-element.21.limit_ref, f32[8,2048]{1,0:T(8,128)S(1)} %pad_maximum_fusion.refs_0_, f32[8,2048]{1,0:T(8,128)S(1)} %collective-permute-done.2.refs_1_, f32[8,2048]{1,0:T(8,128)S(1)} %collective-permute-done.3.refs_2_, ...), custom_call_target="tpu_custom_call" | custom-call | flops 201326592 | bytes 131072 | tf_op jit(solution)/shard_map/attend/pallas_call | solution.py:239
  24.7 0.6 %collective-permute-done.8.recv_ref = f32[32,1152]{1,0:T(8,128)S(1)} collective-permute-done((f32[32,1152]{1,0:T(8,128)S(1)}, f32[32,1152]{1,0:T(8,128)S(1)}, u32[]{:S(2)}, u32[]{:S(2)}) %collective-permute-start.8) | collective-permute-done | bytes 147488 | tf_op jit(solution)/shard_map/ppermute | solution.py:333
  25.3 0.3 merge.1
  25.6 1.6 %collective-permute-start.9 = (f32[32,640]{1,0:T(8,128)S(1)}, f32[32,640]{1,0:T(8,128)S(1)}, u32[]{:S(2)}, u32[]{:S(2)}) collective-permute-start(f32[32,640]{1,0:T(8,128)S(1)} %get-tuple-element.30), channel_id=1, source_target_pairs={{0,2},{1,3},{2,0},{3,1},{4,6},{5,7},{6,4},{7,5},{8,10},{9,11},{10,... | collective-permute-start | bytes 245768 | tf_op jit(solution)/shard_map/ppermute | solution.py:333
  27.2 2.4 %split.3 = (bf16[256,4096]{1,0:T(8,128)(2,1)S(1)}, bf16[256,4096]{1,0:T(8,128)(2,1)S(1)}) custom-call(f32[512,4096]{1,0:T(8,128)} %w_hbm.3), custom_call_target="tpu_custom_call" | custom-call | flops 8388608 | bytes 8388608 | tf_op jit(solution)/shard_map/split/pallas_call | solution.py:172
  29.5 2.4 %split.2 = (bf16[256,4096]{1,0:T(8,128)(2,1)S(1)}, bf16[256,4096]{1,0:T(8,128)(2,1)S(1)}) custom-call(f32[512,4096]{1,0:T(8,128)} %w_hbm.3), custom_call_target="tpu_custom_call" | custom-call | flops 8388608 | bytes 8388608 | tf_op jit(solution)/shard_map/split/pallas_call | solution.py:172
  31.9 1.6 %project.1 = (f32[16,4096]{1,0:T(8,128)S(1)}, f32[16,4096]{1,0:T(8,128)S(1)}) custom-call(f32[32,640]{1,0:T(8,128)S(1)} %get-tuple-element.29.keep_ref, f32[32,640]{1,0:T(8,128)S(1)} %collective-permute-done.9.recv_ref, bf16[256,4096]{1,0:T(8,128)(2,1)S(1)} %get-tuple-element.31.refs_0_, bf16[256,4096]{1,0:T(8,128)(2,1)S(1)} %get-tuple-element.32.refs_1_, ...), custom_call_target="tpu_custom_call" | custom-call | tf_op jit(solution)/shard_map/project/pallas_call | solution.py:316
  33.5 1.5 %collective-permute-done.10 = f32[16,4096]{1,0:T(8,128)S(1)} collective-permute-done((f32[16,4096]{1,0:T(8,128)S(1)}, f32[16,4096]{1,0:T(8,128)S(1)}, u32[]{:S(2)}, u32[]{:S(2)}) %collective-permute-start.10) | collective-permute-done | bytes 262176 | tf_op jit(solution)/shard_map/ppermute | solution.py:333
  35.0 0.1 slice_add_fusion.2
  35.1 2.0 %collective-permute-start.11 = (f32[4,4096]{1,0:T(4,128)S(1)}, f32[4,4096]{1,0:T(4,128)S(1)}, u32[]{:S(2)}, u32[]{:S(2)}) collective-permute-start(f32[4,4096]{1,0:T(4,128)S(1)} %get-tuple-element.37), channel_id=1, source_target_pairs={{0,4},{1,5},{2,6},{3,7},{4,0},{5,1},{6,2},{7,3},{8,12},{9,13},{10,... | collective-permute-start | bytes 196616 | tf_op jit(solution)/shard_map/ppermute | solution.py:333
  37.1 0.0 collective-permute-start.13
  37.2 1.5 %collective-permute-start.12 = (f32[4,4096]{1,0:T(4,128)S(1)}, f32[4,4096]{1,0:T(4,128)S(1)}, u32[]{:S(2)}, u32[]{:S(2)}) collective-permute-start(f32[4,4096]{1,0:T(4,128)S(1)} %get-tuple-element.39), channel_id=1, source_target_pairs={{0,2},{1,3},{2,0},{3,1},{4,6},{5,7},{6,4},{7,5},{8,10},{9,11},{10,... | collective-permute-start | bytes 196616 | tf_op jit(solution)/shard_map/ppermute | solution.py:333
  38.7 0.9 %collective-permute-done.11 = f32[4,4096]{1,0:T(4,128)S(1)} collective-permute-done((f32[4,4096]{1,0:T(4,128)S(1)}, f32[4,4096]{1,0:T(4,128)S(1)}, u32[]{:S(2)}, u32[]{:S(2)}) %collective-permute-start.11) | collective-permute-done | bytes 65568 | tf_op jit(solution)/shard_map/ppermute | solution.py:333
  39.5 2.8 %collective-permute-done.13 = f32[4,4096]{1,0:T(4,128)S(1)} collective-permute-done((f32[4,4096]{1,0:T(4,128)S(1)}, f32[4,4096]{1,0:T(4,128)S(1)}, u32[]{:S(2)}, u32[]{:S(2)}) %collective-permute-start.13) | collective-permute-done | bytes 65568 | tf_op jit(solution)/shard_map/ppermute | solution.py:333
  42.3 0.3 collective-permute-done.12
  42.7 2.3 %collective-permute-start.14 = (f32[2,4096]{1,0:T(2,128)S(1)}, f32[2,4096]{1,0:T(2,128)S(1)}, u32[]{:S(2)}, u32[]{:S(2)}) collective-permute-start(f32[2,4096]{1,0:T(2,128)S(1)} %slice.65), channel_id=1, source_target_pairs={{0,8},{1,9},{2,10},{3,11},{4,12},{5,13},{6,14},{7,15},{8,0},{9,1},... | collective-permute-start | bytes 98312 | tf_op jit(solution)/shard_map/ppermute | solution.py:333
  45.0 2.5 %collective-permute-done.14 = f32[2,4096]{1,0:T(2,128)S(1)} collective-permute-done((f32[2,4096]{1,0:T(2,128)S(1)}, f32[2,4096]{1,0:T(2,128)S(1)}, u32[]{:S(2)}, u32[]{:S(2)}) %collective-permute-start.14) | collective-permute-done | bytes 32800 | tf_op jit(solution)/shard_map/ppermute | solution.py:333
  47.5 0.6 %slice_add_fusion.4 = f32[2,4096]{1,0:T(2,128)} fusion(f32[2,4096]{1,0:T(2,128)S(1)} %collective-permute-done.14, f32[4,4096]{1,0:T(4,128)S(1)} %fusion.2), kind=kLoop, calls=%fused_computation.8 | loop fusion | flops 8192 | bytes 98304 | tf_op jit(solution)/shard_map/add | solution.py:370
  (14 shorter events, 0.1 us)
Async XLA Ops:
  0.8 6.4 %collective-permute-start = (f32[2,4096]{1,0:T(2,128)S(1)}, f32[2,4096]{1,0:T(2,128)S(1)}, u32[]{:S(2)}, u32[]{:S(2)}) collective-permute-start(f32[2,4096]{1,0:T(2,128)S(1)} %get-tuple-element.23), channel_id=1, source_target_pairs={{0,8},{1,9},{2,10},{3,11},{4,12},{5,13},{6,14},{7,15},{8,0},{9,1},... | collective-permute-start | bytes 98312 | tf_op jit(solution)/shard_map/ppermute | solution.py:333
  7.2 7.2 %collective-permute-start.1 = (f32[2,4096]{1,0:T(2,128)S(1)}, f32[2,4096]{1,0:T(2,128)S(1)}, u32[]{:S(2)}, u32[]{:S(2)}) collective-permute-start(f32[2,4096]{1,0:T(2,128)S(1)} %pad_maximum_fusion.1), channel_id=1, source_target_pairs={{0,4},{1,5},{2,6},{3,7},{4,0},{5,1},{6,2},{7,3},{8,12},{9,13},{10,... | collective-permute-start | bytes 98312 | tf_op jit(solution)/shard_map/ppermute | solution.py:333
  10.0 8.8 %collective-permute-start.5 = (f32[256,128]{1,0:T(8,128)S(1)}, f32[256,128]{1,0:T(8,128)S(1)}, u32[]{:S(2)}, u32[]{:S(2)}) collective-permute-start(f32[256,128]{1,0:T(8,128)S(1)} %get-tuple-element.26), channel_id=1, source_target_pairs={{0,4},{1,5},{2,6},{3,7},{4,0},{5,1},{6,2},{7,3},{8,12},{9,13},{10,... | collective-permute-start | bytes 393224 | tf_op jit(solution)/shard_map/ppermute | solution.py:333
  10.5 12.6 %collective-permute-start.6 = (f32[256,128]{1,0:T(8,128)S(1)}, f32[256,128]{1,0:T(8,128)S(1)}, u32[]{:S(2)}, u32[]{:S(2)}) collective-permute-start(f32[256,128]{1,0:T(8,128)S(1)} %get-tuple-element.27), channel_id=1, source_target_pairs={{0,8},{1,9},{2,10},{3,11},{4,12},{5,13},{6,14},{7,15},{8,0},{9,1},... | collective-permute-start | bytes 393224 | tf_op jit(solution)/shard_map/ppermute | solution.py:333
  13.1 10.0 %collective-permute-start.7 = (f32[256,128]{1,0:T(8,128)S(1)}, f32[256,128]{1,0:T(8,128)S(1)}, u32[]{:S(2)}, u32[]{:S(2)}) collective-permute-start(f32[256,128]{1,0:T(8,128)S(1)} %get-tuple-element.28), channel_id=1, source_target_pairs={{0,12},{1,13},{2,14},{3,15},{4,8},{5,9},{6,10},{7,11},{8,4},{9,5},... | collective-permute-start | bytes 393224 | tf_op jit(solution)/shard_map/ppermute | solution.py:333
  14.5 4.3 %collective-permute-start.2 = (f32[8,2048]{1,0:T(8,128)S(1)}, f32[8,2048]{1,0:T(8,128)S(1)}, u32[]{:S(2)}, u32[]{:S(2)}) collective-permute-start(f32[8,2048]{1,0:T(8,128)S(1)} %pad_maximum_fusion.refs_0_), channel_id=1, source_target_pairs={{0,2},{1,3},{2,0},{3,1},{4,6},{5,7},{6,4},{7,5},{8,10},{9,11},{10,... | collective-permute-start | bytes 196616 | tf_op jit(solution)/shard_map/ppermute | solution.py:333
  16.1 2.8 %collective-permute-start.3 = (f32[8,2048]{1,0:T(8,128)S(1)}, f32[8,2048]{1,0:T(8,128)S(1)}, u32[]{:S(2)}, u32[]{:S(2)}) collective-permute-start(f32[8,2048]{1,0:T(8,128)S(1)} %pad_maximum_fusion.refs_0_), channel_id=1, source_target_pairs={{0,1},{1,0},{2,3},{3,2},{4,5},{5,4},{6,7},{7,6},{8,9},{9,8},{10,11... | collective-permute-start | bytes 196616 | tf_op jit(solution)/shard_map/ppermute | solution.py:333
  18.8 4.3 %collective-permute-start.4 = (f32[8,2048]{1,0:T(8,128)S(1)}, f32[8,2048]{1,0:T(8,128)S(1)}, u32[]{:S(2)}, u32[]{:S(2)}) collective-permute-start(f32[8,2048]{1,0:T(8,128)S(1)} %collective-permute-done.2.refs_1_), channel_id=1, source_target_pairs={{0,1},{1,0},{2,3},{3,2},{4,5},{5,4},{6,7},{7,6},{8,9},{9,8},{10,11... | collective-permute-start | bytes 196616 | tf_op jit(solution)/shard_map/ppermute | solution.py:333
  23.9 1.4 %collective-permute-start.8 = (f32[32,1152]{1,0:T(8,128)S(1)}, f32[32,1152]{1,0:T(8,128)S(1)}, u32[]{:S(2)}, u32[]{:S(2)}) collective-permute-start(f32[32,1152]{1,0:T(8,128)S(1)} %attend.3), channel_id=1, source_target_pairs={{0,1},{1,0},{2,3},{3,2},{4,5},{5,4},{6,7},{7,6},{8,9},{9,8},{10,11... | collective-permute-start | bytes 442376 | tf_op jit(solution)/shard_map/ppermute | solution.py:333
  25.6 6.3 %collective-permute-start.9 = (f32[32,640]{1,0:T(8,128)S(1)}, f32[32,640]{1,0:T(8,128)S(1)}, u32[]{:S(2)}, u32[]{:S(2)}) collective-permute-start(f32[32,640]{1,0:T(8,128)S(1)} %get-tuple-element.30), channel_id=1, source_target_pairs={{0,2},{1,3},{2,0},{3,1},{4,6},{5,7},{6,4},{7,5},{8,10},{9,11},{10,... | collective-permute-start | bytes 245768 | tf_op jit(solution)/shard_map/ppermute | solution.py:333
  33.5 1.6 %collective-permute-start.10 = (f32[16,4096]{1,0:T(8,128)S(1)}, f32[16,4096]{1,0:T(8,128)S(1)}, u32[]{:S(2)}, u32[]{:S(2)}) collective-permute-start(f32[16,4096]{1,0:T(8,128)S(1)} %get-tuple-element.36), channel_id=1, source_target_pairs={{0,1},{1,0},{2,3},{3,2},{4,5},{5,4},{6,7},{7,6},{8,9},{9,8},{10,11... | collective-permute-start | bytes 786440 | tf_op jit(solution)/shard_map/ppermute | solution.py:333
  35.1 4.4 %collective-permute-start.11 = (f32[4,4096]{1,0:T(4,128)S(1)}, f32[4,4096]{1,0:T(4,128)S(1)}, u32[]{:S(2)}, u32[]{:S(2)}) collective-permute-start(f32[4,4096]{1,0:T(4,128)S(1)} %get-tuple-element.37), channel_id=1, source_target_pairs={{0,4},{1,5},{2,6},{3,7},{4,0},{5,1},{6,2},{7,3},{8,12},{9,13},{10,... | collective-permute-start | bytes 196616 | tf_op jit(solution)/shard_map/ppermute | solution.py:333
  37.1 5.2 %collective-permute-start.13 = (f32[4,4096]{1,0:T(4,128)S(1)}, f32[4,4096]{1,0:T(4,128)S(1)}, u32[]{:S(2)}, u32[]{:S(2)}) collective-permute-start(f32[4,4096]{1,0:T(4,128)S(1)} %get-tuple-element.38), channel_id=1, source_target_pairs={{0,6},{1,7},{2,4},{3,5},{4,2},{5,3},{6,0},{7,1},{8,14},{9,15},{10,... | collective-permute-start | bytes 196616 | tf_op jit(solution)/shard_map/ppermute | solution.py:333
  37.2 5.4 %collective-permute-start.12 = (f32[4,4096]{1,0:T(4,128)S(1)}, f32[4,4096]{1,0:T(4,128)S(1)}, u32[]{:S(2)}, u32[]{:S(2)}) collective-permute-start(f32[4,4096]{1,0:T(4,128)S(1)} %get-tuple-element.39), channel_id=1, source_target_pairs={{0,2},{1,3},{2,0},{3,1},{4,6},{5,7},{6,4},{7,5},{8,10},{9,11},{10,... | collective-permute-start | bytes 196616 | tf_op jit(solution)/shard_map/ppermute | solution.py:333
  42.7 4.9 %collective-permute-start.14 = (f32[2,4096]{1,0:T(2,128)S(1)}, f32[2,4096]{1,0:T(2,128)S(1)}, u32[]{:S(2)}, u32[]{:S(2)}) collective-permute-start(f32[2,4096]{1,0:T(2,128)S(1)} %slice.65), channel_id=1, source_target_pairs={{0,8},{1,9},{2,10},{3,11},{4,12},{5,13},{6,14},{7,15},{8,0},{9,1},... | collective-permute-start | bytes 98312 | tf_op jit(solution)/shard_map/ppermute | solution.py:333

commit v5 on v4

--- a/solution.py
+++ b/solution.py
@@ -22,13 +22,6 @@
 
 
 VMEM = pltpu.VMEM
-
-
-def reverse_bits(value, bits):
-    out = 0
-    for b in range(bits):
-        out |= ((value >> b) & 1) << (bits - 1 - b)
-    return out
 
 
 def relative(order, bits):
@@ -186,9 +179,10 @@
     )(in_hbm(weight))
 
 
-def attend_kernel(bits, key_count, start, limit_ref, *refs):
+def attend_kernel(bits, key_count, rels, limit_ref, *refs):
     sub = 1 << bits
-    q_refs, kv_refs, ref = refs[: -KVH - 1], refs[-KVH - 1 : -1], refs[-1]
+    inputs, outs = refs[: -len(rels)], refs[-len(rels) :]
+    q_refs, kv_refs = inputs[:-KVH], inputs[-KVH:]
     position = lax.axis_index("blk")
     plane, place = position // sub, position % sub
     rows = limit_ref.shape[0]
@@ -208,39 +202,41 @@
     both = (((1,), (1,)), ((), ()))
     scale = 1.0 / math.sqrt(HD)
 
-    half = GROUP // 2
-    cross = jnp.broadcast_to(visible[None], (half, rows, held))
+    count = len(rels) * per_owner
+    cross = jnp.broadcast_to(visible[None], (count, rows, held))
     heads = []
-    for head in range(start, start + half):
-        owner = place ^ reverse_bits(head // per_owner, bits)
-        lanes = pl.ds(pl.multiple_of((owner * per_owner + head % per_owner) * HD, HD), HD)
-        heads += [q_ref[:, lanes] for q_ref in q_refs]
+    for rel in rels:
+        for i in range(per_owner):
+            lanes = pl.ds(pl.multiple_of(((place ^ rel) * per_owner + i) * HD, HD), HD)
+            heads += [q_ref[:, lanes] for q_ref in q_refs]
     q1, q2, q3 = pieces_of(jnp.concatenate(heads, axis=0), 3)
     q11, q22 = jnp.concatenate([q1, q1], axis=1), jnp.concatenate([q2, q2], axis=1)
     q13 = jnp.concatenate([q1, q3], axis=1)
     scores = times(q11, k12, both) + (times(q22, k12, both) + times(q13, k31, both))
-    scores = scores.reshape(half, rows, held) * scale
+    scores = scores.reshape(count, rows, held) * scale
     masked = jnp.where(cross, scores, NEG_FILL)
     peak = jnp.max(masked, axis=2, keepdims=True)
     weights = jnp.where(cross, jnp.exp(masked - peak), 0.0)
     total = jnp.sum(weights, axis=2, keepdims=True)
-    w1, w2 = pieces_of(weights.reshape(half * rows, held), 2)
+    w1, w2 = pieces_of(weights.reshape(count * rows, held), 2)
     wide = times(w1, v12)
     sums = wide[:, :HD] + (wide[:, HD:] + times(w2, v1))
-    for i in range(half):
-        ref[:, i * HD : (i + 1) * HD] = sums[i * rows : (i + 1) * rows]
-    stats = [peak[i] for i in range(half)] + [total[i] for i in range(half)]
-    ref[:, half * HD :] = lanes_of(stats, rows)
-
-
-def attend(bits, start, limits, q_parts, kv_held):
-    rows, width, key_count = limits.shape[0], GROUP // 2 * HD, kv_held[0].shape[0] // 2
-    pairs = rows * GROUP // 2 * key_count * KVH
+    for n, ref in enumerate(outs):
+        own = range(n * per_owner, (n + 1) * per_owner)
+        for i, head in enumerate(own):
+            ref[:, i * HD : (i + 1) * HD] = sums[head * rows : (head + 1) * rows]
+        ref[:, per_owner * HD :] = lanes_of([peak[h] for h in own] + [total[h] for h in own], rows)
+
+
+def attend(bits, rels, limits, q_parts, kv_held):
+    rows, key_count = limits.shape[0], kv_held[0].shape[0] // 2
+    width = (GROUP >> bits) * HD
+    pairs = rows * (GROUP >> bits) * len(rels) * key_count * KVH
     return pl.pallas_call(
-        functools.partial(attend_kernel, bits, key_count, start),
-        out_shape=jax.ShapeDtypeStruct((rows, width + LANES), jnp.float32),
+        functools.partial(attend_kernel, bits, key_count, rels),
+        out_shape=[jax.ShapeDtypeStruct((rows, width + LANES), jnp.float32)] * len(rels),
         in_specs=[IN_VMEM] * (1 + len(q_parts) + KVH),
-        out_specs=IN_VMEM,
+        out_specs=[IN_VMEM] * len(rels),
         compiler_params=limit(16),
         cost_estimate=pl.CostEstimate(
             flops=12 * pairs * HD, bytes_accessed=4 * rows * width, transcendentals=pairs
@@ -249,50 +245,29 @@
     )(limits, *q_parts, *kv_held)
 
 
-def merged(keep_ref, recv_ref, swap):
-    heads = (keep_ref.shape[1] - LANES) // HD
-    mine, other = keep_ref[:, heads * HD :], swap_rows(recv_ref[:, heads * HD :], swap)
-    sums, peaks, totals = [], [], []
+def merged(parts):
+    heads = (parts[0][0].shape[1] - LANES) // HD
+
+    def read(ref, sizes, cols):
+        return functools.reduce(swap_rows, sizes, ref[:, cols])
+
+    stats = [read(ref, sizes, slice(heads * HD, None)) for ref, sizes in parts]
+    sums, totals = [], []
     for i in range(heads):
-        peak_a, peak_b = mine[:, i : i + 1], other[:, i : i + 1]
-        peak = jnp.maximum(peak_a, peak_b)
-        factor_a, factor_b = jnp.exp(peak_a - peak), jnp.exp(peak_b - peak)
+        peaks = [stat[:, i : i + 1] for stat in stats]
+        peak = functools.reduce(jnp.maximum, peaks)
+        factors = [jnp.exp(x - peak) for x in peaks]
         cols = slice(i * HD, (i + 1) * HD)
-        sums.append(keep_ref[:, cols] * factor_a + swap_rows(recv_ref[:, cols], swap) * factor_b)
-        peaks.append(peak)
-        totals.append(
-            mine[:, heads + i : heads + i + 1] * factor_a + other[:, heads + i : heads + i + 1] * factor_b
-        )
-    return sums, peaks, totals
-
-
-def merge_kernel(swap, keep_ref, recv_ref, send_out, keep_out):
-    sums, peaks, totals = merged(keep_ref, recv_ref, swap)
-    half = len(sums) // 2
-    for start, ref in ((0, keep_out), (half, send_out)):
-        for i in range(half):
-            ref[:, i * HD : (i + 1) * HD] = sums[start + i]
-        stats = peaks[start : start + half] + totals[start : start + half]
-        ref[:, half * HD :] = lanes_of(stats, keep_ref.shape[0])
-
-
-def merge(swap, keep, recv):
-    rows, width = keep.shape
-    half = (width - LANES) // HD // 2
-    out = jax.ShapeDtypeStruct((rows, half * HD + LANES), jnp.float32)
-    return pl.pallas_call(
-        functools.partial(merge_kernel, swap),
-        out_shape=[out, out],
-        in_specs=[IN_VMEM] * 2,
-        out_specs=[IN_VMEM] * 2,
-        compiler_params=limit(4),
-        name="merge",
-    )(keep, recv)
-
-
-def project_kernel(swap, tile, keep_ref, recv_ref, *refs):
+        sums.append(sum(read(*part, cols) * f for part, f in zip(parts, factors)))
+        at = slice(heads + i, heads + i + 1)
+        totals.append(sum(stat[:, at] * f for stat, f in zip(stats, factors)))
+    return sums, totals
+
+
+def project_kernel(swaps, tile, *refs):
+    parts, refs = list(zip(refs[: len(swaps)], swaps)), refs[len(swaps) :]
     piece_refs, (send_out, keep_out) = refs[:-2], refs[-2:]
-    sums, _, totals = merged(keep_ref, recv_ref, swap)
+    sums, totals = merged(parts)
     attended = jnp.concatenate([a / t for a, t in zip(sums, totals)], axis=1)
     rows = attended.shape[0]
     half = rows // 2
@@ -310,17 +285,17 @@
         send_out[:, cols] = out[half:]
 
 
-def project(swap, keep, recv, pieces):
+def project(swaps, parts, pieces):
     width = pieces[0].shape[1]
-    out = jax.ShapeDtypeStruct((keep.shape[0] // 2, width), jnp.float32)
+    out = jax.ShapeDtypeStruct((parts[0].shape[0] // 2, width), jnp.float32)
     return pl.pallas_call(
-        functools.partial(project_kernel, swap, min(width, 512)),
+        functools.partial(project_kernel, swaps, min(width, 512)),
         out_shape=[out, out],
-        in_specs=[IN_VMEM] * (2 + len(pieces)),
+        in_specs=[IN_VMEM] * (len(parts) + len(pieces)),
         out_specs=[IN_VMEM] * 2,
         compiler_params=limit(16),
         name="project",
-    )(keep, recv, *pieces)
+    )(*parts, *pieces)
 
 
 def by_planes(bits, queries, keys, values, weight, lengths):
@@ -355,11 +330,11 @@
     for i in range(2):
         pieces += split_weight(weight, i * features // 2, features // 2)
 
-    send = attend(bits, GROUP // 2, limits, q_parts, kv_held)
-    keep = attend(bits, 0, limits, q_parts, kv_held)
-    for b in range(bits - 1):
-        send, keep = merge(part << (bits - 1 - b), keep, swap(send, 1 << b))
-    send, keep = project(part, keep, swap(send, 1 << (bits - 1)), pieces)
+    core, side = part << 1, part
+    far = attend(bits, (3, 2), limits, q_parts, kv_held)
+    near = attend(bits, (1, 0), limits, q_parts, kv_held)
+    partials = [near[1], swap(near[0], 1), swap(far[1], 2), swap(far[0], 3)]
+    send, keep = project(((), (core,), (side,), (core, side)), partials, pieces)
 
     recv = swap(send, 1)
     quarter = keep.shape[0] // 4
@@ -438,8 +413,8 @@
     bits = sub.bit_length() - 1
     fits = (
         blocks == KVH << bits
-        and bits >= 1
-        and GROUP % sub == 0
+        and bits == 2
+        and PLANE_BITS == 2
         and (KVH * queries.shape[0]) % 8 == 0
         and prefix_keys.shape[0] % LANES == 0
     )

time: 48.4 us -> 48.9 us (1.010)
  starting transfers between devices: 19.4 us -> 20.1 us
    ppermute x15 -> x16, starting transfers between devices: 19.4 us -> 20.1 us  [swap(): return lax.ppermute(x, 'blk', [(i, i ^ mask) for i in range(blocks)])]
    pallas_call x4 -> x3, Pallas kernels: 3.29 us -> 3.04 us  [the longest x1 1.56 us: project(): pl.pallas_call(functools.partial(project_kernel, swaps, min(width, 512)),...]
    ppermute x15 -> x16, waiting for transfers between devices: 17.9 us -> 17.9 us  [swap(): return lax.ppermute(x, 'blk', [(i, i ^ mask) for i in range(blocks)])]
  transfers between devices with their start and end apart: 15 -> 16, of which waited for: 9 -> 8; matrix products, arithmetic and copies ran while one was open for 0% -> 0% of each run, Pallas kernels for 14% -> 14%
where the time goes in v5:
time: 48.9 us; the launch traced here: 48.6 us
  starting transfers between devices  20.1 us (41%)
  waiting for transfers between devices  17.9 us (37%)
  Pallas kernels  9.71 us (20%)
  other arithmetic  0.79 us (2%)
    ppermute x16, starting transfers between devices, swap(): return lax.ppermute(x, 'blk', [(i, i ^ mask) for i in range(blocks)])  20.1 us
    ppermute x16, waiting for transfers between devices, swap(): return lax.ppermute(x, 'blk', [(i, i ^ mask) for i in range(blocks)])  17.9 us
    pallas_call x2, Pallas kernels, split_weight(): pl.pallas_call(functools.partial(split_kernel, first, tile), out_shape=[o...  4.71 us
    pallas_call x1, Pallas kernels, project(): pl.pallas_call(functools.partial(project_kernel, swaps, min(width, 512)),...  1.56 us
    pallas_call x2, Pallas kernels, attend(): pl.pallas_call(functools.partial(attend_kernel, bits, key_count, rels), o...  1.48 us
    pallas_call x1, Pallas kernels, pack_kv(): pl.pallas_call(functools.partial(pack_kv_kernel, bits), out_shape=[kv] *...  1.13 us
  transfers between devices with their start and end apart: 16, of which 8 were waited for; matrix products, arithmetic and copies ran while one was open for 0% of the time, Pallas kernels for 14%

profile of v5, /device:TPU:0, one launch (start us, length us, event | category | flops | bytes accessed | tf_op | source)
XLA Modules:
  0.0 48.6 jit_solution(14213105119789312339)
XLA Ops:
  0.0 0.8 %pack_q.1 = (f32[2,4096]{1,0:T(2,128)S(1)}, f32[2,2048]{1,0:T(2,128)S(1)}, f32[2,2048]{1,0:T(2,128)S(1)}, s32[32,128]{1,0:T(8,128)S(1)}) custom-call(s32[2]{0:T(128)} %len_hbm.1, f32[2,8192]{1,0:T(2,128)} %q_hbm.1), custom_call_target="tpu_custom_call" | custom-call | tf_op jit(solution)/shard_map/pack_q/pallas_call | solution.py:108
  0.8 4.1 %collective-permute-start = (f32[2,4096]{1,0:T(2,128)S(1)}, f32[2,4096]{1,0:T(2,128)S(1)}, u32[]{:S(2)}, u32[]{:S(2)}) collective-permute-start(f32[2,4096]{1,0:T(2,128)S(1)} %get-tuple-element.25), channel_id=1, source_target_pairs={{0,8},{1,9},{2,10},{3,11},{4,12},{5,13},{6,14},{7,15},{8,0},{9,1},... | collective-permute-start | bytes 98312 | tf_op jit(solution)/shard_map/ppermute | solution.py:308
  5.0 2.2 %collective-permute-done = f32[2,4096]{1,0:T(2,128)S(1)} collective-permute-done((f32[2,4096]{1,0:T(2,128)S(1)}, f32[2,4096]{1,0:T(2,128)S(1)}, u32[]{:S(2)}, u32[]{:S(2)}) %collective-permute-start) | collective-permute-done | bytes 32800 | tf_op jit(solution)/shard_map/ppermute | solution.py:308
  7.2 1.6 %collective-permute-start.1 = (f32[2,4096]{1,0:T(2,128)S(1)}, f32[2,4096]{1,0:T(2,128)S(1)}, u32[]{:S(2)}, u32[]{:S(2)}) collective-permute-start(f32[2,4096]{1,0:T(2,128)S(1)} %pad_maximum_fusion.1), channel_id=1, source_target_pairs={{0,4},{1,5},{2,6},{3,7},{4,0},{5,1},{6,2},{7,3},{8,12},{9,13},{10,... | collective-permute-start | bytes 98312 | tf_op jit(solution)/shard_map/ppermute | solution.py:308
  8.9 1.1 %pack_kv.1 = (f32[256,128]{1,0:T(8,128)S(1)}, f32[256,128]{1,0:T(8,128)S(1)}, f32[256,128]{1,0:T(8,128)S(1)}, f32[256,128]{1,0:T(8,128)S(1)}) custom-call(f32[128,512]{1,0:T(8,128)} %k_hbm.1, f32[128,512]{1,0:T(8,128)} %v_hbm.1), custom_call_target="tpu_custom_call" | custom-call | bytes 1048576 | tf_op jit(solution)/shard_map/pack_kv/pallas_call | solution.py:135
  10.0 0.5 %collective-permute-start.5 = (f32[256,128]{1,0:T(8,128)S(1)}, f32[256,128]{1,0:T(8,128)S(1)}, u32[]{:S(2)}, u32[]{:S(2)}) collective-permute-start(f32[256,128]{1,0:T(8,128)S(1)} %get-tuple-element.28), channel_id=1, source_target_pairs={{0,4},{1,5},{2,6},{3,7},{4,0},{5,1},{6,2},{7,3},{8,12},{9,13},{10,... | collective-permute-start | bytes 393224 | tf_op jit(solution)/shard_map/ppermute | solution.py:308
  10.5 2.6 %collective-permute-start.6 = (f32[256,128]{1,0:T(8,128)S(1)}, f32[256,128]{1,0:T(8,128)S(1)}, u32[]{:S(2)}, u32[]{:S(2)}) collective-permute-start(f32[256,128]{1,0:T(8,128)S(1)} %get-tuple-element.29), channel_id=1, source_target_pairs={{0,8},{1,9},{2,10},{3,11},{4,12},{5,13},{6,14},{7,15},{8,0},{9,1},... | collective-permute-start | bytes 393224 | tf_op jit(solution)/shard_map/ppermute | solution.py:308
  13.1 1.3 %collective-permute-start.7 = (f32[256,128]{1,0:T(8,128)S(1)}, f32[256,128]{1,0:T(8,128)S(1)}, u32[]{:S(2)}, u32[]{:S(2)}) collective-permute-start(f32[256,128]{1,0:T(8,128)S(1)} %get-tuple-element.30), channel_id=1, source_target_pairs={{0,12},{1,13},{2,14},{3,15},{4,8},{5,9},{6,10},{7,11},{8,4},{9,5},... | collective-permute-start | bytes 393224 | tf_op jit(solution)/shard_map/ppermute | solution.py:308
  14.5 1.6 %collective-permute-start.2 = (f32[8,2048]{1,0:T(8,128)S(1)}, f32[8,2048]{1,0:T(8,128)S(1)}, u32[]{:S(2)}, u32[]{:S(2)}) collective-permute-start(f32[8,2048]{1,0:T(8,128)S(1)} %pad_maximum_fusion.refs_0_), channel_id=1, source_target_pairs={{0,2},{1,3},{2,0},{3,1},{4,6},{5,7},{6,4},{7,5},{8,10},{9,11},{10,... | collective-permute-start | bytes 196616 | tf_op jit(solution)/shard_map/ppermute | solution.py:308
  16.1 2.7 %collective-permute-done.2.refs_1_ = f32[8,2048]{1,0:T(8,128)S(1)} collective-permute-done((f32[8,2048]{1,0:T(8,128)S(1)}, f32[8,2048]{1,0:T(8,128)S(1)}, u32[]{:S(2)}, u32[]{:S(2)}) %collective-permute-start.2) | collective-permute-done | bytes 65568 | tf_op jit(solution)/shard_map/ppermute | solution.py:308
  18.8 0.0 collective-permute-start.4
  18.8 0.0 collective-permute-done.3.refs_2_
  18.8 4.3 %collective-permute-done.6.refs_6_ = f32[256,128]{1,0:T(8,128)S(1)} collective-permute-done((f32[256,128]{1,0:T(8,128)S(1)}, f32[256,128]{1,0:T(8,128)S(1)}, u32[]{:S(2)}, u32[]{:S(2)}) %collective-permute-start.6) | collective-permute-done | bytes 131104 | tf_op jit(solution)/shard_map/ppermute | solution.py:308
  23.2 0.7 %attend.3 = (f32[32,640]{1,0:T(8,128)S(1)}, f32[32,640]{1,0:T(8,128)S(1)}) custom-call(s32[32,128]{1,0:T(8,128)S(1)} %get-tuple-element.23.limit_ref, f32[8,2048]{1,0:T(8,128)S(1)} %pad_maximum_fusion.refs_0_, f32[8,2048]{1,0:T(8,128)S(1)} %collective-permute-done.2.refs_1_, f32[8,2048]{1,0:T(8,128)S(1)} %collective-permute-done.3.refs_2_, ...), custom_call_target="tpu_custom_call" | custom-call | flops 201326592 | bytes 65536 | tf_op jit(solution)/shard_map/attend/pallas_call | solution.py:235
  23.9 1.6 %collective-permute-start.9 = (f32[32,640]{1,0:T(8,128)S(1)}, f32[32,640]{1,0:T(8,128)S(1)}, u32[]{:S(2)}, u32[]{:S(2)}) collective-permute-start(f32[32,640]{1,0:T(8,128)S(1)} %get-tuple-element.33), channel_id=1, source_target_pairs={{0,2},{1,3},{2,0},{3,1},{4,6},{5,7},{6,4},{7,5},{8,10},{9,11},{10,... | collective-permute-start | bytes 245768 | tf_op jit(solution)/shard_map/ppermute | solution.py:308
  25.5 0.7 %attend.2 = (f32[32,640]{1,0:T(8,128)S(1)}, f32[32,640]{1,0:T(8,128)S(1)}) custom-call(s32[32,128]{1,0:T(8,128)S(1)} %get-tuple-element.23.limit_ref, f32[8,2048]{1,0:T(8,128)S(1)} %pad_maximum_fusion.refs_0_, f32[8,2048]{1,0:T(8,128)S(1)} %collective-permute-done.2.refs_1_, f32[8,2048]{1,0:T(8,128)S(1)} %collective-permute-done.3.refs_2_, ...), custom_call_target="tpu_custom_call" | custom-call | flops 201326592 | bytes 65536 | tf_op jit(solution)/shard_map/attend/pallas_call | solution.py:235
  26.2 0.7 %collective-permute-start.8 = (f32[32,640]{1,0:T(8,128)S(1)}, f32[32,640]{1,0:T(8,128)S(1)}, u32[]{:S(2)}, u32[]{:S(2)}) collective-permute-start(f32[32,640]{1,0:T(8,128)S(1)} %get-tuple-element.32), channel_id=1, source_target_pairs={{0,1},{1,0},{2,3},{3,2},{4,5},{5,4},{6,7},{7,6},{8,9},{9,8},{10,11... | collective-permute-start | bytes 245768 | tf_op jit(solution)/shard_map/ppermute | solution.py:308
  26.9 2.4 %split.3 = (bf16[256,4096]{1,0:T(8,128)(2,1)S(1)}, bf16[256,4096]{1,0:T(8,128)(2,1)S(1)}) custom-call(f32[512,4096]{1,0:T(8,128)} %w_hbm.3), custom_call_target="tpu_custom_call" | custom-call | flops 8388608 | bytes 8388608 | tf_op jit(solution)/shard_map/split/pallas_call | solution.py:165
  29.3 2.4 %split.2 = (bf16[256,4096]{1,0:T(8,128)(2,1)S(1)}, bf16[256,4096]{1,0:T(8,128)(2,1)S(1)}) custom-call(f32[512,4096]{1,0:T(8,128)} %w_hbm.3), custom_call_target="tpu_custom_call" | custom-call | flops 8388608 | bytes 8388608 | tf_op jit(solution)/shard_map/split/pallas_call | solution.py:165
  31.7 1.6 %project.1 = (f32[16,4096]{1,0:T(8,128)S(1)}, f32[16,4096]{1,0:T(8,128)S(1)}) custom-call(f32[32,640]{1,0:T(8,128)S(1)} %get-tuple-element.31.refs_0_, f32[32,640]{1,0:T(8,128)S(1)} %collective-permute-done.8.refs_1_, f32[32,640]{1,0:T(8,128)S(1)} %collective-permute-done.9.refs_2_, f32[32,640]{1,0:T(8,128)S(1)} %collective-permute-done.10.refs_3_, ...), custom_call_target="tpu_custom_call" | custom-call | tf_op jit(solution)/shard_map/project/pallas_call | solution.py:291
  33.2 0.0 collective-permute-start.11
  33.3 1.5 %collective-permute-done.11 = f32[16,4096]{1,0:T(8,128)S(1)} collective-permute-done((f32[16,4096]{1,0:T(8,128)S(1)}, f32[16,4096]{1,0:T(8,128)S(1)}, u32[]{:S(2)}, u32[]{:S(2)}) %collective-permute-start.11) | collective-permute-done | bytes 262176 | tf_op jit(solution)/shard_map/ppermute | solution.py:308
  34.8 0.1 slice_add_fusion.2
  34.9 2.0 %collective-permute-start.12 = (f32[4,4096]{1,0:T(4,128)S(1)}, f32[4,4096]{1,0:T(4,128)S(1)}, u32[]{:S(2)}, u32[]{:S(2)}) collective-permute-start(f32[4,4096]{1,0:T(4,128)S(1)} %get-tuple-element.41), channel_id=1, source_target_pairs={{0,4},{1,5},{2,6},{3,7},{4,0},{5,1},{6,2},{7,3},{8,12},{9,13},{10,... | collective-permute-start | bytes 196616 | tf_op jit(solution)/shard_map/ppermute | solution.py:308
  36.9 1.0 %collective-permute-start.14 = (f32[4,4096]{1,0:T(4,128)S(1)}, f32[4,4096]{1,0:T(4,128)S(1)}, u32[]{:S(2)}, u32[]{:S(2)}) collective-permute-start(f32[4,4096]{1,0:T(4,128)S(1)} %get-tuple-element.42), channel_id=1, source_target_pairs={{0,6},{1,7},{2,4},{3,5},{4,2},{5,3},{6,0},{7,1},{8,14},{9,15},{10,... | collective-permute-start | bytes 196616 | tf_op jit(solution)/shard_map/ppermute | solution.py:308
  37.9 0.5 %collective-permute-start.13 = (f32[4,4096]{1,0:T(4,128)S(1)}, f32[4,4096]{1,0:T(4,128)S(1)}, u32[]{:S(2)}, u32[]{:S(2)}) collective-permute-start(f32[4,4096]{1,0:T(4,128)S(1)} %get-tuple-element.43), channel_id=1, source_target_pairs={{0,2},{1,3},{2,0},{3,1},{4,6},{5,7},{6,4},{7,5},{8,10},{9,11},{10,... | collective-permute-start | bytes 196616 | tf_op jit(solution)/shard_map/ppermute | solution.py:308
  38.4 0.9 %collective-permute-done.12 = f32[4,4096]{1,0:T(4,128)S(1)} collective-permute-done((f32[4,4096]{1,0:T(4,128)S(1)}, f32[4,4096]{1,0:T(4,128)S(1)}, u32[]{:S(2)}, u32[]{:S(2)}) %collective-permute-start.12) | collective-permute-done | bytes 65568 | tf_op jit(solution)/shard_map/ppermute | solution.py:308
  39.3 2.8 %collective-permute-done.14 = f32[4,4096]{1,0:T(4,128)S(1)} collective-permute-done((f32[4,4096]{1,0:T(4,128)S(1)}, f32[4,4096]{1,0:T(4,128)S(1)}, u32[]{:S(2)}, u32[]{:S(2)}) %collective-permute-start.14) | collective-permute-done | bytes 65568 | tf_op jit(solution)/shard_map/ppermute | solution.py:308
  42.1 1.0 %collective-permute-done.13 = f32[4,4096]{1,0:T(4,128)S(1)} collective-permute-done((f32[4,4096]{1,0:T(4,128)S(1)}, f32[4,4096]{1,0:T(4,128)S(1)}, u32[]{:S(2)}, u32[]{:S(2)}) %collective-permute-start.13) | collective-permute-done | bytes 65568 | tf_op jit(solution)/shard_map/ppermute | solution.py:308
  43.1 2.4 %collective-permute-start.15 = (f32[2,4096]{1,0:T(2,128)S(1)}, f32[2,4096]{1,0:T(2,128)S(1)}, u32[]{:S(2)}, u32[]{:S(2)}) collective-permute-start(f32[2,4096]{1,0:T(2,128)S(1)} %slice.65), channel_id=1, source_target_pairs={{0,8},{1,9},{2,10},{3,11},{4,12},{5,13},{6,14},{7,15},{8,0},{9,1},... | collective-permute-start | bytes 98312 | tf_op jit(solution)/shard_map/ppermute | solution.py:308
  45.5 2.5 %collective-permute-done.15 = f32[2,4096]{1,0:T(2,128)S(1)} collective-permute-done((f32[2,4096]{1,0:T(2,128)S(1)}, f32[2,4096]{1,0:T(2,128)S(1)}, u32[]{:S(2)}, u32[]{:S(2)}) %collective-permute-start.15) | collective-permute-done | bytes 32800 | tf_op jit(solution)/shard_map/ppermute | solution.py:308
  48.0 0.6 %slice_add_fusion.4 = f32[2,4096]{1,0:T(2,128)} fusion(f32[2,4096]{1,0:T(2,128)S(1)} %collective-permute-done.15, f32[4,4096]{1,0:T(4,128)S(1)} %fusion.2), kind=kLoop, calls=%fused_computation.8 | loop fusion | flops 8192 | bytes 98304 | tf_op jit(solution)/shard_map/add | solution.py:345
  (15 shorter events, 0.1 us)
Async XLA Ops:
  0.8 6.4 %collective-permute-start = (f32[2,4096]{1,0:T(2,128)S(1)}, f32[2,4096]{1,0:T(2,128)S(1)}, u32[]{:S(2)}, u32[]{:S(2)}) collective-permute-start(f32[2,4096]{1,0:T(2,128)S(1)} %get-tuple-element.25), channel_id=1, source_target_pairs={{0,8},{1,9},{2,10},{3,11},{4,12},{5,13},{6,14},{7,15},{8,0},{9,1},... | collective-permute-start | bytes 98312 | tf_op jit(solution)/shard_map/ppermute | solution.py:308
  7.2 7.2 %collective-permute-start.1 = (f32[2,4096]{1,0:T(2,128)S(1)}, f32[2,4096]{1,0:T(2,128)S(1)}, u32[]{:S(2)}, u32[]{:S(2)}) collective-permute-start(f32[2,4096]{1,0:T(2,128)S(1)} %pad_maximum_fusion.1), channel_id=1, source_target_pairs={{0,4},{1,5},{2,6},{3,7},{4,0},{5,1},{6,2},{7,3},{8,12},{9,13},{10,... | collective-permute-start | bytes 98312 | tf_op jit(solution)/shard_map/ppermute | solution.py:308
  10.0 8.8 %collective-permute-start.5 = (f32[256,128]{1,0:T(8,128)S(1)}, f32[256,128]{1,0:T(8,128)S(1)}, u32[]{:S(2)}, u32[]{:S(2)}) collective-permute-start(f32[256,128]{1,0:T(8,128)S(1)} %get-tuple-element.28), channel_id=1, source_target_pairs={{0,4},{1,5},{2,6},{3,7},{4,0},{5,1},{6,2},{7,3},{8,12},{9,13},{10,... | collective-permute-start | bytes 393224 | tf_op jit(solution)/shard_map/ppermute | solution.py:308
  10.5 12.6 %collective-permute-start.6 = (f32[256,128]{1,0:T(8,128)S(1)}, f32[256,128]{1,0:T(8,128)S(1)}, u32[]{:S(2)}, u32[]{:S(2)}) collective-permute-start(f32[256,128]{1,0:T(8,128)S(1)} %get-tuple-element.29), channel_id=1, source_target_pairs={{0,8},{1,9},{2,10},{3,11},{4,12},{5,13},{6,14},{7,15},{8,0},{9,1},... | collective-permute-start | bytes 393224 | tf_op jit(solution)/shard_map/ppermute | solution.py:308
  13.1 10.0 %collective-permute-start.7 = (f32[256,128]{1,0:T(8,128)S(1)}, f32[256,128]{1,0:T(8,128)S(1)}, u32[]{:S(2)}, u32[]{:S(2)}) collective-permute-start(f32[256,128]{1,0:T(8,128)S(1)} %get-tuple-element.30), channel_id=1, source_target_pairs={{0,12},{1,13},{2,14},{3,15},{4,8},{5,9},{6,10},{7,11},{8,4},{9,5},... | collective-permute-start | bytes 393224 | tf_op jit(solution)/shard_map/ppermute | solution.py:308
  14.5 4.3 %collective-permute-start.2 = (f32[8,2048]{1,0:T(8,128)S(1)}, f32[8,2048]{1,0:T(8,128)S(1)}, u32[]{:S(2)}, u32[]{:S(2)}) collective-permute-start(f32[8,2048]{1,0:T(8,128)S(1)} %pad_maximum_fusion.refs_0_), channel_id=1, source_target_pairs={{0,2},{1,3},{2,0},{3,1},{4,6},{5,7},{6,4},{7,5},{8,10},{9,11},{10,... | collective-permute-start | bytes 196616 | tf_op jit(solution)/shard_map/ppermute | solution.py:308
  16.1 2.8 %collective-permute-start.3 = (f32[8,2048]{1,0:T(8,128)S(1)}, f32[8,2048]{1,0:T(8,128)S(1)}, u32[]{:S(2)}, u32[]{:S(2)}) collective-permute-start(f32[8,2048]{1,0:T(8,128)S(1)} %pad_maximum_fusion.refs_0_), channel_id=1, source_target_pairs={{0,1},{1,0},{2,3},{3,2},{4,5},{5,4},{6,7},{7,6},{8,9},{9,8},{10,11... | collective-permute-start | bytes 196616 | tf_op jit(solution)/shard_map/ppermute | solution.py:308
  18.8 4.3 %collective-permute-start.4 = (f32[8,2048]{1,0:T(8,128)S(1)}, f32[8,2048]{1,0:T(8,128)S(1)}, u32[]{:S(2)}, u32[]{:S(2)}) collective-permute-start(f32[8,2048]{1,0:T(8,128)S(1)} %collective-permute-done.2.refs_1_), channel_id=1, source_target_pairs={{0,1},{1,0},{2,3},{3,2},{4,5},{5,4},{6,7},{7,6},{8,9},{9,8},{10,11... | collective-permute-start | bytes 196616 | tf_op jit(solution)/shard_map/ppermute | solution.py:308
  23.9 7.7 %collective-permute-start.9 = (f32[32,640]{1,0:T(8,128)S(1)}, f32[32,640]{1,0:T(8,128)S(1)}, u32[]{:S(2)}, u32[]{:S(2)}) collective-permute-start(f32[32,640]{1,0:T(8,128)S(1)} %get-tuple-element.33), channel_id=1, source_target_pairs={{0,2},{1,3},{2,0},{3,1},{4,6},{5,7},{6,4},{7,5},{8,10},{9,11},{10,... | collective-permute-start | bytes 245768 | tf_op jit(solution)/shard_map/ppermute | solution.py:308
  25.5 6.2 %collective-permute-start.10 = (f32[32,640]{1,0:T(8,128)S(1)}, f32[32,640]{1,0:T(8,128)S(1)}, u32[]{:S(2)}, u32[]{:S(2)}) collective-permute-start(f32[32,640]{1,0:T(8,128)S(1)} %get-tuple-element.34), channel_id=1, source_target_pairs={{0,3},{1,2},{2,1},{3,0},{4,7},{5,6},{6,5},{7,4},{8,11},{9,10},{10,... | collective-permute-start | bytes 245768 | tf_op jit(solution)/shard_map/ppermute | solution.py:308
  26.2 5.4 %collective-permute-start.8 = (f32[32,640]{1,0:T(8,128)S(1)}, f32[32,640]{1,0:T(8,128)S(1)}, u32[]{:S(2)}, u32[]{:S(2)}) collective-permute-start(f32[32,640]{1,0:T(8,128)S(1)} %get-tuple-element.32), channel_id=1, source_target_pairs={{0,1},{1,0},{2,3},{3,2},{4,5},{5,4},{6,7},{7,6},{8,9},{9,8},{10,11... | collective-permute-start | bytes 245768 | tf_op jit(solution)/shard_map/ppermute | solution.py:308
  33.2 1.6 %collective-permute-start.11 = (f32[16,4096]{1,0:T(8,128)S(1)}, f32[16,4096]{1,0:T(8,128)S(1)}, u32[]{:S(2)}, u32[]{:S(2)}) collective-permute-start(f32[16,4096]{1,0:T(8,128)S(1)} %get-tuple-element.40), channel_id=1, source_target_pairs={{0,1},{1,0},{2,3},{3,2},{4,5},{5,4},{6,7},{7,6},{8,9},{9,8},{10,11... | collective-permute-start | bytes 786440 | tf_op jit(solution)/shard_map/ppermute | solution.py:308
  34.9 4.4 %collective-permute-start.12 = (f32[4,4096]{1,0:T(4,128)S(1)}, f32[4,4096]{1,0:T(4,128)S(1)}, u32[]{:S(2)}, u32[]{:S(2)}) collective-permute-start(f32[4,4096]{1,0:T(4,128)S(1)} %get-tuple-element.41), channel_id=1, source_target_pairs={{0,4},{1,5},{2,6},{3,7},{4,0},{5,1},{6,2},{7,3},{8,12},{9,13},{10,... | collective-permute-start | bytes 196616 | tf_op jit(solution)/shard_map/ppermute | solution.py:308
  36.9 5.2 %collective-permute-start.14 = (f32[4,4096]{1,0:T(4,128)S(1)}, f32[4,4096]{1,0:T(4,128)S(1)}, u32[]{:S(2)}, u32[]{:S(2)}) collective-permute-start(f32[4,4096]{1,0:T(4,128)S(1)} %get-tuple-element.42), channel_id=1, source_target_pairs={{0,6},{1,7},{2,4},{3,5},{4,2},{5,3},{6,0},{7,1},{8,14},{9,15},{10,... | collective-permute-start | bytes 196616 | tf_op jit(solution)/shard_map/ppermute | solution.py:308
  37.9 5.1 %collective-permute-start.13 = (f32[4,4096]{1,0:T(4,128)S(1)}, f32[4,4096]{1,0:T(4,128)S(1)}, u32[]{:S(2)}, u32[]{:S(2)}) collective-permute-start(f32[4,4096]{1,0:T(4,128)S(1)} %get-tuple-element.43), channel_id=1, source_target_pairs={{0,2},{1,3},{2,0},{3,1},{4,6},{5,7},{6,4},{7,5},{8,10},{9,11},{10,... | collective-permute-start | bytes 196616 | tf_op jit(solution)/shard_map/ppermute | solution.py:308
  43.1 4.9 %collective-permute-start.15 = (f32[2,4096]{1,0:T(2,128)S(1)}, f32[2,4096]{1,0:T(2,128)S(1)}, u32[]{:S(2)}, u32[]{:S(2)}) collective-permute-start(f32[2,4096]{1,0:T(2,128)S(1)} %slice.65), channel_id=1, source_target_pairs={{0,8},{1,9},{2,10},{3,11},{4,12},{5,13},{6,14},{7,15},{8,0},{9,1},... | collective-permute-start | bytes 98312 | tf_op jit(solution)/shard_map/ppermute | solution.py:308
